TPU v7x, 32 devices: a whole 2x2x4 slice. The times are simulated.
32 devices in a mesh: dp: 8 (over z, y), tensor: 4 (over x, core).
Axes of the slice: x: 2, y: 2, z: 4, core: 2. Of those that a mesh axis runs over, the one named last changes fastest.
Arguments:
- hidden: bfloat16 [12288, 1536], P('dp'), may hold values from -6 to 6
- segment_ids: int32 [12288], P('dp'), may hold values from -1 to 12287, as said below
- norm_gain: float32 [1536], replicated, may hold values from 0.5 to 1.5
- gate_weight: bfloat16 [1536, 3072], P(None, 'tensor'), may hold values from -0.15625 to 0.15625
- input_weight: bfloat16 [1536, 3072], P(None, 'tensor'), may hold values from -0.15625 to 0.15625
- step_weight: bfloat16 [1536, 48], P(None, 'tensor'), may hold values from -0.15625 to 0.15625
- state_weight: bfloat16 [1536, 256], replicated, may hold values from -0.15625 to 0.15625
- conv_weight: float32 [4, 3072], P(None, 'tensor'), may hold values from -3 to 3
- state_conv_weight: float32 [4, 256], replicated, may hold values from -3 to 3
- conv_bias: float32 [3072], P('tensor'), may hold values from -0.5 to 0.5
- state_conv_bias: float32 [256], replicated, may hold values from -0.5 to 0.5
- step_bias: float32 [48], P('tensor'), may hold values from -6.9 to -2.25
- decay_log: float32 [48], P('tensor'), may hold values from 0 to 2.77
- skip_gain: float32 [48], P('tensor'), may hold values from 0.5 to 1.5
- gate_norm_gain: float32 [3072], P('tensor'), may hold values from 0.5 to 1.5
- out_weight: bfloat16 [3072, 1536], P('tensor'), may hold values from -0.109375 to 0.109375
- cotangent: bfloat16 [12288, 1536], P('dp'), may hold values from -6 to 6
Outputs:
- block_out: bfloat16 [12288, 1536], P('dp')
- grad_hidden: float32 [12288, 1536], P('dp')
- grad_norm_gain: float32 [1536], replicated
- grad_gate_weight: float32 [1536, 3072], P(None, 'tensor')
- grad_input_weight: float32 [1536, 3072], P(None, 'tensor')
- grad_step_weight: float32 [1536, 48], P(None, 'tensor')
- grad_state_weight: float32 [1536, 256], replicated
- grad_conv_weight: float32 [4, 3072], P(None, 'tensor')
- grad_state_conv_weight: float32 [4, 256], replicated
- grad_conv_bias: float32 [3072], P('tensor')
- grad_state_conv_bias: float32 [256], replicated
- grad_step_bias: float32 [48], P('tensor')
- grad_decay_log: float32 [48], P('tensor')
- grad_skip_gain: float32 [48], P('tensor')
- grad_gate_norm_gain: float32 [3072], P('tensor')
- grad_out_weight: float32 [3072, 1536], P('tensor')
Inputs may be any that keep to these rules, and one draw needn't show every extreme that they name: `segment_ids`: each value is -1 for an empty slot or the global index of the first slot of its sequence; a sequence lies within the 1536 slots of one dp index, its slots are consecutive; the empty slots of a dp index come after all its sequences and number a multiple of 256; the last dp index has no empty slot, and the last slot of all starts a sequence of one token.
All inputs are finite; a program needn't handle non-finite values.
Results may differ from a plain program's by a relative error of at most 0.0096.
Values may be sent and summed in bfloat16 or wider, within the bound.
No kernel may reach another device: no remote copies, remote signals or barrier semaphores. Data moves between devices by JAX's collectives and lax.ppermute only.
A program may use at most 256 MiB of HBM per device.

v0:
```python
from functools import partial

import jax
import jax.numpy as jnp
from jax import lax
from jax.sharding import PartitionSpec as P

INNER = 3072
GROUP = 256


EPS = 1e-05
HIGH = lax.Precision.HIGHEST


def conv_silu(inputs, weights, biases, segments):
    summed = biases[None, :] + weights[0][None, :] * inputs
    for offset in range(1, weights.shape[0]):
        shifted = jnp.concatenate(
            [jnp.zeros((offset, inputs.shape[1]), inputs.dtype), inputs[:-offset]], axis=0
        )
        seg_shift = jnp.concatenate([jnp.full((offset,), -2, jnp.int32), segments[:-offset]])
        keeping = (seg_shift == segments).astype(inputs.dtype)
        summed = summed + weights[offset][None, :] * shifted * keeping[:, None]
    return jax.nn.silu(summed)


def ssd_scan(values, states, step_raw, step_bias, decay_log, skip_gain, segments, group):
    length = values.shape[0]
    heads = step_bias.shape[0]
    width = values.shape[1] // heads
    state = states.shape[1] // 2
    blocks = length // group
    step = jax.nn.softplus(step_raw + step_bias[None, :])
    rate = step * (-jnp.exp(decay_log))[None, :]
    x_blk = values.reshape(blocks, group, heads, width)
    b_blk = states[:, :state].reshape(blocks, group, state)
    c_blk = states[:, state:].reshape(blocks, group, state)
    step_h = step.reshape(blocks, group, heads).transpose(0, 2, 1)
    cum_h = jnp.cumsum(rate.reshape(blocks, group, heads), axis=1).transpose(0, 2, 1)
    seg_blk = segments.reshape(blocks, group)
    causal = jnp.tril(jnp.ones((group, group), bool))
    same = ((seg_blk[:, :, None] == seg_blk[:, None, :]) & causal[None])[:, None]
    differ = cum_h[:, :, :, None] - cum_h[:, :, None, :]
    decay = jnp.where(same, jnp.exp(jnp.where(same, differ, 0.0)), 0.0)
    inner_cb = jnp.einsum("cin,cjn->cij", c_blk, b_blk, precision=HIGH)
    mixing = decay * inner_cb[:, None] * step_h[:, :, None, :]
    y_diag = jnp.einsum("chij,cjhp->cihp", mixing, x_blk, precision=HIGH)
    last_seg = seg_blk[:, -1]
    to_end = jnp.exp(cum_h[:, :, -1:] - cum_h) * step_h * (seg_blk == last_seg[:, None])[:, None, :]
    weighted = to_end.transpose(0, 2, 1)[..., None] * x_blk
    local_state = jnp.einsum("cjn,cjhp->chnp", b_blk, weighted, precision=HIGH)
    prev_seg = jnp.concatenate([jnp.full((1,), -3, jnp.int32), last_seg[:-1]])
    carry_keep = (last_seg == prev_seg).astype(values.dtype)[:, None] * jnp.exp(cum_h[:, :, -1])

    def advance(entering, pieces):
        local_part, factor = pieces
        return (local_part + factor[:, None, None] * entering, entering)

    start_state = jnp.zeros((heads, state, width), values.dtype)
    _, entering_all = lax.scan(advance, start_state, (local_state, carry_keep))
    reach = jnp.exp(cum_h).transpose(0, 2, 1) * (seg_blk == prev_seg[:, None])[..., None]
    y_off = jnp.einsum("cin,chnp->cihp", c_blk, entering_all, precision=HIGH) * reach[..., None]
    result = y_diag + y_off + skip_gain[None, None, :, None] * x_blk
    return result.reshape(length, heads * width)


def cross_dot(left, right):
    return lax.dot_general(
        left, right, (((0,), (0,)), ((), ())), preferred_element_type=jnp.float32
    )


def back_dot(left, right):
    return lax.dot_general(
        left, right, (((1,), (1,)), ((), ())), preferred_element_type=jnp.float32
    )


def body(
    hidden,
    segment_ids,
    norm_gain,
    gate_weight,
    input_weight,
    step_weight,
    state_weight,
    conv_weight,
    state_conv_weight,
    conv_bias,
    state_conv_bias,
    step_bias,
    decay_log,
    skip_gain,
    gate_norm_gain,
    out_weight,
    cotangent,
):
    valid = (segment_ids >= 0).astype(jnp.float32)[:, None]
    hidden_f = hidden.astype(jnp.float32)
    inverse = lax.rsqrt(jnp.mean(hidden_f * hidden_f, axis=1, keepdims=True) + EPS)
    normed = (hidden_f * inverse * norm_gain[None, :]).astype(jnp.bfloat16)
    gate_pre = jnp.dot(normed, gate_weight, preferred_element_type=jnp.float32)
    input_pre = jnp.dot(normed, input_weight, preferred_element_type=jnp.float32)
    step_pre = jnp.dot(normed, step_weight, preferred_element_type=jnp.float32)
    state_pre = jnp.dot(normed, state_weight, preferred_element_type=jnp.float32)
    conv_out, conv_back = jax.vjp(
        partial(conv_silu, segments=segment_ids), input_pre, conv_weight, conv_bias
    )
    state_out, state_back = jax.vjp(
        partial(conv_silu, segments=segment_ids), state_pre, state_conv_weight, state_conv_bias
    )
    values_f = lax.optimization_barrier(conv_out.astype(jnp.bfloat16)).astype(jnp.float32)
    states_f = lax.optimization_barrier(state_out.astype(jnp.bfloat16)).astype(jnp.float32)
    mixed_y, ssd_back = jax.vjp(
        partial(ssd_scan, segments=segment_ids, group=GROUP),
        values_f,
        states_f,
        step_pre,
        step_bias,
        decay_log,
        skip_gain,
    )
    gate_act = jax.nn.silu(gate_pre)
    gated = mixed_y * gate_act
    square_sum = lax.psum(jnp.sum(gated * gated, axis=1), "tensor")
    gate_inverse = lax.rsqrt(square_sum / INNER + EPS)[:, None]
    gnormed = (gated * gate_inverse * gate_norm_gain[None, :]).astype(jnp.bfloat16)
    partial_mix = jnp.dot(gnormed, out_weight, preferred_element_type=jnp.float32)
    mix = lax.psum(partial_mix, "tensor")
    block_out = (hidden_f + valid * mix).astype(jnp.bfloat16)
    dmix = (cotangent.astype(jnp.float32) * valid).astype(jnp.bfloat16)
    grad_out = cross_dot(gnormed, dmix)
    d_gn = back_dot(dmix, out_weight)
    grad_gnorm = jnp.sum(d_gn * gated * gate_inverse, axis=0)
    scaled = d_gn * gate_norm_gain[None, :]
    dot_sum = lax.psum(jnp.sum(gated * scaled, axis=1), "tensor")
    d_gated = gate_inverse * scaled - gated * gate_inverse**3 * (dot_sum / INNER)[:, None]
    d_y = d_gated * gate_act
    sigma = jax.nn.sigmoid(gate_pre)
    d_gate = d_gated * mixed_y * sigma * (1.0 + gate_pre * (1.0 - sigma))
    d_values, d_states, d_step, grad_sbias, grad_decay, grad_skip = ssd_back(d_y)
    d_input, grad_conv, grad_cbias = conv_back(d_values)
    gate_b = d_gate.astype(jnp.bfloat16)
    input_b = d_input.astype(jnp.bfloat16)
    step_b = d_step.astype(jnp.bfloat16)
    local_back = (
        back_dot(gate_b, gate_weight)
        + back_dot(input_b, input_weight)
        + back_dot(step_b, step_weight)
    )
    summed_back, states_full = lax.psum((local_back, d_states), "tensor")
    d_state_pre, grad_sconv, grad_scbias = state_back(states_full)
    state_b = d_state_pre.astype(jnp.bfloat16)
    d_normed = summed_back + back_dot(state_b, state_weight)
    grad_norm = jnp.sum(d_normed * hidden_f * inverse, axis=0)
    scaled_in = d_normed * norm_gain[None, :]
    grad_hidden = (
        cotangent.astype(jnp.float32)
        + inverse * scaled_in
        - hidden_f * inverse**3 * jnp.mean(hidden_f * scaled_in, axis=1, keepdims=True)
    )
    grad_gate = cross_dot(normed, gate_b)
    grad_input = cross_dot(normed, input_b)
    grad_step = cross_dot(normed, step_b)
    grad_state = cross_dot(normed, state_b)
    summed = lax.psum(
        (
            grad_norm,
            grad_gate,
            grad_input,
            grad_step,
            grad_state,
            grad_conv,
            grad_sconv,
            grad_cbias,
            grad_scbias,
            grad_sbias,
            grad_decay,
            grad_skip,
            grad_gnorm,
            grad_out,
        ),
        "dp",
    )
    (
        grad_norm,
        grad_gate,
        grad_input,
        grad_step,
        grad_state,
        grad_conv,
        grad_sconv,
        grad_cbias,
        grad_scbias,
        grad_sbias,
        grad_decay,
        grad_skip,
        grad_gnorm,
        grad_out,
    ) = summed
    return (
        block_out,
        grad_hidden,
        grad_norm,
        grad_gate,
        grad_input,
        grad_step,
        grad_state,
        grad_conv,
        grad_sconv,
        grad_cbias,
        grad_scbias,
        grad_sbias,
        grad_decay,
        grad_skip,
        grad_gnorm,
        grad_out,
    )


def solution(mesh):
    return jax.shard_map(
        body,
        mesh=mesh,
        in_specs=(
            P("dp", None),
            P("dp"),
            P(),
            P(None, "tensor"),
            P(None, "tensor"),
            P(None, "tensor"),
            P(),
            P(None, "tensor"),
            P(),
            P("tensor"),
            P(),
            P("tensor"),
            P("tensor"),
            P("tensor"),
            P("tensor"),
            P("tensor", None),
            P("dp", None),
        ),
        out_specs=(
            P("dp", None),
            P("dp", None),
            P(),
            P(None, "tensor"),
            P(None, "tensor"),
            P(None, "tensor"),
            P(),
            P(None, "tensor"),
            P(),
            P("tensor"),
            P(),
            P("tensor"),
            P("tensor"),
            P("tensor"),
            P("tensor"),
            P("tensor", None),
        ),
        check_vma=False,
    )
```

profile of v0, /device:TPU:0, one launch (start us, length us, event | category | flops | bytes accessed | tf_op | source)
XLA Modules:
  0.0 1345.2 jit_solution(4326663023551138808)
XLA Ops:
  8.5 3.5 fusion.14
  14.4 4.0 fusion.117
  19.1 6.5 multiply_convert_fusion.2
  25.6 8.5 reshape.327
  34.1 8.2 reshape.326
  42.9 4.3 compare_select_fusion.2
  47.4 3.4 reduce-window.14
  51.5 9.9 copy.178
  61.4 3.8 fusion.118
  65.3 2.7 multiply_convert_fusion.3
  71.3 3.8 fusion.67
  75.1 2.8 broadcast.168.clone
  77.9 42.7 %while.34 = (s32[]{:T(128)}, f32[12,128,64]{2,1,0:T(8,128)}, f32[6,12,128,64]{3,2,1,0:T(8,128)}, f32[6,12,1,1]{1,3,2,0:T(1,128)}, f32[6,12,128,64]{2,3,1,0:T(8,128)}, /*index=5*/f32[6,12]{1,0:T(8,128)}, s32[]{:T(128)}, s32[]{:T(128)}) while((s32[]{:T(128)}, f32[12,128,64]{2,1,0:T(8,128)}, f32[6,12,128,64]{3,2,1,0:T(8,128)}, ...), condition=%wide.region_4.5_spmd.clone, body=%wide.region_3.4_spmd.clone.sunk | while | flops 393219 | bytes 4327672 | solution.py:61
  120.6 5.4 copy.180
  126.1 5.9 fusion.120
  133.5 7.4 copy.176
  142.0 18.4 %fusion.40 = f32[6,256,12,64]{1,3,2,0:T(8,128)} fusion(f32[6,256,12,64]{1,3,2,0:T(8,128)} %copy.178, f32[6,256,12,64]{1,3,2,0:T(8,128)} %bitcast.225, f32[12]{0:T(128)S(1)} %copy-done.91, f32[6,256,12]{1,2,0:T(8,128)S(1)} %copy-done.30, bf16[6,256,12,64]{1,3,2,0:T(8,128)(2,1)} %copy.176, f32[6,12,256]{2,1,0:T(8,128)S(1)} %bitcast.258, ...), kind=kOutput, calls=%fused_computation.68 | convolution fusion | flops 3652190208 | bytes 18702384 | tf_op jit(solution)/shard_map/jvp(chij,cjhp->cihp)/dot_general | solution.py:48
  160.5 10.7 copy.219
  171.2 9.9 reshape.328
  181.2 10.2 multiply_reduce_fusion.11
  191.4 8.5 psum.133
  200.0 11.5 multiply_reduce_fusion.2
  211.5 6.2 psum.135
  217.8 12.3 multiply_reduce_fusion.3
  230.1 6.1 copy.185
  236.1 6.9 reshape.302
  243.1 19.6 %fusion.77 = f32[6,256,128]{2,1,0:T(8,128)} fusion(f32[6,12,128,64]{3,2,1,0:T(8,128)} %get-tuple-element.547, f32[6,256,12]{1,2,0:T(8,128)S(1)} %copy-done.30, f32[6,256,12,64]{1,0,3,2:T(8,128)} %reshape.302), kind=kOutput, calls=%fused_computation.129 | convolution fusion | flops 1813118976 | bytes 7938048 | tf_op jit(solution)/shard_map/transpose(jvp(cin,chnp->cihp))/dot_general | solution.py:63
  262.6 5.1 multiply_reduce_fusion.8
  267.7 4.9 fusion.70
  272.7 2.8 broadcast.168
  276.0 45.5 %while.35 = (s32[]{:T(128)}, f32[12,128,64]{2,1,0:T(8,128)}, f32[6,12,128,64]{3,2,1,0:T(8,128)}, f32[6,12]{1,0:T(8,128)}, f32[6,12,128,64]{2,3,1,0:T(8,128)}, /*...) while((s32[]{:T(128)}, f32[12,128,64]{2,1,0:T(8,128)}, ...), condition=%wide.region_12.13_spmd.clone, body=%wide.region_10.12_spmd.clone.sunk | while | flops 589816 | bytes 4719024 | solution.py:61
  286.5 2.5 fusion.171
  294.3 2.5 fusion.171
  302.1 2.5 fusion.171
  309.9 2.5 fusion.171
  317.7 2.5 fusion.171
  321.5 18.7 %fusion.80 = f32[6,256,128]{2,1,0:T(8,128)S(1)} fusion(f32[6,12,128,64]{3,2,1,0:T(8,128)} %get-tuple-element.193, f32[6,256,12,64]{1,3,2,0:T(8,128)} %copy.178, f32[6,256,12]{1,2,0:T(8,128)} %copy-done.28), kind=kOutput, calls=%fused_computation.130 | convolution fusion | flops 1813118976 | bytes 7938048 | tf_op jit(solution)/shard_map/transpose(jvp(cjn,cjhp->chnp))/dot_general | solution.py:52
  340.3 8.7 multiply_reduce_fusion.9
  349.1 7.0 fusion.106
  356.2 23.7 %fusion.11 = (f32[6,12,256]{2,1,0:T(8,128)}, f32[6,12,256]{2,1,0:T(8,128)}, f32[6,12,256]{2,1,0:T(8,128)}, f32[6,256,256]{2,1,0:T(8,128)S(1)}) fusion(f32[6,12,256]{2,1,0:T(8,128)S(1)} %bitcast.259, f32[6,256,256]{2,1,0:T(8,128)S(1)} %copy-done.26, f32[6,12,256]{2,1,0:T(8,128)S(1)} %copy-done.25, pred[6,256,256]{2,1,0:T(8,128)(4,1)S(1)} %copy-done.35, ...), kind=kOutput, calls=%fused_computation.31 | convolution fusion | flops 3694209024 | bytes 10985472 | tf_op jit(solution)/shard_map/transpose(jvp(chij,cjhp->cihp))/dot_general | solution.py:48
  381.7 2.3 convolution_add_fusion.3
  386.3 14.9 %reduce-window.16 = f32[6,12,2,128]{3,1,2,0:T(8,128)S(1)} reduce-window(f32[6,12,2,128]{3,1,2,0:T(8,128)S(1)} %copy.201, f32[]{:T(128)} %constant.111.clone.1), window={size=1x1x1x128 pad=0_0x0_0x0_0x0_127}, to_apply=%region_19.20 | reduce-window | flops 2340864 | bytes 147460 | tf_op jit(solution)/shard_map/reduce-window.2
  401.9 24.3 %bitcast_add_fusion.2 = f32[6,256,12,64]{1,3,2,0:T(8,128)} fusion(f32[6,256,12,64]{1,3,2,0:T(8,128)} %get-tuple-element.428, f32[12]{0:T(128)} %param.34, f32[6,256,12]{1,2,0:T(8,128)S(1)} %copy-done.29, f32[6,12,256]{2,1,0:T(8,128)} %bitcast.257, f32[6,256,256]{2,1,0:T(8,128)} %fusion.119, f32[6,12,256]{2,1,0:T(8,128)S(1)} %copy-done.25, ...), kind=kOutput, calls=%fused_computation.62 | convolution fusion | flops 3652190208 | bytes 21061680 | tf_op jit(solution)/shard_map/transpose(jvp(chij,cjhp->cihp))/dot_general | solution.py:48
  426.2 10.7 copy.221
  436.9 10.0 reshape.329
  446.9 9.5 multiply_reduce_fusion.7
  456.5 2.6 multiply_reduce_fusion.6
  462.2 2.9 fusion.107
  465.1 6.5 fusion.122
  471.7 4.0 fusion.121
  477.2 5.1 convolution_add_fusion.1
  482.8 3.9 fusion.97
  486.7 9.6 fusion.124
  496.3 8.6 fusion.123
  505.0 6.6 fusion.63
  511.6 318.5 %all-reduce.34.cloned.1.call-done = (f32[1536,1536]{1,0:T(8,128)}, f32[1536,1536]{1,0:T(8,128)}, f32[1536,256]{1,0:T(8,128)}) async-done(((f32[1536,1536]{1,0:T(8,128)}, f32[1536,1536]{1,0:T(8,128)}, f32[1536,256]{1,0:T(8,128)}), (f32[1536,1536]{1,0:T(8,128)}, f32[1536,1536]{1,0:T(8,128)}, f32[1536,256]{1,0:T(8,128)})) %all-reduce.34.cloned.1.call-update) | async-done | bytes 20447248 | tf_op jit(solution)/shard_map/psum | solution.py:130
  830.1 3.3 multiply_reduce_fusion.15
  837.2 2.6 fusion.125
  840.7 9.4 fusion.21
  850.2 40.7 %all-reduce.26 = (f32[1536]{0:T(1024)}, f32[4,768]{1,0:T(4,128)}, f32[4,256]{1,0:T(4,128)}, f32[768]{0:T(1024)}, f32[256]{0:T(256)}, /*index=5*/f32[12]{0:T(128)}, f32[12]{0:T(128)}, f32[12]{0:T(128)}, f32[768]{0:T(1024)}) all-reduce(f32[1536]{0:T(1024)S(1)} %get-tuple-element.309, ...), channel_id=1, replica_groups=mesh['dp'=8,'tensor'=4] {'dp'}, use_global_device_ids=true, to_apply=%region_26.27 | all-reduce | flops 7460 | bytes 59680 | tf_op jit(solution)/shard_map/psum | solution.py:167
  890.8 17.0 %fusion.13 = (f32[1536,1536]{1,0:T(8,128)}, bf16[1536,1536]{1,0:T(8,128)(2,1)}) fusion(bf16[1536,1536]{1,0:T(8,128)(2,1)} %param.37, bf16[1536,1536]{1,0:T(8,128)(2,1)} %param.21, f32[1536,1536]{1,0:T(8,128)} %get-tuple-element.429, f32[1536]{0:T(1024)S(1)} %broadcast_multiply_fusion.8, f32[1536]{0:T(1024)S(1)} %copy-done.68, f32[1536]{0:T(1024)S(1)} %copy-done.55, ...), kind=kLoop, calls=%fused_computation.35 | loop fusion | flops 25952256 | bytes 42498048 | tf_op jit(solution)/shard_map/sub | solution.py:159
  907.8 418.2 %all-reduce.32.cloned.1.call-done = (f32[1536,768]{1,0:T(8,128)}, f32[1536,768]{1,0:T(8,128)}, f32[1536,12]{0,1:T(8,128)}, f32[1536,256]{1,0:T(8,128)}, f32[768,1536]{1,0:T(8,128)}) async-done(((f32[1536,768]{1,0:T(8,128)}, f32[1536,768]{1,0:T(8,128)}, f32[1536,12]{0,1:T(8,128)}, f32[1536,256]{1,0:T(8,128)}, f32[768,1536]{1,0:T(8,128)}), (f32[1536,768]{1,0:T(8,128)}, f32[1536,768]{1,0:T(8,128)}, ...) | async-done | bytes 15802384 | tf_op jit(solution)/shard_map/psum | solution.py:167
  1326.0 5.2 copy.308
  1331.2 2.4 copy.309
  (384 shorter events, 106.8 us)
Async XLA Ops:
  7.2 174.0 %copy-start = (bf16[1536,768]{1,0:T(8,128)(2,1)S(1)}, bf16[1536,768]{1,0:T(8,128)(2,1)}, u32[]{:S(2)}) copy-start(bf16[1536,768]{1,0:T(8,128)(2,1)} %param.24) | copy-start | bytes 7077892
  7.2 822.9 %all-reduce.34.cloned.1.call-start = ((), (), s32[]{:S(2)}) async-start(), calls=%async_computation.1 | async-start | bytes 40894464 | tf_op jit(solution)/shard_map/psum | solution.py:130
  12.6 6.4 copy-start.60
  12.6 6.4 copy-start.62
  12.7 6.4 copy-start.64
  12.7 6.4 copy-start.66
  18.4 7.2 copy-start.1
  19.1 46.2 %copy-start.37 = (f32[1536]{0:T(1024)}, f32[1536]{0:T(1024)S(1)}, u32[]{:S(2)}) copy-start(f32[1536]{0:T(1024)S(1)} %get-tuple-element.415) | copy-start | bytes 18436
  19.1 46.2 %copy-start.39 = (f32[1536]{0:T(1024)}, f32[1536]{0:T(1024)S(1)}, u32[]{:S(2)}) copy-start(f32[1536]{0:T(1024)S(1)} %get-tuple-element.413) | copy-start | bytes 18436
  19.1 46.2 %copy-start.41 = (f32[1536]{0:T(1024)}, f32[1536]{0:T(1024)S(1)}, u32[]{:S(2)}) copy-start(f32[1536]{0:T(1024)S(1)} %get-tuple-element.414) | copy-start | bytes 18436
  34.0 8.8 copy-start.92
  34.1 8.8 copy-start.45
  34.1 8.9 copy-start.87
  51.3 19.3 %copy-start.23 = (f32[6,12,256]{2,1,0:T(8,128)}, f32[6,12,256]{2,1,0:T(8,128)S(1)}, u32[]{:S(2)}) copy-start(f32[6,12,256]{2,1,0:T(8,128)S(1)} %reduce_window_sum.39) | copy-start | bytes 221188
  51.5 19.1 %copy-start.17 = (f32[6,256,12]{1,0,2:T(8,128)}, f32[6,256,12]{1,0,2:T(8,128)S(1)}, u32[]{:S(2)}) copy-start(f32[6,256,12]{1,0,2:T(8,128)S(1)} %reshape.299) | copy-start | bytes 221188
  51.5 9.9 copy-start.31
  65.2 6.0 slice-start.4
  65.3 6.0 slice-start.5
  68.8 9.0 copy-start.10
  69.7 8.1 copy-start.49
  69.7 8.1 copy-start.58
  69.9 8.0 copy-start.80
  71.2 6.6 copy-start.28
  126.0 5.9 copy-start.11
  133.5 7.4 copy-start.36
  133.5 8.5 copy-start.24
  133.5 8.5 copy-start.30
  133.5 8.5 copy-start.51
  133.5 8.5 copy-start.91
  181.2 18.8 %copy-start.44 = (f32[768]{0:T(1024)S(1)}, f32[768]{0:T(1024)}, u32[]{:S(2)}) copy-start(f32[768]{0:T(1024)} %param.35) | copy-start | bytes 9220
  181.2 18.8 %copy-start.56 = (f32[1536]{0:T(1024)S(1)}, f32[1536]{0:T(1024)}, u32[]{:S(2)}) copy-start(f32[1536]{0:T(1024)} %get-tuple-element.412) | copy-start | bytes 18436
  243.0 19.6 %copy-start.4 = (f32[6,256,12,64]{1,0,3,2:T(8,128)S(1)}, f32[6,256,12,64]{1,0,3,2:T(8,128)}, u32[]{:S(2)}) copy-start(f32[6,256,12,64]{1,0,3,2:T(8,128)} %reshape.302) | copy-start | bytes 14155780
  321.5 18.7 %copy-start.7 = (f32[6,12,128,64]{3,2,1,0:T(8,128)S(1)}, f32[6,12,128,64]{3,2,1,0:T(8,128)}, u32[]{:S(2)}) copy-start(f32[6,12,128,64]{3,2,1,0:T(8,128)} %get-tuple-element.193) | copy-start | bytes 7077892
  321.5 18.7 %copy-start.12 = (bf16[1536,128]{1,0:T(8,128)(2,1)S(1)}, bf16[1536,128]{1,0:T(8,128)(2,1)}, u32[]{:S(2)}) copy-start(bf16[1536,128]{1,0:T(8,128)(2,1)} %copy-done.10) | copy-start | bytes 1179652
  321.5 27.5 %slice-start.12 = ((s8[4718592]{0:T(1024)(128)(4,1)}), s8[4194304]{0:T(1024)(128)(4,1)S(1)}, s32[]{:S(2)}) async-start(s8[4718592]{0:T(1024)(128)(4,1)} %bitcast.229), calls=%async_computation.14 | async-start | bytes 8388608
  340.3 8.8 slice-start.13
  340.3 8.8 copy-start.89
  340.3 15.8 %slice-start.2 = ((s8[6291456]{0:T(1024)(128)(4,1)}), s8[4194304]{0:T(1024)(128)(4,1)S(1)}, s32[]{:S(2)}) async-start(s8[6291456]{0:T(1024)(128)(4,1)} %bitcast.216), calls=%async_computation.4 | async-start | bytes 8388608
  349.1 7.0 slice-start.3
  349.1 7.0 copy-start.22
  349.1 7.0 copy-start.25
  349.1 7.0 copy-start.26
  349.1 7.0 copy-start.35
  349.1 7.0 copy-start.52
  356.2 23.7 %copy-start.14 = (f32[6,256,128]{2,1,0:T(8,128)S(1)}, f32[6,256,128]{2,1,0:T(8,128)}, u32[]{:S(2)}) copy-start(f32[6,256,128]{2,1,0:T(8,128)} %fusion.77) | copy-start | bytes 2359300
  356.2 25.5 %copy-start.9 = (bf16[1536,128]{1,0:T(8,128)(2,1)S(1)}, bf16[1536,128]{1,0:T(8,128)(2,1)}, u32[]{:S(2)}) copy-start(bf16[1536,128]{1,0:T(8,128)(2,1)} %get-tuple-element.400) | copy-start | bytes 1179652
  379.9 22.0 %copy-start.29 = (f32[6,256,12]{1,2,0:T(8,128)S(1)}, f32[6,256,12]{1,2,0:T(8,128)}, u32[]{:S(2)}) copy-start(f32[6,256,12]{1,2,0:T(8,128)} %copy-done.28) | copy-start | bytes 221188
  436.9 10.0 copy-start.38
  436.9 19.6 %slice-start = ((s8[4718592]{0:T(1024)(128)(4,1)}), s8[524288]{0:T(1024)(128)(4,1)S(1)}, s32[]{:S(2)}) async-start(s8[4718592]{0:T(1024)(128)(4,1)} %bitcast.205), calls=%async_computation.2 | async-start | bytes 1048576
  446.9 9.6 slice-start.1
  446.9 9.6 copy-start.40
  446.9 9.6 copy-start.42
  465.1 6.5 copy-start.20
  471.7 5.5 copy-start.46
  482.4 843.6 %all-reduce.32.cloned.1.call-start = ((), (), s32[]{:S(2)}) async-start(), calls=%async_computation | async-start | bytes 31653888 | tf_op jit(solution)/shard_map/psum | solution.py:167
  486.7 9.6 copy-start.21
  486.7 18.2 %slice-start.8 = ((s8[4718592]{0:T(1024)(128)(4,1)}), s8[4194304]{0:T(1024)(128)(4,1)S(1)}, s32[]{:S(2)}) async-start(s8[4718592]{0:T(1024)(128)(4,1)} %bitcast.223), calls=%async_computation.10 | async-start | bytes 8388608
  486.7 18.2 %slice-start.14 = ((s8[4718592]{0:T(1024)(128)(4,1)}), s8[4194304]{0:T(1024)(128)(4,1)S(1)}, s32[]{:S(2)}) async-start(s8[4718592]{0:T(1024)(128)(4,1)} %bitcast.231), calls=%async_computation.16 | async-start | bytes 8388608
  496.3 8.6 slice-start.9
  496.3 8.6 slice-start.15
  496.3 8.6 copy-start.57
  840.7 9.4 copy-start.85
  840.7 50.1 %copy-start.68 = (f32[1536]{0:T(1024)S(1)}, f32[1536]{0:T(1024)}, u32[]{:S(2)}) copy-start(f32[1536]{0:T(1024)} %get-tuple-element.408) | copy-start | bytes 18436
  1326.0 10.0 slice-start.16
  (50 other events, 158.6 us)
Sparse Core Ops, SparseCore 0:
  482.5 347.5 all-reduce.33
  839.9 486.0 all-reduce.31
where the time goes:
time: 1350 us
  waiting for transfers between devices  737 us (55%)
  matrix products  231 us (17%)
  local copies, waits for them, and re-layouts  161 us (12%)
  other arithmetic  145 us (11%)
  blocking collectives  55.4 us (4%)
  between operations  15.7 us (1%)
    psum x1, waiting for transfers between devices, body(): lax.psum((grad_norm, grad_gate, grad_input, grad_step, grad_state, grad_c...  418 us
    psum x1, waiting for transfers between devices, body(): mix = lax.psum(partial_mix, 'tensor')  319 us
    dot_general x3, matrix products, ssd_scan(): y_diag = jnp.einsum('chij,cjhp->cihp', mixing, x_blk, precision=HIGH)  66.4 us
    reshape x6, local copies, waits for them, and re-layouts, ssd_scan(): x_blk = values.reshape(blocks, group, heads, width)  54.7 us
    psum x1, blocking collectives, body(): lax.psum((grad_norm, grad_gate, grad_input, grad_step, grad_state, grad_c...  40.7 us
    dot_general x5, matrix products, back_dot(): lax.dot_general(left, right, (((1,), (1,)), ((), ())), preferred_element_...  36.6 us
    dot_general x3, matrix products, ssd_scan(): local_state = jnp.einsum('cjn,cjhp->chnp', b_blk, weighted, precision=HIGH)  31.3 us
    dot_general x5, matrix products, cross_dot(): lax.dot_general(left, right, (((0,), (0,)), ((), ())), preferred_element_...  31.3 us
  transfers between devices with their start and end apart: 2, of which 2 were waited for; matrix products, arithmetic and copies ran while one was open for 4% of the time, Pallas kernels for 0%

commit v1 on v0

v1 whole, which is shorter than its diff:
```python
from functools import partial

import jax
import jax.numpy as jnp
from jax import lax
from jax.experimental import pallas as pl
from jax.experimental.pallas import tpu as pltpu
from jax.sharding import PartitionSpec as P


GROUP = 256
LANES = 128
EPS = 1e-05
LOG2E = 1.4426950408889634
F32 = jnp.float32
BF16 = jnp.bfloat16

NN = (((1,), (0,)), ((), ()))
NT = (((1,), (1,)), ((), ()))
TN = (((0,), (0,)), ((), ()))


def mm(left, right, dims=NN):
    return lax.dot_general(left, right, dims, preferred_element_type=F32)


def halves(v):
    high = v.astype(BF16)
    return high, (v - high.astype(F32)).astype(BF16)


def thirds(v):
    high = v.astype(BF16)
    rest = v - high.astype(F32)
    mid = rest.astype(BF16)
    return high, mid, (rest - mid.astype(F32)).astype(BF16)


def expand(v, onehot):
    high, low = halves(v)
    return mm(high, onehot) + mm(low, onehot)


def head_sum(v, onehot):
    high, low = halves(v)
    return mm(high, onehot, NT) + mm(low, onehot, NT)


def head_onehot(channels, width, base=0):
    lane = lax.broadcasted_iota(jnp.int32, (LANES, channels), 0)
    chan = lax.broadcasted_iota(jnp.int32, (LANES, channels), 1)
    return (lane == base + chan // width).astype(F32).astype(BF16)


def step_terms(step_pre, seg_col, head_row, last_seg, prev_seg, group):
    raw = step_pre + head_row[0:1, :]
    step = jnp.maximum(raw, 0.0) + jnp.log1p(jnp.exp(-jnp.abs(raw)))
    rate2 = step * head_row[1:2, :]
    row = lax.broadcasted_iota(jnp.int32, (group, group), 0)
    col = lax.broadcasted_iota(jnp.int32, (group, group), 1)
    lower = (row >= col).astype(F32).astype(BF16)
    cum = sum(mm(lower, part) for part in thirds(rate2))
    last = cum[group - 1 : group, :]
    reach = jnp.where(seg_col == prev_seg, jnp.exp2(cum), 0.0)
    to_end = jnp.where(seg_col == last_seg, jnp.exp2(jnp.minimum(last - cum, 0.0)), 0.0)
    keep = jnp.exp2(last) * (last_seg == prev_seg).astype(F32)
    return raw, step, cum, reach, to_end, keep


def block_segments(seg_s, block, group):
    last = seg_s[block * group + group - 1].astype(F32)
    prev_at = jnp.maximum(block * group - 1, 0)
    prev = jnp.where(block > 0, seg_s[prev_at].astype(F32), -3.0)
    return last, prev


def forward_kernel(
    dims,
    seg_s, hid, seg_row, cot, norm_gain, gate_w, input_w, state_w, step_w,
    conv_w, conv_b, sconv_w, sconv_b, head_row, gng, out_w,
    normed_o, gate_o, u_o, z_o, sz_o, su_o, st_o, step_o, y_o, sin_o, dgn_o, sums_o,
    ubuf, vbuf, segbuf, carry, cum_t, cum_s, gram, xs_s,
):
    group, channels, _, width, state = dims
    block = pl.program_id(0)
    tiles = channels // LANES
    last_seg, prev_seg = block_segments(seg_s, block, group)

    @pl.when(block == 0)
    def _():
        ubuf[0:8, :] = jnp.zeros((8, channels), F32)
        vbuf[0:8, :] = jnp.zeros((8, 2 * state), F32)
        segbuf[0:8, :] = jnp.full((8, LANES), -2.0, F32)
        carry[...] = jnp.zeros_like(carry)

    h = hid[...].astype(F32)
    inverse = lax.rsqrt(jnp.mean(h * h, axis=1, keepdims=True) + EPS)
    normed = (h * inverse * norm_gain[...]).astype(BF16)
    normed_o[...] = normed
    step_pre = mm(normed, step_w[...])
    step_o[...] = step_pre
    ubuf[8:, :] = mm(normed, input_w[...])
    vbuf[8:, :] = mm(normed, state_w[...])
    gate_o[...] = mm(normed, gate_w[...])

    seg_mat = jnp.broadcast_to(seg_row[...], (group, group))
    seg_full = seg_mat.T
    seg_col = seg_full[:, :LANES]
    segbuf[8:, :] = seg_col
    valid = (seg_col >= 0.0).astype(F32)
    same = [(segbuf[8 - k : 8 - k + group, :] == seg_col).astype(F32) for k in range(1, 4)]

    _, step, cum, reach, to_end, keep = step_terms(
        step_pre, seg_col, head_row[...], last_seg, prev_seg, group
    )
    cum_s[...] = cum
    cum_t[...] = cum.T
    onehot = head_onehot(channels, width)

    for c in range(2 * state // LANES):
        s = slice(c * LANES, (c + 1) * LANES)
        z = sconv_b[:, s] + sconv_w[0:1, s] * vbuf[8:, s]
        for k in range(1, 4):
            z = z + sconv_w[k : k + 1, s] * (vbuf[8 - k : 8 - k + group, s] * same[k - 1])
        sz_o[:, s] = z
        su_o[:, s] = vbuf[8:, s]
        st_o[:, s] = (z * jax.nn.sigmoid(z)).astype(BF16)
    b_mat = st_o[:, :state]
    c_mat = st_o[:, state:]

    row = lax.broadcasted_iota(jnp.int32, (group, group), 0)
    col = lax.broadcasted_iota(jnp.int32, (group, group), 1)
    gram[...] = jnp.where((seg_full == seg_mat) & (row >= col), mm(c_mat, b_mat, NT), 0.0)

    sin_o[...] = carry[...]
    entering = carry[...].astype(BF16)
    b_t = b_mat.T
    lane = lax.broadcasted_iota(jnp.int32, (group, LANES), 1)
    half = group // 2
    square = jnp.zeros((group, LANES), F32)
    dotted = jnp.zeros((group, LANES), F32)
    keep_rows = jnp.broadcast_to(keep, (8, LANES))
    skip_rows = jnp.broadcast_to(head_row[2:3, :], (8, LANES))
    for c in range(tiles):
        s = slice(c * LANES, (c + 1) * LANES)
        hot = onehot[:, s]
        z = conv_b[:, s] + conv_w[0:1, s] * ubuf[8:, s]
        for k in range(1, 4):
            z = z + conv_w[k : k + 1, s] * (ubuf[8 - k : 8 - k + group, s] * same[k - 1])
        z_o[:, s] = z
        u_o[:, s] = ubuf[8:, s].astype(BF16)
        x = (z * jax.nn.sigmoid(z)).astype(BF16).astype(F32)
        xs = (expand(step, hot) * x).astype(BF16)
        xs_s[:, s] = xs
        weighted = (expand(to_end, hot) * xs.astype(F32)).astype(BF16)
        carry[:, s] = mm(b_t, weighted) + expand(keep_rows, hot)[0:1, :] * carry[:, s]
        y = mm(c_mat, entering[:, s]) * expand(reach, hot) + expand(skip_rows, hot)[0:1, :] * x
        top = y[:half]
        low = y[half:]
        pair = xs_s[:, s]
        per = LANES // width
        for q in range(per):
            head = c * per + q
            masked = jnp.where(lane // width == q, pair, jnp.zeros_like(pair))
            cum_row = cum_t[head : head + 1, :]
            diff = cum_s[:half, head : head + 1] - cum_row[:, :half]
            w = (jnp.exp2(jnp.minimum(diff, 0.0)) * gram[:half, :half]).astype(BF16)
            top = top + mm(w, masked[:half])
            diff = cum_s[half:, head : head + 1] - cum_row
            w = (jnp.exp2(jnp.minimum(diff, 0.0)) * gram[half:, :]).astype(BF16)
            low = low + mm(w, masked)
        y_o[:half, s] = top
        y_o[half:, s] = low
    for c in range(tiles):
        s = slice(c * LANES, (c + 1) * LANES)
        gate = gate_o[:, s]
        gated = y_o[:, s] * (gate * jax.nn.sigmoid(gate))
        d_gn = mm(cot[...], out_w[s, :], NT) * valid
        dgn_o[:, s] = d_gn
        square = square + gated * gated
        dotted = dotted + gated * (d_gn * gng[:, s])
    sums_o[...] = jnp.concatenate(
        [jnp.sum(square.T, axis=0, keepdims=True), jnp.sum(dotted.T, axis=0, keepdims=True)], axis=0
    )
    ubuf[0:8, :] = ubuf[group : group + 8, :]
    vbuf[0:8, :] = vbuf[group : group + 8, :]
    segbuf[0:8, :] = segbuf[group : group + 8, :]


def gate_kernel(dims, sums, seg_row, y_i, gate_i, dgn_i, gng, gn_o, dy_o, dgate_o, ggn_o):
    group, channels, inner = dims

    @pl.when(pl.program_id(0) == 0)
    def _():
        ggn_o[...] = jnp.zeros_like(ggn_o)

    def column(v):
        return jnp.broadcast_to(v, (LANES, group)).T

    valid = (column(seg_row[...]) >= 0.0).astype(F32)
    inverse = lax.rsqrt(column(sums[0:1, :]) / inner + EPS)
    pull = inverse * inverse * inverse * (column(sums[1:2, :]) / inner)
    inverse_v = inverse * valid
    for c in range(channels // LANES):
        s = slice(c * LANES, (c + 1) * LANES)
        y = y_i[:, s]
        gate = gate_i[:, s]
        d_gn = dgn_i[:, s]
        sig = jax.nn.sigmoid(gate)
        act = gate * sig
        gated = y * act
        gn_o[:, s] = (gated * inverse_v * gng[:, s]).astype(BF16)
        ggn_o[0:1, s] += jnp.sum(d_gn * gated * inverse, axis=0, keepdims=True)
        d_gated = inverse * (d_gn * gng[:, s]) - gated * pull
        dy_o[:, s] = (d_gated * act).astype(BF16)
        dgate_o[:, s] = (d_gated * y * sig * (1.0 + gate * (1.0 - sig))).astype(BF16)


def backward_kernel(
    dims, *refs
):
    group, channels, base, width, state, blocks, extra = dims
    seg_s, seg_row, dy_i, y_i, z_i, u_i, st_i, step_i, sin_i, conv_w, head_row = refs[:11]
    dinput_o, dstep_o, dstates_o, gconv_o, gcb_o, ghead_o = refs[11 + extra : 17 + extra]
    dzbuf, segbuf, carry, sdot, cum_t, cum_s, gram_t, dgram_t, w_mat, e_mat, s_mat = refs[17 + extra :]
    at = pl.program_id(0)
    block = blocks - 1 - at
    tiles = channels // LANES
    half = group // 2
    last_seg, prev_seg = block_segments(seg_s, block, group)

    @pl.when(at == 0)
    def _():
        dzbuf[group:, :] = jnp.zeros((8, channels), F32)
        segbuf[group:, :] = jnp.full((8, LANES), -5.0, F32)
        carry[...] = jnp.zeros_like(carry)
        sdot[...] = jnp.zeros_like(sdot)
        gconv_o[...] = jnp.zeros_like(gconv_o)
        gcb_o[...] = jnp.zeros_like(gcb_o)
        ghead_o[...] = jnp.zeros_like(ghead_o)

    seg_mat = jnp.broadcast_to(seg_row[...], (group, group))
    seg_full = seg_mat.T
    seg_col = seg_full[:, :LANES]
    segbuf[:group, :] = seg_col
    raw, step, cum, reach, to_end, keep = step_terms(
        step_i[...], seg_col, head_row[...], last_seg, prev_seg, group
    )
    cum_s[...] = cum
    cum_t[...] = cum.T
    onehot = head_onehot(channels, width, base)
    b_mat = st_i[:, :state]
    c_mat = st_i[:, state:]
    row = lax.broadcasted_iota(jnp.int32, (group, group), 0)
    col = lax.broadcasted_iota(jnp.int32, (group, group), 1)
    gram_t[...] = jnp.where((seg_full == seg_mat) & (row <= col), mm(b_mat, c_mat, NT), 0.0)
    dgram_t[...] = jnp.zeros_like(dgram_t)
    c_t = c_mat.T
    leaving = carry[...].astype(BF16)
    lane = lax.broadcasted_iota(jnp.int32, (group, LANES), 1)
    keep_rows = jnp.broadcast_to(keep, (8, LANES))
    skip_rows = jnp.broadcast_to(head_row[2:3, :], (8, LANES))
    masks = [(segbuf[k : k + group, :] == seg_col).astype(F32) for k in range(1, 4)]
    hs_step = jnp.zeros((group, LANES), F32)
    hs_row = jnp.zeros((group, LANES), F32)
    hs_skip = jnp.zeros((8, LANES), F32)
    hs_dot = jnp.zeros((8, LANES), F32)
    per = LANES // width
    for c in range(tiles):
        s = slice(c * LANES, (c + 1) * LANES)
        hot = onehot[:, s]
        z = z_i[:, s]
        sig = jax.nn.sigmoid(z)
        x = (z * sig).astype(BF16).astype(F32)
        step_x = expand(step, hot)
        pair = (step_x * x).astype(BF16)
        d_pair = dy_i[:, s]
        end_x = expand(to_end, hot)
        weighted = (end_x * pair.astype(F32)).astype(BF16)
        w_mat[:, s] = weighted
        from_next = mm(b_mat, leaving[:, s])
        top = jnp.zeros((half, LANES), F32)
        low = jnp.zeros((half, LANES), F32)
        for q in range(per):
            head = base + c * per + q
            pick = lane // width == q
            d_mask = jnp.where(pick, d_pair, jnp.zeros_like(d_pair))
            x_mask = jnp.where(pick, pair, jnp.zeros_like(pair))
            cum_row = cum_t[head : head + 1, :]
            decay = jnp.exp2(jnp.minimum(cum_row - cum_s[:half, head : head + 1], 0.0))
            top = top + mm((decay * gram_t[:half, :]).astype(BF16), d_mask)
            dgram_t[:half, :] += decay * mm(x_mask[:half], d_pair, NT)
            decay = jnp.exp2(jnp.minimum(cum_row[:, half:] - cum_s[half:, head : head + 1], 0.0))
            low = low + mm((decay * gram_t[half:, half:]).astype(BF16), d_mask[half:])
            dgram_t[half:, half:] += decay * mm(x_mask[half:], d_pair[half:], NT)
        d_inner = jnp.concatenate([top, low], axis=0)
        d_xs = d_inner + from_next * end_x
        d_y = d_pair.astype(F32)
        skip_x = expand(skip_rows, hot)[0:1, :]
        reach_x = expand(reach, hot)
        reached = (reach_x * d_y).astype(BF16)
        e_mat[:, s] = reached
        entering = sin_i[:, s]
        s_mat[:, s] = entering.astype(BF16)
        carried = mm(c_mat, s_mat[:, s])
        hs_step = hs_step + head_sum(d_xs * x, hot)
        hs_row = hs_row + head_sum(
            d_y * (y_i[:, s] - skip_x * x - reach_x * carried)
            + reached.astype(F32) * carried
            - d_inner * pair.astype(F32)
            - from_next * weighted.astype(F32),
            hot,
        )
        skip_col = jnp.sum(d_y * x, axis=0, keepdims=True)
        hs_skip = hs_skip + head_sum(jnp.broadcast_to(skip_col, (8, LANES)), hot)
        d_z = (step_x * d_xs + skip_x * d_y) * (sig * (1.0 + z * (1.0 - sig)))
        dzbuf[:group, s] = d_z
        u = u_i[:, s].astype(F32)
        gcb_o[0:1, s] += jnp.sum(d_z, axis=0, keepdims=True)
        gconv_o[0:1, s] += jnp.sum(d_z * u, axis=0, keepdims=True)
        d_u = conv_w[0:1, s] * d_z
        for k in range(1, 4):
            moved = dzbuf[k : k + group, s] * masks[k - 1]
            d_u = d_u + conv_w[k : k + 1, s] * moved
            gconv_o[k : k + 1, s] += jnp.sum(moved * u, axis=0, keepdims=True)
        dinput_o[:, s] = d_u.astype(BF16)
        new = mm(c_t, reached) + expand(keep_rows, hot)[0:1, :] * carry[:, s]
        carry[:, s] = new
        dot_col = jnp.sum(
            new.astype(BF16).astype(F32) * entering, axis=0, keepdims=True
        )
        hs_dot = hs_dot + head_sum(jnp.broadcast_to(dot_col, (8, LANES)), hot)
    d_gram_t = jnp.where((seg_full == seg_mat) & (row <= col), dgram_t[...], 0.0).astype(BF16)
    dstates_o[:, :state] = (mm(d_gram_t, c_mat) + mm(w_mat[...], leaving, NT)).astype(BF16)
    dstates_o[:, state:] = (
        mm(d_gram_t, b_mat, TN) + mm(e_mat[...], s_mat[...], NT)
    ).astype(BF16)

    final = lax.broadcasted_iota(jnp.int32, (group, LANES), 0) == group - 1
    d_cum = hs_row + jnp.where(final, sdot[0:1, :], 0.0)
    upper = (row <= col).astype(F32).astype(BF16)
    d_rate = sum(mm(upper, part) for part in thirds(d_cum))
    neg_a = head_row[3:4, :]
    d_step = (hs_step + neg_a * d_rate) * jax.nn.sigmoid(raw)
    dstep_o[...] = d_step.astype(BF16)
    ghead_o[0:1, :] += jnp.sum(d_step, axis=0, keepdims=True)
    ghead_o[1:2, :] += jnp.sum(d_rate * step, axis=0, keepdims=True) * neg_a
    ghead_o[2:3, :] += hs_skip[0:1, :]
    sdot[...] = hs_dot
    dzbuf[group:, :] = dzbuf[0:8, :]
    segbuf[group:, :] = segbuf[0:8, :]


def state_kernel(dims, place, seg_row, own, got, z_i, u_i, conv_w, dsp_o, gconv_o, gcb_o, dzbuf, segbuf):
    group, channels, blocks = dims
    at = pl.program_id(0)

    @pl.when(at == 0)
    def _():
        dzbuf[group:, :] = jnp.zeros((8, channels), F32)
        segbuf[group:, :] = jnp.full((8, LANES), -5.0, F32)
        gconv_o[...] = jnp.zeros_like(gconv_o)
        gcb_o[...] = jnp.zeros_like(gcb_o)

    seg_col = jnp.broadcast_to(seg_row[...], (LANES, group)).T
    segbuf[:group, :] = seg_col
    masks = [(segbuf[k : k + group, :] == seg_col).astype(F32) for k in range(1, 4)]
    mine = (blocks - 1 - at) // (blocks // 2) == place[0]
    for c in range(channels // LANES):
        s = slice(c * LANES, (c + 1) * LANES)
        z = z_i[:, s]
        sig = jax.nn.sigmoid(z)
        d_z = jnp.where(mine, own[:, s].astype(F32), got[:, s].astype(F32)) * (sig * (1.0 + z * (1.0 - sig)))
        dzbuf[:group, s] = d_z
        u = u_i[:, s]
        gcb_o[0:1, s] += jnp.sum(d_z, axis=0, keepdims=True)
        gconv_o[0:1, s] += jnp.sum(d_z * u, axis=0, keepdims=True)
        d_u = conv_w[0:1, s] * d_z
        for k in range(1, 4):
            moved = dzbuf[k : k + group, s] * masks[k - 1]
            d_u = d_u + conv_w[k : k + 1, s] * moved
            gconv_o[k : k + 1, s] += jnp.sum(moved * u, axis=0, keepdims=True)
        dsp_o[:, s] = d_u.astype(BF16)
    dzbuf[group:, :] = dzbuf[0:8, :]
    segbuf[group:, :] = segbuf[0:8, :]


def project_kernel(dg, di, ds, gate_w, input_w, step_w, *refs):
    total = mm(dg[...], gate_w[...], NT) + mm(di[...], input_w[...], NT)
    refs[-1][...] = (total + mm(ds[...], step_w[...], NT)).astype(BF16)


def final_kernel(half, place, own, got, sb_i, sw, hid, cot, norm_gain, gh_o, gn_o):
    @pl.when(pl.program_id(0) == 0)
    def _():
        gn_o[...] = jnp.zeros_like(gn_o)

    h = hid[...].astype(F32)
    inverse = lax.rsqrt(jnp.mean(h * h, axis=1, keepdims=True) + EPS)
    first = pl.program_id(0) < half
    summed = jnp.where(first, own[...].astype(F32), got[...].astype(F32))
    d_normed = summed + mm(sb_i[...], sw[...], NT)
    hi = h * inverse
    gn_o[0:1, :] += jnp.sum(d_normed * hi, axis=0, keepdims=True)
    scaled = d_normed * norm_gain[...]
    pull = jnp.mean(hi * scaled, axis=1, keepdims=True)
    gh_o[...] = cot[...].astype(F32) + inverse * (scaled - hi * pull)


def bits_of(size):
    return max(size.bit_length() - 1, 0)


def partner(x, axis, size, mask):
    return lax.ppermute(x, axis, [(i, i ^ mask) for i in range(size)])


def small_cost(us):
    return pl.CostEstimate(flops=0, transcendentals=0, bytes_accessed=int(us * 3.3e6))


def spread_kernel(count, place, keep, got, *refs):
    outs = refs[-count:]
    rows = outs[0].shape[0]
    for d in range(count):
        at = pl.multiple_of(place[1 + d] * rows, rows)
        outs[d][...] = (
            keep[pl.ds(at, rows), :].astype(F32) + got[pl.ds(at, rows), :].astype(F32)
        ).astype(BF16)


def spread_blocks_kernel(count, place, keep, got, *refs):
    outs = refs[-count:]
    for d in range(count):

        @pl.when(pl.program_id(0) == d)
        def _(d=d):
            outs[d][...] = (keep[...].astype(F32) + got[...].astype(F32)).astype(BF16)


def join_kernel(count, place, mine, got, out):
    rows = out.shape[0] // count

    def fill(source):
        for d in range(count):
            at = pl.multiple_of(place[1 + d] * rows, rows)
            out[pl.ds(at, rows), :] = source[d * rows : (d + 1) * rows, :].astype(out.dtype)

    @pl.when(pl.program_id(0) == 0)
    def _():
        fill(mine)

    @pl.when(pl.program_id(0) == 1)
    def _():
        fill(got)


def join_blocks_kernel(count, place, mine, got, out):
    @pl.when(pl.program_id(0) < count)
    def _():
        out[...] = mine[...].astype(F32)

    @pl.when(pl.program_id(0) >= count)
    def _():
        out[...] = got[...].astype(F32)


def start_reduce(x, axis, size):
    near = lax.axis_index(axis) & 1
    rows = x.shape[0] // 2
    send = lax.dynamic_slice_in_dim(x, (1 - near) * rows, rows, 0)
    return x, send, partner(send, axis, size, 1)


def near_reduce(started, axis, size, after=()):
    x, _, got = started
    me = lax.axis_index(axis)
    near, far = me & 1, me >> 1
    count = size // 2
    rows, cols = x.shape[0] // size, x.shape[1]
    order = jnp.stack([far ^ d for d in range(count)])
    outs = [jax.ShapeDtypeStruct((rows, cols), BF16)] * count
    out_spec = pl.BlockSpec((rows, cols), lambda i, pr: (0, 0))
    waits = [pl.BlockSpec(memory_space=pl.ANY)] * len(after)
    if rows % 16 == 0:
        place = jnp.concatenate([near[None], order]).astype(jnp.int32)
        return pl.pallas_call(
            partial(spread_kernel, count),
            name="spread_rows",
            cost_estimate=small_cost(3),
            out_shape=outs,
            grid_spec=pltpu.PrefetchScalarGridSpec(
                num_scalar_prefetch=1,
                grid=(1,),
                in_specs=[
                    pl.BlockSpec((rows * count, cols), lambda i, pr: (pr[0], 0)),
                    pl.BlockSpec((rows * count, cols), lambda i, pr: (0, 0)),
                ] + waits,
                out_specs=[out_spec] * count,
            ),
        )(place, x, got, *after)
    place = jnp.concatenate([near * count + order, order]).astype(jnp.int32)
    return pl.pallas_call(
        partial(spread_blocks_kernel, count),
        name="spread_rows",
        cost_estimate=small_cost(3),
        out_shape=outs,
        grid_spec=pltpu.PrefetchScalarGridSpec(
            num_scalar_prefetch=1,
            grid=(count,),
            in_specs=[
                pl.BlockSpec((rows, cols), lambda i, pr: (pr[i], 0)),
                pl.BlockSpec((rows, cols), lambda i, pr: (pr[count + i], 0)),
            ] + waits,
            out_specs=[out_spec] * count,
        ),
    )(place, x, got, *after)


def add_kernel(count, *refs):
    total = refs[0][...].astype(F32)
    for d in range(1, count):
        total = total + refs[d][...].astype(F32)
    refs[-1][...] = total.astype(BF16)


def far_reduce(parts, axis, size, after=()):
    count = size // 2
    got = [parts[0]] + [partner(parts[d], axis, size, d << 1) for d in range(1, count)]
    spec = pl.BlockSpec(parts[0].shape, lambda: (0, 0))
    return pl.pallas_call(
        partial(add_kernel, count),
        name="add_rows",
        cost_estimate=small_cost(2),
        out_shape=jax.ShapeDtypeStruct(parts[0].shape, BF16),
        in_specs=[spec] * count + [pl.BlockSpec(memory_space=pl.ANY)] * len(after),
        out_specs=spec,
    )(*got, *after)


def gather_rows(x, axis, size):
    me = lax.axis_index(axis)
    near, far = me & 1, me >> 1
    count = size // 2
    rows, cols = x.shape
    mine = jnp.concatenate([x] + [partner(x, axis, size, d << 1) for d in range(1, count)], axis=0)
    got = partner(mine, axis, size, 1)
    order = jnp.stack([far ^ d for d in range(count)])
    if rows % 16 == 0:
        place = jnp.concatenate([near[None], order]).astype(jnp.int32)
        half = pl.BlockSpec((rows * count, cols), lambda i, pr: (0, 0))
        return pl.pallas_call(
            partial(join_kernel, count),
            name="join_rows",
            cost_estimate=small_cost(4),
            out_shape=jax.ShapeDtypeStruct((rows * size, cols), F32),
            grid_spec=pltpu.PrefetchScalarGridSpec(
                num_scalar_prefetch=1,
                grid=(2,),
                in_specs=[half, half],
                out_specs=pl.BlockSpec(
                    (rows * count, cols), lambda i, pr: (jnp.where(i == 0, pr[0], 1 - pr[0]), 0)
                ),
            ),
        )(place, mine, got)
    place = jnp.concatenate([near * count + order, (1 - near) * count + order])
    return pl.pallas_call(
        partial(join_blocks_kernel, count),
        name="join_rows",
        cost_estimate=small_cost(4),
        out_shape=jax.ShapeDtypeStruct((rows * size, cols), F32),
        grid_spec=pltpu.PrefetchScalarGridSpec(
            num_scalar_prefetch=1,
            grid=(size,),
            in_specs=[
                pl.BlockSpec((rows, cols), lambda i, pr: (jnp.minimum(i, count - 1), 0)),
                pl.BlockSpec((rows, cols), lambda i, pr: (jnp.maximum(i - count, 0), 0)),
            ],
            out_specs=pl.BlockSpec((rows, cols), lambda i, pr: (pr[i], 0)),
        ),
    )(place.astype(jnp.int32), mine, got)


def sum_doubling(x, axis, size):
    for b in range(bits_of(size)):
        x = x + partner(x, axis, size, 1 << b)
    return x


def start_half(x, axis, size):
    mine = lax.axis_index(axis) & 1
    half = x.shape[0] // 2
    send = lax.dynamic_slice_in_dim(x, (1 - mine) * half, half, 0)
    return x, partner(send, axis, size, 1)


def near_half(started, axis, size):
    x, got = started
    mine = lax.axis_index(axis) & 1
    keep = lax.dynamic_slice_in_dim(x, mine * got.shape[0], got.shape[0], 0)
    low = (keep.astype(F32) + got.astype(F32)).astype(BF16)
    if bits_of(size) < 2:
        return None, low, None
    return size, low, partner(low, axis, size, 2)


def far_half(state, axis, size):
    _, low, got = state
    total = low.astype(F32)
    if got is not None:
        total = total + got.astype(F32)
    for b in range(2, bits_of(size)):
        low = total.astype(BF16)
        total = low.astype(F32) + partner(low, axis, size, 1 << b).astype(F32)
    return total


def share_half(x, axis, size):
    return x, partner(x, axis, size, 1)


def paste_kernel(place, own, got, out):
    @pl.when(pl.program_id(0) == place[0])
    def _():
        out[...] = own[...]

    @pl.when(pl.program_id(0) != place[0])
    def _():
        out[...] = got[...]


def paste_halves(own, got, me):
    rows, cols = own.shape
    half = pl.BlockSpec((rows, cols), lambda i, pr: (0, 0))
    return pl.pallas_call(
        paste_kernel,
        name="paste_halves",
        cost_estimate=small_cost(4),
        out_shape=jax.ShapeDtypeStruct((rows * 2, cols), own.dtype),
        grid_spec=pltpu.PrefetchScalarGridSpec(
            num_scalar_prefetch=1,
            grid=(2,),
            in_specs=[half, half],
            out_specs=pl.BlockSpec((rows, cols), lambda i, pr: (i, 0)),
        ),
    )((me & 1).astype(jnp.int32).reshape(1), own, got)


def body(
    dp, tensor,
    hidden, segment_ids, norm_gain, gate_weight, input_weight, step_weight, state_weight,
    conv_weight, state_conv_weight, conv_bias, state_conv_bias, step_bias, decay_log,
    skip_gain, gate_norm_gain, out_weight, cotangent,
):
    tokens, model = hidden.shape
    channels = gate_weight.shape[1]
    heads = step_bias.shape[0]
    width = channels // heads
    state = state_weight.shape[1] // 2
    group = GROUP
    blocks = tokens // group
    me_t = lax.axis_index("tensor")
    side = (me_t & 1).astype(jnp.int32).reshape(1)

    seg_row = segment_ids.astype(F32).reshape(blocks, 1, group)
    pad = LANES - heads
    step_w = jnp.pad(step_weight, ((0, 0), (0, pad)))
    neg_a = -jnp.exp(decay_log)
    head_row = jnp.pad(
        jnp.stack([step_bias, neg_a * LOG2E, skip_gain, neg_a]), ((0, 4), (0, pad))
    )
    row2 = lambda v: v.reshape(1, -1)

    full = lambda shape: pl.BlockSpec(shape, lambda i, *_: (0,) * len(shape))
    once = lambda shape: pl.BlockSpec(
        shape, lambda i, *_: (0,) * len(shape), pipeline_mode=pl.Buffered(1)
    )
    tok = lambda cols: pl.BlockSpec((group, cols), lambda i, *_: (i, 0))
    segs = pl.BlockSpec((None, 1, group), lambda i, *_: (i, 0, 0))
    rev = lambda cols: pl.BlockSpec((group, cols), lambda i, *_: (blocks - 1 - i, 0))
    seg_rev = pl.BlockSpec((None, 1, group), lambda i, *_: (blocks - 1 - i, 0, 0))
    sds = jax.ShapeDtypeStruct
    cost = lambda us: pl.CostEstimate(
        flops=0, transcendentals=0, bytes_accessed=int(us * 3.3e6)
    )
    params = pltpu.CompilerParams(
        dimension_semantics=("arbitrary",), vmem_limit_bytes=60 * 1024 * 1024
    )

    (normed, gate_pre, u, z, state_z, state_u, states, step_pre, y, s_in, d_gn, sums) = pl.pallas_call(
        partial(forward_kernel, (group, channels, heads, width, state)),
        name="forward_scan",
        cost_estimate=cost(40),
        out_shape=(
            sds((tokens, model), BF16),
            sds((tokens, channels), F32),
            sds((tokens, channels), BF16),
            sds((tokens, channels), F32),
            sds((tokens, 2 * state), F32),
            sds((tokens, 2 * state), F32),
            sds((tokens, 2 * state), BF16),
            sds((tokens, LANES), F32),
            sds((tokens, channels), F32),
            sds((blocks, state, channels), F32),
            sds((tokens, channels), F32),
            sds((blocks, 2, group), F32),
        ),
        grid_spec=pltpu.PrefetchScalarGridSpec(
            num_scalar_prefetch=1,
            grid=(blocks,),
            in_specs=[
                tok(model), segs, tok(model), once((1, model)),
                once((model, channels)), once((model, channels)), once((model, 2 * state)),
                once((model, LANES)), once((4, channels)), once((1, channels)),
                once((4, 2 * state)), once((1, 2 * state)), once((8, LANES)),
                once((1, channels)), once((channels, model)),
            ],
            out_specs=[
                tok(model), tok(channels), tok(channels), tok(channels), tok(2 * state),
                tok(2 * state), tok(2 * state), tok(LANES), tok(channels),
                pl.BlockSpec((None, state, channels), lambda i, *_: (i, 0, 0)),
                tok(channels),
                pl.BlockSpec((None, 2, group), lambda i, *_: (i, 0, 0)),
            ],
            scratch_shapes=[
                pltpu.VMEM((group + 8, channels), F32),
                pltpu.VMEM((group + 8, 2 * state), F32),
                pltpu.VMEM((group + 8, LANES), F32),
                pltpu.VMEM((state, channels), F32),
                pltpu.VMEM((LANES, group), F32),
                pltpu.VMEM((group, LANES), F32),
                pltpu.VMEM((group, group), F32),
                pltpu.VMEM((group, channels), BF16),
            ],
        ),
        compiler_params=params,
    )(
        segment_ids, hidden, seg_row, cotangent, row2(norm_gain), gate_weight, input_weight,
        state_weight, step_w, conv_weight, row2(conv_bias), state_conv_weight,
        row2(state_conv_bias), head_row, row2(gate_norm_gain), out_weight,
    )

    sums = lax.psum(sums, "tensor")
    gnormed, d_y, d_gate, grad_gnorm = pl.pallas_call(
        partial(gate_kernel, (group, channels, float(channels * tensor))),
        name="gating",
        cost_estimate=cost(10),
        out_shape=(
            sds((tokens, channels), BF16), sds((tokens, channels), BF16),
            sds((tokens, channels), BF16), sds((8, channels), F32),
        ),
        grid_spec=pl.GridSpec(
            grid=(blocks,),
            in_specs=[
                pl.BlockSpec((None, 2, group), lambda i: (i, 0, 0)), segs,
                tok(channels), tok(channels), tok(channels), full((1, channels)),
            ],
            out_specs=[tok(channels), tok(channels), tok(channels), full((8, channels))],
        ),
        compiler_params=params,
    )(sums, seg_row, y, gate_pre, d_gn, row2(gate_norm_gain))

    g_out = start_reduce(mm(gnormed, cotangent, TN).astype(BF16), "dp", dp)
    mix = start_half(mm(gnormed, out_weight).astype(BF16), "tensor", tensor)
    g_gate = start_reduce(mm(normed, d_gate, TN).astype(BF16), "dp", dp)

    part = channels

    def backward(k, waits):
        revc = pl.BlockSpec((group, part), lambda i, *_: (blocks - 1 - i, k))
        return pl.pallas_call(
            partial(
                backward_kernel,
                (group, part, k * (heads // 2), width, state, blocks, len(waits)),
            ),
            name="backward_scan",
            cost_estimate=cost(42),
            out_shape=(
                sds((tokens, part), BF16), sds((tokens, LANES), BF16),
                sds((tokens, 2 * state), BF16), sds((8, part), F32),
                sds((8, part), F32), sds((8, LANES), F32),
            ),
            grid_spec=pltpu.PrefetchScalarGridSpec(
                num_scalar_prefetch=1,
                grid=(blocks,),
                in_specs=[
                    seg_rev, revc, revc, revc, revc, rev(2 * state), rev(LANES),
                    pl.BlockSpec((None, state, part), lambda i, *_: (blocks - 1 - i, 0, k)),
                    pl.BlockSpec((4, part), lambda i, *_: (0, k)), once((8, LANES)),
                ] + [pl.BlockSpec(memory_space=pl.ANY)] * len(waits),
                out_specs=[
                    rev(part), rev(LANES), rev(2 * state),
                    full((8, part)), full((8, part)), full((8, LANES)),
                ],
                scratch_shapes=[
                    pltpu.VMEM((group + 8, part), F32),
                    pltpu.VMEM((group + 8, LANES), F32),
                    pltpu.VMEM((state, part), F32),
                    pltpu.VMEM((8, LANES), F32),
                    pltpu.VMEM((LANES, group), F32),
                    pltpu.VMEM((group, LANES), F32),
                    pltpu.VMEM((group, group), F32),
                    pltpu.VMEM((group, group), F32),
                    pltpu.VMEM((group, part), BF16),
                    pltpu.VMEM((group, part), BF16),
                    pltpu.VMEM((state, part), BF16),
                ],
            ),
            compiler_params=params,
        )(
            segment_ids, seg_row, d_y, y, z, u, states, step_pre, s_in, conv_weight, head_row,
            *waits,
        )

    mix = near_half(mix, "tensor", tensor)
    d_input, d_step, d_states, grad_conv, grad_cb, grad_head = backward(
        0, [g_out[1], mix[1], g_gate[1]]
    )

    states_half = far_half(
        near_half(start_half(d_states, "tensor", tensor), "tensor", tensor), "tensor", tensor,
    ).astype(BF16)
    g_in = start_reduce(mm(normed, d_input, TN).astype(BF16), "dp", dp)
    g_out = near_reduce(g_out, "dp", dp, [d_step])
    g_gate = near_reduce(g_gate, "dp", dp, [d_step])
    local_back = pl.pallas_call(
        project_kernel,
        name="project_back",
        cost_estimate=cost(10),
        out_shape=sds((tokens, model), BF16),
        grid_spec=pl.GridSpec(
            grid=(blocks,),
            in_specs=[
                tok(channels), tok(channels), tok(LANES),
                once((model, channels)), once((model, channels)), once((model, LANES)),
            ] + [pl.BlockSpec(memory_space=pl.ANY)] * 3,
            out_specs=tok(model),
        ),
        compiler_params=params,
    )(
        d_gate, d_input, d_step, gate_weight, input_weight, step_w,
        g_in[1], g_gate[1], g_out[1],
    )
    back_half = near_half(start_half(local_back, "tensor", tensor), "tensor", tensor)
    mix_half = far_half(mix, "tensor", tensor)
    d_states = share_half(states_half, "tensor", tensor)
    low = back_half[1]
    g_out = far_reduce(g_out, "dp", dp, [low])
    g_gate = far_reduce(g_gate, "dp", dp, [low])
    g_in = near_reduce(g_in, "dp", dp, [low])
    g_in = far_reduce(g_in, "dp", dp)
    back_half = far_half(back_half, "tensor", tensor).astype(BF16)

    state_b, grad_sconv, grad_scb = pl.pallas_call(
        partial(state_kernel, (group, 2 * state, blocks)),
        name="state_conv",
        cost_estimate=cost(6),
        out_shape=(
            sds((tokens, 2 * state), BF16), sds((8, 2 * state), F32), sds((8, 2 * state), F32),
        ),
        grid_spec=pltpu.PrefetchScalarGridSpec(
            num_scalar_prefetch=1,
            grid=(blocks,),
            in_specs=[
                seg_rev,
                pl.BlockSpec((group, 2 * state), lambda i, *_: (lax.rem(blocks - 1 - i, blocks // 2), 0)),
                pl.BlockSpec((group, 2 * state), lambda i, *_: (lax.rem(blocks - 1 - i, blocks // 2), 0)),
                rev(2 * state), rev(2 * state), full((4, 2 * state)),
            ],
            out_specs=[rev(2 * state), full((8, 2 * state)), full((8, 2 * state))],
            scratch_shapes=[
                pltpu.VMEM((group + 8, 2 * state), F32), pltpu.VMEM((group + 8, LANES), F32),
            ],
        ),
        compiler_params=params,
    )(side, seg_row, *d_states, state_z, state_u, state_conv_weight)

    rows_t = model // tensor
    normed_part = lax.dynamic_slice_in_dim(normed, me_t * rows_t, rows_t, 1)
    g_state = sum_doubling(mm(normed_part, state_b, TN), "dp", dp).astype(BF16)
    grad_step = mm(d_step, normed, TN)[:16]

    rows = tokens // 2
    hid_half = lax.dynamic_slice_in_dim(hidden, (me_t & 1) * rows, rows, 0)
    out_half = (hid_half.astype(F32) + mix_half).astype(BF16)
    block_out = paste_halves(*share_half(out_half, "tensor", tensor), me_t)
    back = share_half(back_half, "tensor", tensor)

    own_first = lambda cols: pl.BlockSpec(
        (group, cols), lambda i, pr: (lax.rem(i + pr[0] * (blocks // 2), blocks), 0)
    )
    grad_hidden, grad_norm = pl.pallas_call(
        partial(final_kernel, blocks // 2),
        name="final_grad",
        cost_estimate=cost(12),
        out_shape=(sds((tokens, model), F32), sds((8, model), F32)),
        grid_spec=pltpu.PrefetchScalarGridSpec(
            num_scalar_prefetch=1,
            grid=(blocks,),
            in_specs=[
                pl.BlockSpec((group, model), lambda i, pr: (jnp.minimum(i, blocks // 2 - 1), 0)),
                pl.BlockSpec((group, model), lambda i, pr: (jnp.maximum(i - blocks // 2, 0), 0)),
                own_first(2 * state), full((model, 2 * state)), own_first(model),
                own_first(model), full((1, model)),
            ],
            out_specs=[own_first(model), full((8, model))],
        ),
        compiler_params=params,
    )(side, *back, state_b, state_weight, hidden, cotangent, row2(norm_gain))

    grad_out = gather_rows(g_out, "dp", dp)
    grad_gate = gather_rows(g_gate, "dp", dp)
    grad_input = gather_rows(g_in, "dp", dp)
    pieces = [g_state]
    for b in range(bits_of(tensor)):
        low = (me_t >> b) & 1
        pieces = [
            jnp.where(low == 0, jnp.concatenate([v, w]), jnp.concatenate([w, v]))
            for v, w in ((v, partner(v, "tensor", tensor, 1 << b)) for v in pieces)
        ]
    grad_state = pieces[0].astype(F32)

    def line(*parts):
        flat = jnp.concatenate([v.reshape(1, -1) for v in parts], axis=1)
        fill = -flat.shape[1] % model
        return jnp.pad(flat, ((0, 0), (0, fill))).reshape(-1, model)

    taps = conv_weight.shape[0]
    small = jnp.concatenate(
        [
            grad_step,
            grad_norm[0:1],
            line(grad_conv[:taps]),
            line(grad_cb[0:1], grad_gnorm[0:1]),
            line(grad_sconv[:taps], grad_scb[0:1]),
            line(grad_head[0:3]),
        ],
        axis=0,
    )
    fill = -small.shape[0] % 8
    small = sum_doubling(jnp.pad(small, ((0, fill), (0, 0))), "dp", dp)
    flat = small.reshape(-1)
    at = 0

    def take(count, shape):
        nonlocal at
        out = flat[at : at + count].reshape(shape)
        at += count
        return out

    def align():
        nonlocal at
        at += -at % model

    grad_step = small[:heads].T
    at = 16 * model
    grad_norm = take(model, (model,))
    grad_conv = take(taps * channels, (taps, channels))
    align()
    grad_cb = take(channels, (channels,))
    grad_gnorm = take(channels, (channels,))
    align()
    grad_sconv = take(taps * 2 * state, (taps, 2 * state))
    grad_scb = take(2 * state, (2 * state,))
    align()
    heads_out = take(3 * LANES, (3, LANES))
    grad_sbias, grad_decay, grad_skip = (heads_out[k, :heads] for k in range(3))
    return (
        block_out, grad_hidden, grad_norm, grad_gate, grad_input, grad_step, grad_state,
        grad_conv, grad_sconv, grad_cb, grad_scb, grad_sbias, grad_decay, grad_skip,
        grad_gnorm, grad_out,
    )


def solution(mesh):
    return jax.shard_map(
        partial(body, mesh.shape["dp"], mesh.shape["tensor"]),
        mesh=mesh,
        in_specs=(
            P("dp", None), P("dp"), P(), P(None, "tensor"), P(None, "tensor"),
            P(None, "tensor"), P(), P(None, "tensor"), P(), P("tensor"), P(), P("tensor"),
            P("tensor"), P("tensor"), P("tensor"), P("tensor", None), P("dp", None),
        ),
        out_specs=(
            P("dp", None), P("dp", None), P(), P(None, "tensor"), P(None, "tensor"),
            P(None, "tensor"), P(), P(None, "tensor"), P(), P("tensor"), P(), P("tensor"),
            P("tensor"), P("tensor"), P("tensor"), P("tensor", None),
        ),
        check_vma=False,
    )
```

time: 1350 us -> 547 us (0.41)
  waiting for transfers between devices: 737 us -> 168 us
  matrix products: 231 us -> 31.9 us
  Pallas kernels: 0 us -> 165 us
  local copies, waits for them, and re-layouts: 161 us -> 32.7 us
  other arithmetic: 145 us -> 30.9 us
  starting transfers between devices: 0.48 us -> 97.1 us
  blocking collectives: 55.4 us -> 14.4 us
  between operations: 15.7 us -> 1.4 us
    psum x2 -> x0, waiting for transfers between devices: 737 us -> none  [the longest x1 418 us: body(): lax.psum((grad_norm, grad_gate, grad_input, grad_step, grad_state, grad_c...]
    dot_general x26 -> x6, matrix products: 225 us -> 31.9 us  [mm(): return lax.dot_general(left, right, dims, preferred_element_type=F32)]
    ppermute x0 -> x41, waiting for transfers between devices: none -> 168 us  [partner(): return lax.ppermute(x, axis, [(i, i ^ mask) for i in range(size)])]
    pallas_call x0 -> x16, Pallas kernels: none -> 165 us  [the longest x1 42.6 us: backward(): pl.pallas_call(partial(backward_kernel, (group, part, k * (heads // 2), w...]
    ppermute x0 -> x41, starting transfers between devices: none -> 97.1 us  [partner(): return lax.ppermute(x, axis, [(i, i ^ mask) for i in range(size)])]
    reshape x20 -> x7, local copies, waits for them, and re-layouts: 83.3 us -> 5.09 us  [the longest x3 3.83 us: body(): row2 = lambda v: v.reshape(1, -1)]
    reduce_sum x18 -> x0, other arithmetic: 56 us -> none  [the longest x4 16.5 us: conv_silu(): summed = summed + weights[offset][None, :] * shifted * keeping[:, None]]
    psum x3 -> x1, blocking collectives: 55.4 us -> 14.4 us  [body(): sums = lax.psum(sums, 'tensor')]
  transfers between devices with their start and end apart: 2 -> 41, of which waited for: 2 -> 18; matrix products, arithmetic and copies ran while one was open for 4% -> 12% of each run, Pallas kernels for 0% -> 18%
where the time goes in v1:
time: 547 us; the launch traced here: 541 us
  waiting for transfers between devices  168 us (31%)
  Pallas kernels  165 us (30%)
  starting transfers between devices  97.1 us (18%)
  local copies, waits for them, and re-layouts  32.7 us (6%)
  matrix products  31.9 us (6%)
  other arithmetic  30.9 us (6%)
  blocking collectives  14.4 us (3%)
    ppermute x41, waiting for transfers between devices, partner(): return lax.ppermute(x, axis, [(i, i ^ mask) for i in range(size)])  168 us
    ppermute x41, starting transfers between devices, partner(): return lax.ppermute(x, axis, [(i, i ^ mask) for i in range(size)])  97.1 us
    pallas_call x1, Pallas kernels, backward(): pl.pallas_call(partial(backward_kernel, (group, part, k * (heads // 2), w...  42.6 us
    pallas_call x1, Pallas kernels, body(): pl.pallas_call(partial(forward_kernel, (group, channels, heads, width, st...  41.2 us
    dot_general x6, matrix products, mm(): return lax.dot_general(left, right, dims, preferred_element_type=F32)  31.9 us
    psum x1, blocking collectives, body(): sums = lax.psum(sums, 'tensor')  14.4 us
    pallas_call x3, Pallas kernels, gather_rows(): pl.pallas_call(partial(join_kernel, count), name='join_rows', cost_estima...  14 us
    pallas_call x1, Pallas kernels, body(): pl.pallas_call(project_kernel, name='project_back', cost_estimate=cost(10...  13.8 us
  transfers between devices with their start and end apart: 41, of which 18 were waited for; matrix products, arithmetic and copies ran while one was open for 12% of the time, Pallas kernels for 18%

profile of v1, /device:TPU:0, one launch (start us, length us, event | category | flops | bytes accessed | tf_op | source)
XLA Modules:
  0.0 540.7 jit_solution(12618936300387987177)
XLA Ops:
  9.6 41.2 %forward_scan.1 = (bf16[1536,1536]{1,0:T(8,128)(2,1)}, f32[1536,768]{1,0:T(8,128)}, bf16[1536,768]{1,0:T(8,128)(2,1)}, f32[1536,768]{1,0:T(8,128)}, f32[1536,256...) custom-call(s32[1536]{0:T(1024)} %refs_0_.1, ...), custom_call_target="tpu_custom_call" | custom-call | bytes 132000000 | tf_op jit(solution)/shard_map/forward_scan/pallas_call | solution.py:690
  50.8 14.4 %psum.7.sums = f32[6,2,256]{2,1,0:T(2,128)} all-reduce(f32[6,2,256]{2,1,0:T(2,128)} %get-tuple-element.55), channel_id=1, replica_groups=mesh['dp'=8,'tensor'=4] {'tensor'}, use_global_device_ids=true, to_apply=%region_0.1 | all-reduce | flops 3072 | bytes 24576 | tf_op jit(solution)/shard_map/psum | solution.py:743
  65.2 10.8 %gating.1 = (bf16[1536,768]{1,0:T(8,128)(2,1)}, bf16[1536,768]{1,0:T(8,128)(2,1)}, bf16[1536,768]{1,0:T(8,128)(2,1)}, f32[8,768]{1,0:T(8,128)}) custom-call(f32[6,2,256]{2,1,0:T(2,128)} %psum.7.sums, f32[6,1,256]{2,1,0:T(1,128)} %reshape.80.seg_row.refs_1_, f32[1536,768]{1,0:T(8,128)} %get-tuple-element.56.y_i.refs_3_, ...), custom_call_target="tpu_custom_call" | custom-call | bytes 33000000 | tf_op jit(solution)/shard_map/gating/pallas_call | solution.py:744
  76.0 7.1 %convolution_convert_fusion = bf16[1536,1536]{1,0:T(8,128)(2,1)} fusion(bf16[1536,768]{1,0:T(8,128)(2,1)} %get-tuple-element.59, bf16[768,1536]{1,0:T(8,128)(2,1)S(1)} %copy-done.10), kind=kOutput, calls=%fused_computation | convolution fusion | flops 3626237952 | bytes 9437184 | tf_op jit(solution)/shard_map/dot_general | solution.py:24
  83.1 3.4 constant_dynamic-slice_fusion.5
  86.5 6.4 %convolution_convert_fusion.3.keep = bf16[768,1536]{1,0:T(8,128)(2,1)S(1)} fusion(bf16[1536,768]{1,0:T(8,128)(2,1)S(1)} %copy-done.36, bf16[1536,1536]{1,0:T(8,128)(2,1)} %cot.3), kind=kOutput, calls=%fused_computation.7 | convolution fusion | flops 3625058304 | bytes 9437184 | tf_op jit(solution)/shard_map/dot_general | solution.py:24
  93.1 1.6 collective-permute-start.4
  95.9 6.2 %convolution_convert_fusion.2.keep = bf16[1536,768]{1,0:T(8,128)(2,1)S(1)} fusion(bf16[1536,1536]{1,0:T(8,128)(2,1)} %get-tuple-element.67, bf16[1536,768]{1,0:T(8,128)(2,1)S(1)} %copy-done.11), kind=kOutput, calls=%fused_computation.6 | convolution fusion | flops 3625058304 | bytes 9437184 | tf_op jit(solution)/shard_map/dot_general | solution.py:24
  103.4 1.5 collective-permute-start.3
  105.5 4.4 add_convert_fusion.3.refs_12_
  109.9 42.6 %backward_scan.1 = (bf16[1536,768]{1,0:T(8,128)(2,1)}, bf16[1536,128]{1,0:T(8,128)(2,1)}, bf16[1536,256]{1,0:T(8,128)(2,1)}, f32[8,768]{1,0:T(8,128)}, f32[8,768]{1,0:T(8,128)}, /*index=5*/f32[8,128]{1,0:T(8,128)}) custom-call(s32[1536]{0:T(1024)} %refs_0_.1, f32[6,1,256]{2,1,0:T(1,128)} %reshape.80.seg_row.refs_1_, ...), custom_call_target="tpu_custom_call" | custom-call | bytes 138600000 | tf_op jit(solution)/shard_map/backward_scan/pallas_call | solution.py:771
  152.5 3.7 spread_rows.4
  156.3 6.2 %convolution_convert_fusion.1.keep = bf16[1536,768]{1,0:T(8,128)(2,1)S(1)} fusion(bf16[1536,1536]{1,0:T(8,128)(2,1)} %get-tuple-element.67, bf16[1536,768]{1,0:T(8,128)(2,1)S(1)} %copy-done.12), kind=kOutput, calls=%fused_computation.5 | convolution fusion | flops 3625058304 | bytes 9437184 | tf_op jit(solution)/shard_map/dot_general | solution.py:24
  165.1 3.6 spread_rows.3
  168.7 13.8 %project_back.1 = bf16[1536,1536]{1,0:T(8,128)(2,1)} custom-call(bf16[1536,768]{1,0:T(8,128)(2,1)} %get-tuple-element.60.dg, bf16[1536,768]{1,0:T(8,128)(2,1)} %get-tuple-element.68.di, bf16[1536,128]{1,0:T(8,128)(2,1)} %get-tuple-element.69.refs_0_.ds, bf16[1536,768]{1,0:T(8,128)(2,1)} %gate_w.3, bf16[1536,768]{1,0:T(8,128)(2,1)} %input_w.3, ...), custom_call_target="tpu_custom_call" | custom-call | bytes 33000000 | tf_op jit(solution)/shard_map/project_back/pallas_call | solution.py:826
  182.5 2.0 constant_dynamic-slice_fusion.1
  184.7 4.3 collective-permute-done.5
  190.4 1.7 collective-permute-done.8
  192.2 1.6 collective-permute-start.9
  193.8 57.8 %collective-permute-done.9 = bf16[768,256]{1,0:T(8,128)(2,1)S(1)} collective-permute-done((bf16[768,256]{1,0:T(8,128)(2,1)S(1)}, bf16[768,256]{1,0:T(8,128)(2,1)S(1)}, u32[]{:S(2)}, u32[]{:S(2)}) %collective-permute-start.9) | collective-permute-done | bytes 393248 | tf_op jit(solution)/shard_map/ppermute | solution.py:415
  254.2 6.7 %state_conv.1 = (bf16[1536,256]{1,0:T(8,128)(2,1)}, f32[8,256]{1,0:T(8,128)}, f32[8,256]{1,0:T(8,128)}) custom-call(s32[1]{0:T(128)} %bitcast.place, f32[6,1,256]{2,1,0:T(1,128)} %reshape.80.seg_row.refs_1_, bf16[768,256]{1,0:T(8,128)(2,1)} %copy-done.13, bf16[768,256]{1,0:T(8,128)(2,1)} %copy-done.19, f32[1536,256]{1,0:T(8,128)} %get-tuple-element.73.z_i, ...), custom_call_target="tpu_custom_call" | custom-call | bytes 19800000 | tf_op jit(solution)/shard_map/state_conv/pallas_call | solution.py:854
  261.0 2.2 fusion
  263.7 1.6 collective-permute-start.34
  265.3 1.5 collective-permute-start.21
  266.8 8.4 %collective-permute-done.29 = f32[384,256]{1,0:T(8,128)S(1)} collective-permute-done((f32[384,256]{1,0:T(8,128)S(1)}, f32[384,256]{1,0:T(8,128)S(1)}, u32[]{:S(2)}, u32[]{:S(2)}) %collective-permute-start.29) | collective-permute-done | bytes 393248 | tf_op jit(solution)/shard_map/ppermute | solution.py:415
  275.2 2.6 collective-permute-start.35
  277.9 1.4 collective-permute-start.36
  280.1 3.7 add_convert_fusion.own
  283.8 13.5 %collective-permute-done.35.refs_2_ = bf16[96,1536]{1,0:T(8,128)(2,1)S(1)} collective-permute-done((bf16[96,1536]{1,0:T(8,128)(2,1)S(1)}, bf16[96,1536]{1,0:T(8,128)(2,1)S(1)}, u32[]{:S(2)}, u32[]{:S(2)}) %collective-permute-start.35) | collective-permute-done | bytes 294944 | tf_op jit(solution)/shard_map/ppermute | solution.py:415
  297.4 5.8 %collective-permute-start.14 = (bf16[192,768]{1,0:T(8,128)(2,1)S(1)}, bf16[192,768]{1,0:T(8,128)(2,1)S(1)}, u32[]{:S(2)}, u32[]{:S(2)}) collective-permute-start(bf16[192,768]{1,0:T(8,128)(2,1)S(1)} %copy-done.30), channel_id=1, source_target_pairs={{0,8},{4,12},{8,0},{12,4},{16,24},{20,28},{24,16},{28,20},{1,9},{5... | collective-permute-start | bytes 884744 | tf_op jit(solution)/shard_map/ppermute | solution.py:415
  303.2 2.0 collective-permute-start.15
  306.0 10.7 %collective-permute-done.14.refs_1_ = bf16[192,768]{1,0:T(8,128)(2,1)S(1)} collective-permute-done((bf16[192,768]{1,0:T(8,128)(2,1)S(1)}, bf16[192,768]{1,0:T(8,128)(2,1)S(1)}, u32[]{:S(2)}, u32[]{:S(2)}) %collective-permute-start.14) | collective-permute-done | bytes 294944 | tf_op jit(solution)/shard_map/ppermute | solution.py:415
  318.2 2.1 add_rows.5
  320.3 12.0 %collective-permute-start.16 = (bf16[192,768]{1,0:T(8,128)(2,1)}, bf16[192,768]{1,0:T(8,128)(2,1)S(1)}, u32[]{:S(2)}, u32[]{:S(2)}) collective-permute-start(bf16[192,768]{1,0:T(8,128)(2,1)} %get-tuple-element.86), channel_id=1, source_target_pairs={{0,24},{4,28},{8,16},{12,20},{16,8},{20,12},{24,0},{28,4},{1,25},{... | collective-permute-start | bytes 884744 | tf_op jit(solution)/shard_map/ppermute | solution.py:415
  332.4 3.7 fusion.3
  336.1 3.6 spread_rows.5
  340.5 11.0 %collective-permute-start.38 = (bf16[96,1536]{1,0:T(8,128)(2,1)S(1)}, bf16[96,1536]{1,0:T(8,128)(2,1)S(1)}, u32[]{:S(2)}, u32[]{:S(2)}) collective-permute-start(bf16[96,1536]{1,0:T(8,128)(2,1)S(1)} %copy-done.16), channel_id=1, source_target_pairs={{0,16},{4,20},{8,24},{12,28},{16,0},{20,4},{24,8},{28,12},{1,17},{... | collective-permute-start | bytes 884744 | tf_op jit(solution)/shard_map/ppermute | solution.py:415
  353.2 3.5 collective-permute-start.23
  356.6 4.0 add_convert_fusion.2.own
  360.7 12.3 %collective-permute-done.38 = bf16[96,1536]{1,0:T(8,128)(2,1)S(1)} collective-permute-done((bf16[96,1536]{1,0:T(8,128)(2,1)S(1)}, bf16[96,1536]{1,0:T(8,128)(2,1)S(1)}, u32[]{:S(2)}, u32[]{:S(2)}) %collective-permute-start.38) | collective-permute-done | bytes 294944 | tf_op jit(solution)/shard_map/ppermute | solution.py:415
  375.3 2.1 add_rows.3
  377.3 17.7 %collective-permute-start.17 = (bf16[192,768]{1,0:T(8,128)(2,1)}, bf16[192,768]{1,0:T(8,128)(2,1)S(1)}, u32[]{:S(2)}, u32[]{:S(2)}) collective-permute-start(bf16[192,768]{1,0:T(8,128)(2,1)} %add_rows.3), channel_id=1, source_target_pairs={{0,8},{4,12},{8,0},{12,4},{16,24},{20,28},{24,16},{28,20},{1,9},{5... | collective-permute-start | bytes 884744 | tf_op jit(solution)/shard_map/ppermute | solution.py:415
  395.1 2.3 collective-permute-done.23.refs_2_
  399.6 2.1 add_rows.4
  401.7 2.5 collective-permute-done.17
  404.3 15.0 %collective-permute-start.25 = (bf16[192,768]{1,0:T(8,128)(2,1)}, bf16[192,768]{1,0:T(8,128)(2,1)}, u32[]{:S(2)}, u32[]{:S(2)}) collective-permute-start(bf16[192,768]{1,0:T(8,128)(2,1)} %add_rows.4), channel_id=1, source_target_pairs={{0,8},{4,12},{8,0},{12,4},{16,24},{20,28},{24,16},{28,20},{1,9},{5... | collective-permute-start | bytes 884744 | tf_op jit(solution)/shard_map/ppermute | solution.py:415
  419.3 3.4 collective-permute-done.18
  425.0 13.5 %final_grad.1 = (f32[1536,1536]{1,0:T(8,128)}, f32[8,1536]{1,0:T(8,128)}) custom-call(s32[1]{0:T(128)} %bitcast.place, bf16[768,1536]{1,0:T(8,128)(2,1)} %add_convert_fusion.own, bf16[768,1536]{1,0:T(8,128)(2,1)} %collective-permute-done.7.got, bf16[1536,256]{1,0:T(8,128)(2,1)} %get-tuple-element.75.sb_i, bf16[1536,256]{1,0:T(8,128)(2,1)} %sw.1, ...), custom_call_target="tpu_custom_call" | custom-call | bytes 39600000 | tf_op jit(solution)/shard_map/final_grad/pallas_call | solution.py:892
  439.9 2.9 concatenate.41
  444.5 2.3 pad_maximum_fusion.mine
  448.5 1.5 collective-permute-start.20
  450.0 2.2 pad_maximum_fusion.1.mine
  454.1 4.7 collective-permute-start.12
  458.9 2.1 maximum_select_fusion.1
  462.8 1.7 add.84
  464.5 6.5 %collective-permute-done.33 = bf16[768,256]{1,0:T(8,128)(2,1)} collective-permute-done((bf16[768,256]{1,0:T(8,128)(2,1)}, bf16[768,256]{1,0:T(8,128)(2,1)}, u32[]{:S(2)}, u32[]{:S(2)}) %collective-permute-start.33) | collective-permute-done | bytes 393248 | tf_op jit(solution)/shard_map/ppermute | solution.py:415
  471.0 3.1 collective-permute-start.13
  474.1 2.7 fusion.2
  476.9 4.7 join_rows.5
  481.6 20.6 %collective-permute-done.20.got = bf16[768,768]{1,0:T(8,128)(2,1)} collective-permute-done((bf16[768,768]{1,0:T(8,128)(2,1)}, bf16[768,768]{1,0:T(8,128)(2,1)}, u32[]{:S(2)}, u32[]{:S(2)}) %collective-permute-start.20) | collective-permute-done | bytes 1179680 | tf_op jit(solution)/shard_map/ppermute | solution.py:415
  502.2 4.7 join_rows.3
  506.9 19.0 %collective-permute-done.28.got = bf16[768,768]{1,0:T(8,128)(2,1)} collective-permute-done((bf16[768,768]{1,0:T(8,128)(2,1)}, bf16[768,768]{1,0:T(8,128)(2,1)}, u32[]{:S(2)}, u32[]{:S(2)}) %collective-permute-start.28) | collective-permute-done | bytes 1179680 | tf_op jit(solution)/shard_map/ppermute | solution.py:415
  525.9 4.7 join_rows.4
  530.5 4.7 paste_halves.1
  (177 shorter events, 45.8 us)
Async XLA Ops:
  65.2 10.8 %copy-start.10 = (bf16[768,1536]{1,0:T(8,128)(2,1)S(1)}, bf16[768,1536]{1,0:T(8,128)(2,1)}, u32[]{:S(2)}) copy-start(bf16[768,1536]{1,0:T(8,128)(2,1)} %out_w.1) | copy-start | bytes 7077892
  86.5 19.0 %collective-permute-start = (bf16[768,1536]{1,0:T(8,128)(2,1)}, bf16[768,1536]{1,0:T(8,128)(2,1)}, u32[]{:S(2)}, u32[]{:S(2)}) collective-permute-start(bf16[768,1536]{1,0:T(8,128)(2,1)} %constant_dynamic-slice_fusion.5), channel_id=1, source_target_pairs={{0,1},{1,0},{2,3},{3,2},{4,5},{5,4},{6,7},{7,6},{8,9},{9,8},{10,11... | collective-permute-start | bytes 7077896 | tf_op jit(solution)/shard_map/ppermute | solution.py:415
  93.1 9.1 %copy-start.9 = (bf16[384,1536]{1,0:T(8,128)(2,1)}, bf16[384,1536]{1,0:T(8,128)(2,1)S(1)}, u32[]{:S(2)}) copy-start(bf16[384,1536]{1,0:T(8,128)(2,1)S(1)} %constant_dynamic-slice_fusion.4.refs_11_) | copy-start | bytes 3538948
  93.1 59.4 %collective-permute-start.4 = (bf16[384,1536]{1,0:T(8,128)(2,1)S(1)}, bf16[384,1536]{1,0:T(8,128)(2,1)}, u32[]{:S(2)}, u32[]{:S(2)}) collective-permute-start(bf16[384,1536]{1,0:T(8,128)(2,1)S(1)} %constant_dynamic-slice_fusion.4.refs_11_), channel_id=1, source_target_pairs={{0,4},{4,0},{8,12},{12,8},{16,20},{20,16},{24,28},{28,24},{1,5},{5... | collective-permute-start | bytes 3538952 | tf_op jit(solution)/shard_map/ppermute | solution.py:415
  102.2 7.7 %copy-start.5 = (bf16[1536,768]{1,0:T(8,128)(2,1)}, bf16[1536,768]{1,0:T(8,128)(2,1)S(1)}, u32[]{:S(2)}) copy-start(bf16[1536,768]{1,0:T(8,128)(2,1)S(1)} %convolution_convert_fusion.2.keep) | copy-start | bytes 7077892
  103.4 61.7 %collective-permute-start.3 = (bf16[768,768]{1,0:T(8,128)(2,1)}, bf16[768,768]{1,0:T(8,128)(2,1)}, u32[]{:S(2)}, u32[]{:S(2)}) collective-permute-start(bf16[768,768]{1,0:T(8,128)(2,1)} %constant_dynamic-slice_fusion.3.refs_13_), channel_id=1, source_target_pairs={{0,4},{4,0},{8,12},{12,8},{16,20},{20,16},{24,28},{28,24},{1,5},{5... | collective-permute-start | bytes 3538952 | tf_op jit(solution)/shard_map/ppermute | solution.py:415
  182.5 6.6 %copy-start.1 = (bf16[1536,1536]{1,0:T(8,128)(2,1)S(1)}, bf16[1536,1536]{1,0:T(8,128)(2,1)}, u32[]{:S(2)}) copy-start(bf16[1536,1536]{1,0:T(8,128)(2,1)} %project_back.1) | copy-start | bytes 14155780
  184.4 5.8 %copy-start.17 = (bf16[1536,256]{1,0:T(8,128)(2,1)S(1)}, bf16[1536,256]{1,0:T(8,128)(2,1)}, u32[]{:S(2)}) copy-start(bf16[1536,256]{1,0:T(8,128)(2,1)} %get-tuple-element.72) | copy-start | bytes 2359300
  184.4 4.6 collective-permute-start.5
  189.7 90.5 %copy-start = (bf16[768,1536]{1,0:T(8,128)(2,1)}, bf16[768,1536]{1,0:T(8,128)(2,1)S(1)}, u32[]{:S(2)}) copy-start(bf16[768,1536]{1,0:T(8,128)(2,1)S(1)} %add_convert_fusion.1.refs_4_.refs_0_) | copy-start | bytes 7077892
  189.7 89.6 %collective-permute-start.6 = (bf16[768,1536]{1,0:T(8,128)(2,1)S(1)}, bf16[768,1536]{1,0:T(8,128)(2,1)}, u32[]{:S(2)}, u32[]{:S(2)}) collective-permute-start(bf16[768,1536]{1,0:T(8,128)(2,1)S(1)} %add_convert_fusion.1.refs_4_.refs_0_), channel_id=1, source_target_pairs={{0,2},{1,3},{2,0},{3,1},{4,6},{5,7},{6,4},{7,5},{8,10},{9,11},{10,... | collective-permute-start | bytes 7077896 | tf_op jit(solution)/shard_map/ppermute | solution.py:415
  190.3 1.8 collective-permute-start.8
  192.2 59.4 %collective-permute-start.9 = (bf16[768,256]{1,0:T(8,128)(2,1)S(1)}, bf16[768,256]{1,0:T(8,128)(2,1)S(1)}, u32[]{:S(2)}, u32[]{:S(2)}) collective-permute-start(bf16[768,256]{1,0:T(8,128)(2,1)S(1)} %add_convert_fusion.5), channel_id=1, source_target_pairs={{0,2},{1,3},{2,0},{3,1},{4,6},{5,7},{6,4},{7,5},{8,10},{9,11},{10,... | collective-permute-start | bytes 1179656 | tf_op jit(solution)/shard_map/ppermute | solution.py:415
  251.7 1.8 collective-permute-start.10
  251.8 99.7 %collective-permute-start.1 = (bf16[768,1536]{1,0:T(8,128)(2,1)}, bf16[768,1536]{1,0:T(8,128)(2,1)}, u32[]{:S(2)}, u32[]{:S(2)}) collective-permute-start(bf16[768,1536]{1,0:T(8,128)(2,1)} %add_convert_fusion.3.refs_12_), channel_id=1, source_target_pairs={{0,2},{1,3},{2,0},{3,1},{4,6},{5,7},{6,4},{7,5},{8,10},{9,11},{10,... | collective-permute-start | bytes 7077896 | tf_op jit(solution)/shard_map/ppermute | solution.py:415
  260.9 14.2 %copy-start.38 = (bf16[96,1536]{1,0:T(8,128)(2,1)S(1)}, bf16[96,1536]{1,0:T(8,128)(2,1)}, u32[]{:S(2)}) copy-start(bf16[96,1536]{1,0:T(8,128)(2,1)} %get-tuple-element.92) | copy-start | bytes 884740
  261.0 16.9 %copy-start.37 = (bf16[96,1536]{1,0:T(8,128)(2,1)S(1)}, bf16[96,1536]{1,0:T(8,128)(2,1)}, u32[]{:S(2)}) copy-start(bf16[96,1536]{1,0:T(8,128)(2,1)} %get-tuple-element.93) | copy-start | bytes 884740
  263.1 12.1 %collective-permute-start.29 = (f32[384,256]{1,0:T(8,128)S(1)}, f32[384,256]{1,0:T(8,128)S(1)}, u32[]{:S(2)}, u32[]{:S(2)}) collective-permute-start(f32[384,256]{1,0:T(8,128)S(1)} %fusion), channel_id=1, source_target_pairs={{0,4},{4,0},{8,12},{12,8},{16,20},{20,16},{24,28},{28,24},{1,5},{5... | collective-permute-start | bytes 1179656 | tf_op jit(solution)/shard_map/ppermute | solution.py:415
  263.7 14.1 %collective-permute-start.34 = (bf16[96,1536]{1,0:T(8,128)(2,1)S(1)}, bf16[96,1536]{1,0:T(8,128)(2,1)S(1)}, u32[]{:S(2)}, u32[]{:S(2)}) collective-permute-start(bf16[96,1536]{1,0:T(8,128)(2,1)S(1)} %copy-done.31), channel_id=1, source_target_pairs={{0,8},{4,12},{8,0},{12,4},{16,24},{20,28},{24,16},{28,20},{1,9},{5... | collective-permute-start | bytes 884744 | tf_op jit(solution)/shard_map/ppermute | solution.py:415
  265.3 67.1 %collective-permute-start.21 = (bf16[768,768]{1,0:T(8,128)(2,1)S(1)}, bf16[768,768]{1,0:T(8,128)(2,1)}, u32[]{:S(2)}, u32[]{:S(2)}) collective-permute-start(bf16[768,768]{1,0:T(8,128)(2,1)S(1)} %copy-done.7), channel_id=1, source_target_pairs={{0,4},{4,0},{8,12},{12,8},{16,20},{20,16},{24,28},{28,24},{1,5},{5... | collective-permute-start | bytes 3538952 | tf_op jit(solution)/shard_map/ppermute | solution.py:415
  275.2 22.2 %collective-permute-start.35 = (bf16[96,1536]{1,0:T(8,128)(2,1)S(1)}, bf16[96,1536]{1,0:T(8,128)(2,1)S(1)}, u32[]{:S(2)}, u32[]{:S(2)}) collective-permute-start(bf16[96,1536]{1,0:T(8,128)(2,1)S(1)} %copy-done.38), channel_id=1, source_target_pairs={{0,16},{4,20},{8,24},{12,28},{16,0},{20,4},{24,8},{28,12},{1,17},{... | collective-permute-start | bytes 884744 | tf_op jit(solution)/shard_map/ppermute | solution.py:415
  277.9 19.5 %copy-start.30 = (bf16[192,768]{1,0:T(8,128)(2,1)S(1)}, bf16[192,768]{1,0:T(8,128)(2,1)}, u32[]{:S(2)}) copy-start(bf16[192,768]{1,0:T(8,128)(2,1)} %get-tuple-element.70.refs_1_) | copy-start | bytes 884740
  277.9 38.9 %copy-start.35 = (f32[8,128]{1,0:T(8,128)S(1)}, f32[8,128]{1,0:T(8,128)}, u32[]{:S(2)}) copy-start(f32[8,128]{1,0:T(8,128)} %get-tuple-element.83) | copy-start | bytes 12292
  277.9 39.7 %copy-start.33 = (f32[8,768]{1,0:T(8,128)S(1)}, f32[8,768]{1,0:T(8,128)}, u32[]{:S(2)}) copy-start(f32[8,768]{1,0:T(8,128)} %get-tuple-element.78) | copy-start | bytes 73732
  277.9 19.5 %collective-permute-start.36 = (bf16[96,1536]{1,0:T(8,128)(2,1)S(1)}, bf16[96,1536]{1,0:T(8,128)(2,1)S(1)}, u32[]{:S(2)}, u32[]{:S(2)}) collective-permute-start(bf16[96,1536]{1,0:T(8,128)(2,1)S(1)} %copy-done.37), channel_id=1, source_target_pairs={{0,24},{4,28},{8,16},{12,20},{16,8},{20,12},{24,0},{28,4},{1,25},{... | collective-permute-start | bytes 884744 | tf_op jit(solution)/shard_map/ppermute | solution.py:415
  279.3 23.9 %collective-permute-start.30 = (f32[384,256]{1,0:T(8,128)S(1)}, f32[384,256]{1,0:T(8,128)S(1)}, u32[]{:S(2)}, u32[]{:S(2)}) collective-permute-start(f32[384,256]{1,0:T(8,128)S(1)} %add.87), channel_id=1, source_target_pairs={{0,8},{4,12},{8,0},{12,4},{16,24},{20,28},{24,16},{28,20},{1,9},{5... | collective-permute-start | bytes 1179656 | tf_op jit(solution)/shard_map/ppermute | solution.py:415
  297.3 19.4 %copy-start.28 = (bf16[96,1536]{1,0:T(8,128)(2,1)}, bf16[96,1536]{1,0:T(8,128)(2,1)S(1)}, u32[]{:S(2)}) copy-start(bf16[96,1536]{1,0:T(8,128)(2,1)S(1)} %collective-permute-done.35.refs_2_) | copy-start | bytes 884740
  297.3 125.4 %collective-permute-start.7 = (bf16[768,1536]{1,0:T(8,128)(2,1)}, bf16[768,1536]{1,0:T(8,128)(2,1)}, u32[]{:S(2)}, u32[]{:S(2)}) collective-permute-start(bf16[768,1536]{1,0:T(8,128)(2,1)} %add_convert_fusion.own), channel_id=1, source_target_pairs={{0,1},{1,0},{2,3},{3,2},{4,5},{5,4},{6,7},{7,6},{8,9},{9,8},{10,11... | collective-permute-start | bytes 7077896 | tf_op jit(solution)/shard_map/ppermute | solution.py:415
  297.4 19.4 %copy-start.29 = (bf16[96,1536]{1,0:T(8,128)(2,1)}, bf16[96,1536]{1,0:T(8,128)(2,1)S(1)}, u32[]{:S(2)}) copy-start(bf16[96,1536]{1,0:T(8,128)(2,1)S(1)} %collective-permute-done.36.refs_3_) | copy-start | bytes 884740
  297.4 19.4 %collective-permute-start.14 = (bf16[192,768]{1,0:T(8,128)(2,1)S(1)}, bf16[192,768]{1,0:T(8,128)(2,1)S(1)}, u32[]{:S(2)}, u32[]{:S(2)}) collective-permute-start(bf16[192,768]{1,0:T(8,128)(2,1)S(1)} %copy-done.30), channel_id=1, source_target_pairs={{0,8},{4,12},{8,0},{12,4},{16,24},{20,28},{24,16},{28,20},{1,9},{5... | collective-permute-start | bytes 884744 | tf_op jit(solution)/shard_map/ppermute | solution.py:415
  303.2 17.1 %collective-permute-start.15 = (bf16[192,768]{1,0:T(8,128)(2,1)}, bf16[192,768]{1,0:T(8,128)(2,1)S(1)}, u32[]{:S(2)}, u32[]{:S(2)}) collective-permute-start(bf16[192,768]{1,0:T(8,128)(2,1)} %get-tuple-element.85), channel_id=1, source_target_pairs={{0,16},{4,20},{8,24},{12,28},{16,0},{20,4},{24,8},{28,12},{1,17},{... | collective-permute-start | bytes 884744 | tf_op jit(solution)/shard_map/ppermute | solution.py:415
  306.0 26.4 %copy-start.3 = (bf16[1536,128]{1,0:T(8,128)(2,1)S(1)}, bf16[1536,128]{1,0:T(8,128)(2,1)}, u32[]{:S(2)}) copy-start(bf16[1536,128]{1,0:T(8,128)(2,1)} %get-tuple-element.69.refs_0_.ds) | copy-start | bytes 1179652
  316.7 15.6 %copy-start.24 = (bf16[192,768]{1,0:T(8,128)(2,1)}, bf16[192,768]{1,0:T(8,128)(2,1)S(1)}, u32[]{:S(2)}) copy-start(bf16[192,768]{1,0:T(8,128)(2,1)S(1)} %collective-permute-done.14.refs_1_) | copy-start | bytes 884740
  316.7 35.7 %collective-permute-start.31 = (f32[384,256]{1,0:T(8,128)S(1)}, f32[384,256]{1,0:T(8,128)S(1)}, u32[]{:S(2)}, u32[]{:S(2)}) collective-permute-start(f32[384,256]{1,0:T(8,128)S(1)} %add.88), channel_id=1, source_target_pairs={{0,16},{4,20},{8,24},{12,28},{16,0},{20,4},{24,8},{28,12},{1,17},{... | collective-permute-start | bytes 1179656 | tf_op jit(solution)/shard_map/ppermute | solution.py:415
  320.3 12.1 %copy-start.25 = (bf16[192,768]{1,0:T(8,128)(2,1)}, bf16[192,768]{1,0:T(8,128)(2,1)S(1)}, u32[]{:S(2)}) copy-start(bf16[192,768]{1,0:T(8,128)(2,1)S(1)} %collective-permute-done.15.refs_2_) | copy-start | bytes 884740
  320.3 20.2 %collective-permute-start.16 = (bf16[192,768]{1,0:T(8,128)(2,1)}, bf16[192,768]{1,0:T(8,128)(2,1)S(1)}, u32[]{:S(2)}, u32[]{:S(2)}) collective-permute-start(bf16[192,768]{1,0:T(8,128)(2,1)} %get-tuple-element.86), channel_id=1, source_target_pairs={{0,24},{4,28},{8,16},{12,20},{16,8},{20,12},{24,0},{28,4},{1,25},{... | collective-permute-start | bytes 884744 | tf_op jit(solution)/shard_map/ppermute | solution.py:415
  332.3 20.1 %collective-permute-start.37 = (bf16[96,1536]{1,0:T(8,128)(2,1)}, bf16[96,1536]{1,0:T(8,128)(2,1)S(1)}, u32[]{:S(2)}, u32[]{:S(2)}) collective-permute-start(bf16[96,1536]{1,0:T(8,128)(2,1)} %add_rows.5), channel_id=1, source_target_pairs={{0,8},{4,12},{8,0},{12,4},{16,24},{20,28},{24,16},{28,20},{1,9},{5... | collective-permute-start | bytes 884744 | tf_op jit(solution)/shard_map/ppermute | solution.py:415
  340.5 12.0 %copy-start.27 = (bf16[192,768]{1,0:T(8,128)(2,1)}, bf16[192,768]{1,0:T(8,128)(2,1)S(1)}, u32[]{:S(2)}) copy-start(bf16[192,768]{1,0:T(8,128)(2,1)S(1)} %collective-permute-done.16.refs_3_) | copy-start | bytes 884740
  340.5 32.5 %collective-permute-start.38 = (bf16[96,1536]{1,0:T(8,128)(2,1)S(1)}, bf16[96,1536]{1,0:T(8,128)(2,1)S(1)}, u32[]{:S(2)}, u32[]{:S(2)}) collective-permute-start(bf16[96,1536]{1,0:T(8,128)(2,1)S(1)} %copy-done.16), channel_id=1, source_target_pairs={{0,16},{4,20},{8,24},{12,28},{16,0},{20,4},{24,8},{28,12},{1,17},{... | collective-permute-start | bytes 884744 | tf_op jit(solution)/shard_map/ppermute | solution.py:415
  351.5 22.3 %collective-permute-start.39 = (bf16[96,1536]{1,0:T(8,128)(2,1)S(1)}, bf16[96,1536]{1,0:T(8,128)(2,1)S(1)}, u32[]{:S(2)}, u32[]{:S(2)}) collective-permute-start(bf16[96,1536]{1,0:T(8,128)(2,1)S(1)} %copy-done.16), channel_id=1, source_target_pairs={{0,24},{4,28},{8,16},{12,20},{16,8},{20,12},{24,0},{28,4},{1,25},{... | collective-permute-start | bytes 884744 | tf_op jit(solution)/shard_map/ppermute | solution.py:415
  352.4 24.9 %collective-permute-start.22 = (bf16[192,768]{1,0:T(8,128)(2,1)}, bf16[192,768]{1,0:T(8,128)(2,1)}, u32[]{:S(2)}, u32[]{:S(2)}) collective-permute-start(bf16[192,768]{1,0:T(8,128)(2,1)} %get-tuple-element.88), channel_id=1, source_target_pairs={{0,8},{4,12},{8,0},{12,4},{16,24},{20,28},{24,16},{28,20},{1,9},{5... | collective-permute-start | bytes 884744 | tf_op jit(solution)/shard_map/ppermute | solution.py:415
  353.2 21.4 %copy-start.34 = (f32[8,256]{1,0:T(8,128)S(1)}, f32[8,256]{1,0:T(8,128)}, u32[]{:S(2)}) copy-start(f32[8,256]{1,0:T(8,128)} %get-tuple-element.81) | copy-start | bytes 24580
  353.2 44.2 %collective-permute-start.23 = (bf16[192,768]{1,0:T(8,128)(2,1)}, bf16[192,768]{1,0:T(8,128)(2,1)}, u32[]{:S(2)}, u32[]{:S(2)}) collective-permute-start(bf16[192,768]{1,0:T(8,128)(2,1)} %get-tuple-element.89), channel_id=1, source_target_pairs={{0,16},{4,20},{8,24},{12,28},{16,0},{20,4},{24,8},{28,12},{1,17},{... | collective-permute-start | bytes 884744 | tf_op jit(solution)/shard_map/ppermute | solution.py:415
  360.7 39.0 %copy-start.2 = (bf16[768,1536]{1,0:T(8,128)(2,1)}, bf16[768,1536]{1,0:T(8,128)(2,1)S(1)}, u32[]{:S(2)}) copy-start(bf16[768,1536]{1,0:T(8,128)(2,1)S(1)} %add_convert_fusion.2.own) | copy-start | bytes 7077892
  372.9 25.1 %collective-permute-start.24 = (bf16[192,768]{1,0:T(8,128)(2,1)}, bf16[192,768]{1,0:T(8,128)(2,1)}, u32[]{:S(2)}, u32[]{:S(2)}) collective-permute-start(bf16[192,768]{1,0:T(8,128)(2,1)} %get-tuple-element.90), channel_id=1, source_target_pairs={{0,24},{4,28},{8,16},{12,20},{16,8},{20,12},{24,0},{28,4},{1,25},{... | collective-permute-start | bytes 884744 | tf_op jit(solution)/shard_map/ppermute | solution.py:415
  373.8 156.7 %collective-permute-start.2 = (bf16[768,1536]{1,0:T(8,128)(2,1)S(1)}, bf16[768,1536]{1,0:T(8,128)(2,1)}, u32[]{:S(2)}, u32[]{:S(2)}) collective-permute-start(bf16[768,1536]{1,0:T(8,128)(2,1)S(1)} %add_convert_fusion.2.own), channel_id=1, source_target_pairs={{0,1},{1,0},{2,3},{3,2},{4,5},{5,4},{6,7},{7,6},{8,9},{9,8},{10,11... | collective-permute-start | bytes 7077896 | tf_op jit(solution)/shard_map/ppermute | solution.py:415
  377.3 26.9 %collective-permute-start.17 = (bf16[192,768]{1,0:T(8,128)(2,1)}, bf16[192,768]{1,0:T(8,128)(2,1)S(1)}, u32[]{:S(2)}, u32[]{:S(2)}) collective-permute-start(bf16[192,768]{1,0:T(8,128)(2,1)} %add_rows.3), channel_id=1, source_target_pairs={{0,8},{4,12},{8,0},{12,4},{16,24},{20,28},{24,16},{28,20},{1,9},{5... | collective-permute-start | bytes 884744 | tf_op jit(solution)/shard_map/ppermute | solution.py:415
  397.4 25.3 %collective-permute-start.18 = (bf16[192,768]{1,0:T(8,128)(2,1)}, bf16[192,768]{1,0:T(8,128)(2,1)}, u32[]{:S(2)}, u32[]{:S(2)}) collective-permute-start(bf16[192,768]{1,0:T(8,128)(2,1)} %add_rows.3), channel_id=1, source_target_pairs={{0,16},{4,20},{8,24},{12,28},{16,0},{20,4},{24,8},{28,12},{1,17},{... | collective-permute-start | bytes 884744 | tf_op jit(solution)/shard_map/ppermute | solution.py:415
  398.0 45.9 %collective-permute-start.19 = (bf16[192,768]{1,0:T(8,128)(2,1)}, bf16[192,768]{1,0:T(8,128)(2,1)}, u32[]{:S(2)}, u32[]{:S(2)}) collective-permute-start(bf16[192,768]{1,0:T(8,128)(2,1)} %add_rows.3), channel_id=1, source_target_pairs={{0,24},{4,28},{8,16},{12,20},{16,8},{20,12},{24,0},{28,4},{1,25},{... | collective-permute-start | bytes 884744 | tf_op jit(solution)/shard_map/ppermute | solution.py:415
  404.3 18.5 %copy-start.23 = (bf16[192,768]{1,0:T(8,128)(2,1)}, bf16[192,768]{1,0:T(8,128)(2,1)S(1)}, u32[]{:S(2)}) copy-start(bf16[192,768]{1,0:T(8,128)(2,1)S(1)} %collective-permute-done.17) | copy-start | bytes 884740
  404.3 42.5 %collective-permute-start.25 = (bf16[192,768]{1,0:T(8,128)(2,1)}, bf16[192,768]{1,0:T(8,128)(2,1)}, u32[]{:S(2)}, u32[]{:S(2)}) collective-permute-start(bf16[192,768]{1,0:T(8,128)(2,1)} %add_rows.4), channel_id=1, source_target_pairs={{0,8},{4,12},{8,0},{12,4},{16,24},{20,28},{24,16},{28,20},{1,9},{5... | collective-permute-start | bytes 884744 | tf_op jit(solution)/shard_map/ppermute | solution.py:415
  422.7 25.3 %collective-permute-start.26 = (bf16[192,768]{1,0:T(8,128)(2,1)}, bf16[192,768]{1,0:T(8,128)(2,1)}, u32[]{:S(2)}, u32[]{:S(2)}) collective-permute-start(bf16[192,768]{1,0:T(8,128)(2,1)} %add_rows.4), channel_id=1, source_target_pairs={{0,16},{4,20},{8,24},{12,28},{16,0},{20,4},{24,8},{28,12},{1,17},{... | collective-permute-start | bytes 884744 | tf_op jit(solution)/shard_map/ppermute | solution.py:415
  422.7 25.8 %collective-permute-start.27 = (bf16[192,768]{1,0:T(8,128)(2,1)}, bf16[192,768]{1,0:T(8,128)(2,1)}, u32[]{:S(2)}, u32[]{:S(2)}) collective-permute-start(bf16[192,768]{1,0:T(8,128)(2,1)} %add_rows.4), channel_id=1, source_target_pairs={{0,24},{4,28},{8,16},{12,20},{16,8},{20,12},{24,0},{28,4},{1,25},{... | collective-permute-start | bytes 884744 | tf_op jit(solution)/shard_map/ppermute | solution.py:415
  425.0 23.0 %copy-start.8 = (bf16[384,1536]{1,0:T(8,128)(2,1)}, bf16[384,1536]{1,0:T(8,128)(2,1)S(1)}, u32[]{:S(2)}) copy-start(bf16[384,1536]{1,0:T(8,128)(2,1)S(1)} %pad_maximum_fusion.2.mine) | copy-start | bytes 3538948
  442.9 7.1 %copy-start.15 = (bf16[192,768]{1,0:T(8,128)(2,1)S(1)}, bf16[192,768]{1,0:T(8,128)(2,1)}, u32[]{:S(2)}) copy-start(bf16[192,768]{1,0:T(8,128)(2,1)} %add_rows.4) | copy-start | bytes 884740
  443.9 8.9 %copy-start.14 = (f32[22,1536]{1,0:T(8,128)S(1)}, f32[22,1536]{1,0:T(8,128)}, u32[]{:S(2)}) copy-start(f32[22,1536]{1,0:T(8,128)} %concatenate.41) | copy-start | bytes 405508
  443.9 8.4 %collective-permute-start.11 = (f32[24,1536]{1,0:T(8,128)S(1)}, f32[24,1536]{1,0:T(8,128)S(1)}, u32[]{:S(2)}, u32[]{:S(2)}) collective-permute-start(f32[24,1536]{1,0:T(8,128)S(1)} %pad.24), channel_id=1, source_target_pairs={{0,4},{4,0},{8,12},{12,8},{16,20},{20,16},{24,28},{28,24},{1,5},{5... | collective-permute-start | bytes 442376 | tf_op jit(solution)/shard_map/ppermute | solution.py:415
  446.8 6.7 %collective-permute-start.32 = (bf16[384,256]{1,0:T(8,128)(2,1)S(1)}, bf16[384,256]{1,0:T(8,128)(2,1)S(1)}, u32[]{:S(2)}, u32[]{:S(2)}) collective-permute-start(bf16[384,256]{1,0:T(8,128)(2,1)S(1)} %copy-done.18), channel_id=1, source_target_pairs={{0,1},{1,0},{2,3},{3,2},{4,5},{5,4},{6,7},{7,6},{8,9},{9,8},{10,11... | collective-permute-start | bytes 589832 | tf_op jit(solution)/shard_map/ppermute | solution.py:415
  448.0 28.9 %collective-permute-start.40 = (bf16[384,1536]{1,0:T(8,128)(2,1)S(1)}, bf16[384,1536]{1,0:T(8,128)(2,1)}, u32[]{:S(2)}, u32[]{:S(2)}) collective-permute-start(bf16[384,1536]{1,0:T(8,128)(2,1)S(1)} %pad_maximum_fusion.2.mine), channel_id=1, source_target_pairs={{0,4},{4,0},{8,12},{12,8},{16,20},{20,16},{24,28},{28,24},{1,5},{5... | collective-permute-start | bytes 3538952 | tf_op jit(solution)/shard_map/ppermute | solution.py:415
  448.5 53.7 %collective-permute-start.20 = (bf16[768,768]{1,0:T(8,128)(2,1)}, bf16[768,768]{1,0:T(8,128)(2,1)}, u32[]{:S(2)}, u32[]{:S(2)}) collective-permute-start(bf16[768,768]{1,0:T(8,128)(2,1)} %pad_maximum_fusion.mine), channel_id=1, source_target_pairs={{0,4},{4,0},{8,12},{12,8},{16,20},{20,16},{24,28},{28,24},{1,5},{5... | collective-permute-start | bytes 3538952 | tf_op jit(solution)/shard_map/ppermute | solution.py:415
  452.3 73.6 %collective-permute-start.28 = (bf16[768,768]{1,0:T(8,128)(2,1)}, bf16[768,768]{1,0:T(8,128)(2,1)}, u32[]{:S(2)}, u32[]{:S(2)}) collective-permute-start(bf16[768,768]{1,0:T(8,128)(2,1)} %pad_maximum_fusion.1.mine), channel_id=1, source_target_pairs={{0,4},{4,0},{8,12},{12,8},{16,20},{20,16},{24,28},{28,24},{1,5},{5... | collective-permute-start | bytes 3538952 | tf_op jit(solution)/shard_map/ppermute | solution.py:415
  454.1 8.2 %collective-permute-start.12 = (f32[24,1536]{1,0:T(8,128)}, f32[24,1536]{1,0:T(8,128)}, u32[]{:S(2)}, u32[]{:S(2)}) collective-permute-start(f32[24,1536]{1,0:T(8,128)} %pad_add_fusion), channel_id=1, source_target_pairs={{0,8},{4,12},{8,0},{12,4},{16,24},{20,28},{24,16},{28,20},{1,9},{5... | collective-permute-start | bytes 442376 | tf_op jit(solution)/shard_map/ppermute | solution.py:415
  462.3 8.7 %collective-permute-start.33 = (bf16[768,256]{1,0:T(8,128)(2,1)}, bf16[768,256]{1,0:T(8,128)(2,1)}, u32[]{:S(2)}, u32[]{:S(2)}) collective-permute-start(bf16[768,256]{1,0:T(8,128)(2,1)} %maximum_select_fusion.1), channel_id=1, source_target_pairs={{0,2},{1,3},{2,0},{3,1},{4,6},{5,7},{6,4},{7,5},{8,10},{9,11},{10,... | collective-permute-start | bytes 1179656 | tf_op jit(solution)/shard_map/ppermute | solution.py:415
  471.0 64.3 %collective-permute-start.13 = (f32[24,1536]{1,0:T(8,128)}, f32[24,1536]{1,0:T(8,128)}, u32[]{:S(2)}, u32[]{:S(2)}) collective-permute-start(f32[24,1536]{1,0:T(8,128)} %add.84), channel_id=1, source_target_pairs={{0,16},{4,20},{8,24},{12,28},{16,0},{20,4},{24,8},{28,12},{1,17},{... | collective-permute-start | bytes 442376 | tf_op jit(solution)/shard_map/ppermute | solution.py:415
  (16 other events, 35.7 us)

commit v2 on v1

--- a/solution.py
+++ b/solution.py
@@ -37,13 +37,11 @@
 
 
 def expand(v, onehot):
-    high, low = halves(v)
-    return mm(high, onehot) + mm(low, onehot)
+    return mm(jnp.concatenate(halves(v), axis=1), jnp.concatenate([onehot, onehot], axis=0))
 
 
 def head_sum(v, onehot):
-    high, low = halves(v)
-    return mm(high, onehot, NT) + mm(low, onehot, NT)
+    return mm(jnp.concatenate(halves(v), axis=1), jnp.concatenate([onehot, onehot], axis=1), NT)
 
 
 def head_onehot(channels, width, base=0):
@@ -102,6 +100,7 @@
     ubuf[8:, :] = mm(normed, input_w[...])
     vbuf[8:, :] = mm(normed, state_w[...])
     gate_o[...] = mm(normed, gate_w[...])
+    dgn_o[...] = mm(cot[...], out_w[...], NT)
 
     seg_mat = jnp.broadcast_to(seg_row[...], (group, group))
     seg_full = seg_mat.T
@@ -159,23 +158,26 @@
         low = y[half:]
         pair = xs_s[:, s]
         per = LANES // width
+        upper_w, upper_x = [], []
         for q in range(per):
             head = c * per + q
             masked = jnp.where(lane // width == q, pair, jnp.zeros_like(pair))
             cum_row = cum_t[head : head + 1, :]
             diff = cum_s[:half, head : head + 1] - cum_row[:, :half]
             w = (jnp.exp2(jnp.minimum(diff, 0.0)) * gram[:half, :half]).astype(BF16)
-            top = top + mm(w, masked[:half])
+            upper_w.append(w)
+            upper_x.append(masked[:half])
             diff = cum_s[half:, head : head + 1] - cum_row
             w = (jnp.exp2(jnp.minimum(diff, 0.0)) * gram[half:, :]).astype(BF16)
             low = low + mm(w, masked)
+        top = top + mm(jnp.concatenate(upper_w, axis=1), jnp.concatenate(upper_x, axis=0))
         y_o[:half, s] = top
         y_o[half:, s] = low
     for c in range(tiles):
         s = slice(c * LANES, (c + 1) * LANES)
         gate = gate_o[:, s]
         gated = y_o[:, s] * (gate * jax.nn.sigmoid(gate))
-        d_gn = mm(cot[...], out_w[s, :], NT) * valid
+        d_gn = dgn_o[:, s] * valid
         dgn_o[:, s] = d_gn
         square = square + gated * gated
         dotted = dotted + gated * (d_gn * gng[:, s])
@@ -280,7 +282,7 @@
         w_mat[:, s] = weighted
         from_next = mm(b_mat, leaving[:, s])
         top = jnp.zeros((half, LANES), F32)
-        low = jnp.zeros((half, LANES), F32)
+        lower_w, lower_d = [], []
         for q in range(per):
             head = base + c * per + q
             pick = lane // width == q
@@ -291,8 +293,10 @@
             top = top + mm((decay * gram_t[:half, :]).astype(BF16), d_mask)
             dgram_t[:half, :] += decay * mm(x_mask[:half], d_pair, NT)
             decay = jnp.exp2(jnp.minimum(cum_row[:, half:] - cum_s[half:, head : head + 1], 0.0))
-            low = low + mm((decay * gram_t[half:, half:]).astype(BF16), d_mask[half:])
+            lower_w.append((decay * gram_t[half:, half:]).astype(BF16))
+            lower_d.append(d_mask[half:])
             dgram_t[half:, half:] += decay * mm(x_mask[half:], d_pair[half:], NT)
+        low = mm(jnp.concatenate(lower_w, axis=1), jnp.concatenate(lower_d, axis=0))
         d_inner = jnp.concatenate([top, low], axis=0)
         d_xs = d_inner + from_next * end_x
         d_y = d_pair.astype(F32)
@@ -581,9 +585,10 @@
     )(place.astype(jnp.int32), mine, got)
 
 
-def sum_doubling(x, axis, size):
+def sum_doubling(x, axis, size, hop=F32):
     for b in range(bits_of(size)):
-        x = x + partner(x, axis, size, 1 << b)
+        low = x.astype(hop)
+        x = low.astype(F32) + partner(low, axis, size, 1 << b).astype(F32)
     return x
 
 
@@ -740,7 +745,7 @@
         row2(state_conv_bias), head_row, row2(gate_norm_gain), out_weight,
     )
 
-    sums = lax.psum(sums, "tensor")
+    sums = sum_doubling(sums, "tensor", tensor)
     gnormed, d_y, d_gate, grad_gnorm = pl.pallas_call(
         partial(gate_kernel, (group, channels, float(channels * tensor))),
         name="gating",
@@ -761,8 +766,10 @@
     )(sums, seg_row, y, gate_pre, d_gn, row2(gate_norm_gain))
 
     g_out = start_reduce(mm(gnormed, cotangent, TN).astype(BF16), "dp", dp)
-    mix = start_half(mm(gnormed, out_weight).astype(BF16), "tensor", tensor)
-    g_gate = start_reduce(mm(normed, d_gate, TN).astype(BF16), "dp", dp)
+    mix = mm(gnormed, out_weight).astype(BF16)
+    mix = start_half(mix, "tensor", tensor)
+    g_gate = mm(normed, d_gate, TN).astype(BF16)
+    g_gate = start_reduce(g_gate, "dp", dp)
 
     part = channels
 
@@ -813,15 +820,16 @@
         )
 
     mix = near_half(mix, "tensor", tensor)
+    g_out = near_reduce(g_out, "dp", dp, [mix[1], g_gate[1]])
     d_input, d_step, d_states, grad_conv, grad_cb, grad_head = backward(
-        0, [g_out[1], mix[1], g_gate[1]]
+        0, [g_out[1]]
     )
 
     states_half = far_half(
         near_half(start_half(d_states, "tensor", tensor), "tensor", tensor), "tensor", tensor,
     ).astype(BF16)
     g_in = start_reduce(mm(normed, d_input, TN).astype(BF16), "dp", dp)
-    g_out = near_reduce(g_out, "dp", dp, [d_step])
+    g_out = far_reduce(g_out, "dp", dp, [d_step])
     g_gate = near_reduce(g_gate, "dp", dp, [d_step])
     local_back = pl.pallas_call(
         project_kernel,
@@ -839,13 +847,12 @@
         compiler_params=params,
     )(
         d_gate, d_input, d_step, gate_weight, input_weight, step_w,
-        g_in[1], g_gate[1], g_out[1],
+        g_in[1], g_gate[1], g_out,
     )
     back_half = near_half(start_half(local_back, "tensor", tensor), "tensor", tensor)
     mix_half = far_half(mix, "tensor", tensor)
     d_states = share_half(states_half, "tensor", tensor)
     low = back_half[1]
-    g_out = far_reduce(g_out, "dp", dp, [low])
     g_gate = far_reduce(g_gate, "dp", dp, [low])
     g_in = near_reduce(g_in, "dp", dp, [low])
     g_in = far_reduce(g_in, "dp", dp)
@@ -877,7 +884,7 @@
 
     rows_t = model // tensor
     normed_part = lax.dynamic_slice_in_dim(normed, me_t * rows_t, rows_t, 1)
-    g_state = sum_doubling(mm(normed_part, state_b, TN), "dp", dp).astype(BF16)
+    g_state = mm(normed_part, state_b, TN)
     grad_step = mm(d_step, normed, TN)[:16]
 
     rows = tokens // 2
@@ -911,6 +918,31 @@
     grad_out = gather_rows(g_out, "dp", dp)
     grad_gate = gather_rows(g_gate, "dp", dp)
     grad_input = gather_rows(g_in, "dp", dp)
+
+    def line(*parts):
+        flat = jnp.concatenate([v.reshape(1, -1) for v in parts], axis=1)
+        fill = -flat.shape[1] % model
+        return jnp.pad(flat, ((0, 0), (0, fill))).reshape(-1, model)
+
+    taps = conv_weight.shape[0]
+    small = jnp.concatenate(
+        [
+            grad_step,
+            line(grad_conv[:taps]),
+            line(grad_cb[0:1], grad_gnorm[0:1]),
+            line(grad_sconv[:taps], grad_scb[0:1]),
+            line(grad_head[0:3]),
+        ],
+        axis=0,
+    )
+    fill = -small.shape[0] % 8
+    small = jnp.pad(small, ((0, fill), (0, 0)))
+    lines = small.shape[0]
+    small = sum_doubling(
+        jnp.concatenate([small, g_state.reshape(-1, model)], axis=0), "dp", dp, BF16
+    )
+    g_state = small[lines:].reshape(rows_t, 2 * state).astype(BF16)
+    grad_norm = sum_doubling(grad_norm, "dp", dp)[0]
     pieces = [g_state]
     for b in range(bits_of(tensor)):
         low = (me_t >> b) & 1
@@ -920,25 +952,6 @@
         ]
     grad_state = pieces[0].astype(F32)
 
-    def line(*parts):
-        flat = jnp.concatenate([v.reshape(1, -1) for v in parts], axis=1)
-        fill = -flat.shape[1] % model
-        return jnp.pad(flat, ((0, 0), (0, fill))).reshape(-1, model)
-
-    taps = conv_weight.shape[0]
-    small = jnp.concatenate(
-        [
-            grad_step,
-            grad_norm[0:1],
-            line(grad_conv[:taps]),
-            line(grad_cb[0:1], grad_gnorm[0:1]),
-            line(grad_sconv[:taps], grad_scb[0:1]),
-            line(grad_head[0:3]),
-        ],
-        axis=0,
-    )
-    fill = -small.shape[0] % 8
-    small = sum_doubling(jnp.pad(small, ((0, fill), (0, 0))), "dp", dp)
     flat = small.reshape(-1)
     at = 0
 
@@ -954,7 +967,6 @@
 
     grad_step = small[:heads].T
     at = 16 * model
-    grad_norm = take(model, (model,))
     grad_conv = take(taps * channels, (taps, channels))
     align()
     grad_cb = take(channels, (channels,))

time: 547 us -> 489 us (0.89)
  waiting for transfers between devices: 168 us -> 130 us
  blocking collectives: 14.4 us -> 0 us
  starting transfers between devices: 97.1 us -> 87 us
    ppermute x41 -> x43, waiting for transfers between devices: 168 us -> 130 us  [partner(): return lax.ppermute(x, axis, [(i, i ^ mask) for i in range(size)])]
    psum x1 -> x0, blocking collectives: 14.4 us -> none  [body(): sums = lax.psum(sums, 'tensor')]
    ppermute x41 -> x43, starting transfers between devices: 97.1 us -> 87 us  [partner(): return lax.ppermute(x, axis, [(i, i ^ mask) for i in range(size)])]
  transfers between devices with their start and end apart: 41 -> 43, of which waited for: 18 -> 15; matrix products, arithmetic and copies ran while one was open for 12% -> 16% of each run, Pallas kernels for 18% -> 20%
where the time goes in v2:
time: 489 us; the launch traced here: 481 us
  Pallas kernels  160 us (33%)
  waiting for transfers between devices  130 us (27%)
  starting transfers between devices  87 us (18%)
  local copies, waits for them, and re-layouts  35.9 us (7%)
  other arithmetic  34.8 us (7%)
  matrix products  32.4 us (7%)
    ppermute x43, waiting for transfers between devices, partner(): return lax.ppermute(x, axis, [(i, i ^ mask) for i in range(size)])  130 us
    ppermute x43, starting transfers between devices, partner(): return lax.ppermute(x, axis, [(i, i ^ mask) for i in range(size)])  87 us
    pallas_call x1, Pallas kernels, backward(): pl.pallas_call(partial(backward_kernel, (group, part, k * (heads // 2), w...  41.2 us
    pallas_call x1, Pallas kernels, body(): pl.pallas_call(partial(forward_kernel, (group, channels, heads, width, st...  38.2 us
    dot_general x6, matrix products, mm(): return lax.dot_general(left, right, dims, preferred_element_type=F32)  32.4 us
    pallas_call x3, Pallas kernels, gather_rows(): pl.pallas_call(partial(join_kernel, count), name='join_rows', cost_estima...  14 us
    pallas_call x1, Pallas kernels, body(): pl.pallas_call(project_kernel, name='project_back', cost_estimate=cost(10...  13.7 us
    pallas_call x1, Pallas kernels, body(): pl.pallas_call(partial(final_kernel, blocks // 2), name='final_grad', cos...  13.2 us
  transfers between devices with their start and end apart: 43, of which 15 were waited for; matrix products, arithmetic and copies ran while one was open for 16% of the time, Pallas kernels for 20%

profile of v2, /device:TPU:0, one launch (start us, length us, event | category | flops | bytes accessed | tf_op | source)
XLA Modules:
  0.0 481.3 jit_solution(5346174646616720695)
XLA Ops:
  9.6 38.2 %forward_scan.1 = (bf16[1536,1536]{1,0:T(8,128)(2,1)}, f32[1536,768]{1,0:T(8,128)}, bf16[1536,768]{1,0:T(8,128)(2,1)}, f32[1536,768]{1,0:T(8,128)}, f32[1536,256...) custom-call(s32[1536]{0:T(1024)} %refs_0_.1, ...), custom_call_target="tpu_custom_call" | custom-call | bytes 132000000 | tf_op jit(solution)/shard_map/forward_scan/pallas_call | solution.py:695
  50.2 2.8 collective-permute-start.1
  53.0 1.7 collective-permute-done.1
  55.2 10.8 %gating.1 = (bf16[1536,768]{1,0:T(8,128)(2,1)}, bf16[1536,768]{1,0:T(8,128)(2,1)}, bf16[1536,768]{1,0:T(8,128)(2,1)}, f32[8,768]{1,0:T(8,128)}) custom-call(f32[6,2,256]{2,1,0:T(2,128)} %add.78.sums, f32[6,1,256]{2,1,0:T(1,128)} %reshape.88.seg_row.refs_1_, f32[1536,768]{1,0:T(8,128)} %get-tuple-element.56.y_i.refs_3_, ...), custom_call_target="tpu_custom_call" | custom-call | bytes 33000000 | tf_op jit(solution)/shard_map/gating/pallas_call | solution.py:749
  66.0 6.2 %convolution_convert_fusion = bf16[1536,1536]{1,0:T(8,128)(2,1)S(1)} fusion(bf16[1536,768]{1,0:T(8,128)(2,1)} %get-tuple-element.59, bf16[768,1536]{1,0:T(8,128)(2,1)S(1)} %copy-done.9), kind=kOutput, calls=%fused_computation | convolution fusion | flops 3626237952 | bytes 9437184 | tf_op jit(solution)/shard_map/dot_general | solution.py:24
  72.2 1.7 constant_dynamic-slice_fusion.5
  75.7 7.1 %convolution_convert_fusion.3.keep = bf16[768,1536]{1,0:T(8,128)(2,1)S(1)} fusion(bf16[1536,768]{1,0:T(8,128)(2,1)} %get-tuple-element.59, bf16[1536,1536]{1,0:T(8,128)(2,1)} %cot.3), kind=kOutput, calls=%fused_computation.7 | convolution fusion | flops 3625058304 | bytes 9437184 | tf_op jit(solution)/shard_map/dot_general | solution.py:24
  82.9 2.1 collective-permute-start.5
  85.0 6.3 %convolution_convert_fusion.2.keep = bf16[1536,768]{1,0:T(8,128)(2,1)S(1)} fusion(bf16[1536,1536]{1,0:T(8,128)(2,1)} %get-tuple-element.67, bf16[1536,768]{1,0:T(8,128)(2,1)S(1)} %copy-done.10), kind=kOutput, calls=%fused_computation.6 | convolution fusion | flops 3625058304 | bytes 9437184 | tf_op jit(solution)/shard_map/dot_general | solution.py:24
  93.8 3.7 add_convert_fusion.3.refs_0_
  97.5 14.5 %collective-permute-done.5.got = bf16[384,1536]{1,0:T(8,128)(2,1)} collective-permute-done((bf16[384,1536]{1,0:T(8,128)(2,1)S(1)}, bf16[384,1536]{1,0:T(8,128)(2,1)}, u32[]{:S(2)}, u32[]{:S(2)}) %collective-permute-start.5) | collective-permute-done | bytes 1179680 | tf_op jit(solution)/shard_map/ppermute | solution.py:419
  112.0 3.5 spread_rows.3
  115.5 2.1 collective-permute-start.7
  117.5 2.6 collective-permute-start.8
  120.1 41.2 %backward_scan.1 = (bf16[1536,768]{1,0:T(8,128)(2,1)}, bf16[1536,128]{1,0:T(8,128)(2,1)}, bf16[1536,256]{1,0:T(8,128)(2,1)}, f32[8,768]{1,0:T(8,128)}, f32[8,768]{1,0:T(8,128)}, /*index=5*/f32[8,128]{1,0:T(8,128)}) custom-call(s32[1536]{0:T(1024)} %refs_0_.1, f32[6,1,256]{2,1,0:T(1,128)} %reshape.88.seg_row.refs_1_, ...), custom_call_target="tpu_custom_call" | custom-call | bytes 138600000 | tf_op jit(solution)/shard_map/backward_scan/pallas_call | solution.py:778
  161.3 7.0 %convolution_convert_fusion.1.keep = bf16[1536,768]{1,0:T(8,128)(2,1)S(1)} fusion(bf16[1536,1536]{1,0:T(8,128)(2,1)} %get-tuple-element.67, bf16[1536,768]{1,0:T(8,128)(2,1)} %get-tuple-element.69.di), kind=kOutput, calls=%fused_computation.5 | convolution fusion | flops 3625058304 | bytes 9437184 | tf_op jit(solution)/shard_map/dot_general | solution.py:24
  168.4 3.6 spread_rows.4
  173.2 2.1 add_rows.3.refs_2_
  175.3 13.7 %project_back.1 = bf16[1536,1536]{1,0:T(8,128)(2,1)} custom-call(bf16[1536,768]{1,0:T(8,128)(2,1)} %get-tuple-element.60.dg, bf16[1536,768]{1,0:T(8,128)(2,1)} %get-tuple-element.69.di, bf16[1536,128]{1,0:T(8,128)(2,1)} %get-tuple-element.70.refs_0_.refs_4_.ds, bf16[1536,768]{1,0:T(8,128)(2,1)} %gate_w.3, bf16[1536,768]{1,0:T(8,128)(2,1)} %input_w.3, ...), custom_call_target="tpu_custom_call" | custom-call | bytes 33000000 | tf_op jit(solution)/shard_map/project_back/pallas_call | solution.py:834
  189.0 3.3 constant_dynamic-slice_fusion.1
  192.9 4.7 collective-permute-done.13
  197.8 1.8 collective-permute-start.14
  200.8 8.1 %collective-permute-done.14 = bf16[768,256]{1,0:T(8,128)(2,1)S(1)} collective-permute-done((bf16[768,256]{1,0:T(8,128)(2,1)S(1)}, bf16[768,256]{1,0:T(8,128)(2,1)S(1)}, u32[]{:S(2)}, u32[]{:S(2)}) %collective-permute-start.14) | collective-permute-done | bytes 393248 | tf_op jit(solution)/shard_map/ppermute | solution.py:419
  209.2 3.3 fusion.14
  212.6 1.8 collective-permute-start.26
  219.4 3.5 collective-permute-start.40
  222.9 6.7 %state_conv.1 = (bf16[1536,256]{1,0:T(8,128)(2,1)}, f32[8,256]{1,0:T(8,128)}, f32[8,256]{1,0:T(8,128)}) custom-call(s32[1]{0:T(128)} %bitcast.place, f32[6,1,256]{2,1,0:T(1,128)} %reshape.88.seg_row.refs_1_, bf16[768,256]{1,0:T(8,128)(2,1)} %copy-done.11, bf16[768,256]{1,0:T(8,128)(2,1)} %copy-done.18, f32[1536,256]{1,0:T(8,128)} %get-tuple-element.76.z_i, ...), custom_call_target="tpu_custom_call" | custom-call | bytes 19800000 | tf_op jit(solution)/shard_map/state_conv/pallas_call | solution.py:861
  229.6 3.1 add_convert_fusion.1.refs_4_.refs_0_
  234.7 2.5 fusion.2
  237.8 1.8 reshape.96
  239.6 2.8 concatenate.50
  244.0 6.7 %collective-permute-done.34 = bf16[88,1536]{1,0:T(8,128)(2,1)S(1)} collective-permute-done((bf16[88,1536]{1,0:T(8,128)(2,1)S(1)}, bf16[88,1536]{1,0:T(8,128)(2,1)S(1)}, u32[]{:S(2)}, u32[]{:S(2)}) %collective-permute-start.34) | collective-permute-done | bytes 270368 | tf_op jit(solution)/shard_map/ppermute | solution.py:419
  252.5 7.3 %collective-permute-done.41 = bf16[96,1536]{1,0:T(8,128)(2,1)S(1)} collective-permute-done((bf16[96,1536]{1,0:T(8,128)(2,1)}, bf16[96,1536]{1,0:T(8,128)(2,1)S(1)}, u32[]{:S(2)}, u32[]{:S(2)}) %collective-permute-start.41) | collective-permute-done | bytes 294944 | tf_op jit(solution)/shard_map/ppermute | solution.py:419
  259.9 5.1 %collective-permute-start.35 = (bf16[88,1536]{1,0:T(8,128)(2,1)S(1)}, bf16[88,1536]{1,0:T(8,128)(2,1)S(1)}, u32[]{:S(2)}, u32[]{:S(2)}) collective-permute-start(bf16[88,1536]{1,0:T(8,128)(2,1)S(1)} %add_convert_fusion.7), channel_id=1, source_target_pairs={{0,8},{4,12},{8,0},{12,4},{16,24},{20,28},{24,16},{28,20},{1,9},{5... | collective-permute-start | bytes 811016 | tf_op jit(solution)/shard_map/ppermute | solution.py:419
  264.9 2.2 pad_maximum_fusion.2.mine
  268.3 4.0 collective-permute-done.35
  274.0 3.5 spread_rows.5
  277.6 13.0 %collective-permute-done.20.refs_2_ = bf16[192,768]{1,0:T(8,128)(2,1)S(1)} collective-permute-done((bf16[192,768]{1,0:T(8,128)(2,1)}, bf16[192,768]{1,0:T(8,128)(2,1)S(1)}, u32[]{:S(2)}, u32[]{:S(2)}) %collective-permute-start.20) | collective-permute-done | bytes 294944 | tf_op jit(solution)/shard_map/ppermute | solution.py:419
  291.4 12.6 %collective-permute-start.27 = (bf16[192,768]{1,0:T(8,128)(2,1)}, bf16[192,768]{1,0:T(8,128)(2,1)S(1)}, u32[]{:S(2)}, u32[]{:S(2)}) collective-permute-start(bf16[192,768]{1,0:T(8,128)(2,1)} %get-tuple-element.85), channel_id=1, source_target_pairs={{0,8},{4,12},{8,0},{12,4},{16,24},{20,28},{24,16},{28,20},{1,9},{5... | collective-permute-start | bytes 884744 | tf_op jit(solution)/shard_map/ppermute | solution.py:419
  304.0 14.4 %collective-permute-done.11 = bf16[768,1536]{1,0:T(8,128)(2,1)} collective-permute-done((bf16[768,1536]{1,0:T(8,128)(2,1)S(1)}, bf16[768,1536]{1,0:T(8,128)(2,1)}, u32[]{:S(2)}, u32[]{:S(2)}) %collective-permute-start.11) | collective-permute-done | bytes 2359328 | tf_op jit(solution)/shard_map/ppermute | solution.py:419
  318.4 1.7 collective-permute-start.28
  320.1 3.0 add_convert_fusion.own
  323.2 2.9 add_rows.4
  326.1 2.5 collective-permute-start.22
  328.6 2.4 collective-permute-start.24
  331.0 4.8 collective-permute-done.28.refs_2_
  336.8 5.4 %add_convert_fusion.2.own = bf16[768,1536]{1,0:T(8,128)(2,1)} fusion(bf16[768,1536]{1,0:T(8,128)(2,1)} %collective-permute-done.3, bf16[768,1536]{1,0:T(8,128)(2,1)} %add_convert_fusion.3.refs_0_, bf16[1536,1536]{1,0:T(8,128)(2,1)} %hid.3, s32[]{:T(128)S(6)} %select_n.37), kind=kLoop, calls=%fused_computation.3 | loop fusion | flops 7077888 | bytes 9437188 | tf_op jit(solution)/shard_map/convert_element_type | solution.py:892
  342.2 12.4 %collective-permute-done.29.refs_3_ = bf16[192,768]{1,0:T(8,128)(2,1)S(1)} collective-permute-done((bf16[192,768]{1,0:T(8,128)(2,1)}, bf16[192,768]{1,0:T(8,128)(2,1)S(1)}, u32[]{:S(2)}, u32[]{:S(2)}) %collective-permute-start.29) | collective-permute-done | bytes 294944 | tf_op jit(solution)/shard_map/ppermute | solution.py:419
  355.4 4.7 join_rows.5
  360.0 2.1 add_rows.5
  362.2 17.9 %collective-permute-start.30 = (bf16[192,768]{1,0:T(8,128)(2,1)}, bf16[192,768]{1,0:T(8,128)(2,1)}, u32[]{:S(2)}, u32[]{:S(2)}) collective-permute-start(bf16[192,768]{1,0:T(8,128)(2,1)} %add_rows.5), channel_id=1, source_target_pairs={{0,8},{4,12},{8,0},{12,4},{16,24},{20,28},{24,16},{28,20},{1,9},{5... | collective-permute-start | bytes 884744 | tf_op jit(solution)/shard_map/ppermute | solution.py:419
  384.5 1.8 convert_element_type.146
  386.3 2.2 pad_maximum_fusion.mine
  388.5 5.4 %collective-permute-done.30 = bf16[192,768]{1,0:T(8,128)(2,1)} collective-permute-done((bf16[192,768]{1,0:T(8,128)(2,1)}, bf16[192,768]{1,0:T(8,128)(2,1)}, u32[]{:S(2)}, u32[]{:S(2)}) %collective-permute-start.30) | collective-permute-done | bytes 294944 | tf_op jit(solution)/shard_map/ppermute | solution.py:419
  394.0 9.8 %collective-permute-done.31 = bf16[192,768]{1,0:T(8,128)(2,1)} collective-permute-done((bf16[192,768]{1,0:T(8,128)(2,1)}, bf16[192,768]{1,0:T(8,128)(2,1)}, u32[]{:S(2)}, u32[]{:S(2)}) %collective-permute-start.31) | collective-permute-done | bytes 294944 | tf_op jit(solution)/shard_map/ppermute | solution.py:419
  404.3 2.2 pad_maximum_fusion.1.mine
  412.3 13.2 %final_grad.1 = (f32[1536,1536]{1,0:T(8,128)}, f32[8,1536]{1,0:T(8,128)}) custom-call(s32[1]{0:T(128)} %bitcast.place, bf16[768,1536]{1,0:T(8,128)(2,1)} %copy-done.1, bf16[768,1536]{1,0:T(8,128)(2,1)} %collective-permute-done.12.got, bf16[1536,256]{1,0:T(8,128)(2,1)} %get-tuple-element.78.sb_i, bf16[1536,256]{1,0:T(8,128)(2,1)} %sw.1, ...), custom_call_target="tpu_custom_call" | custom-call | bytes 39600000 | tf_op jit(solution)/shard_map/final_grad/pallas_call | solution.py:899
  427.4 21.6 %collective-permute-done.16 = f32[8,1536]{1,0:T(8,128)S(1)} collective-permute-done((f32[8,1536]{1,0:T(8,128)}, f32[8,1536]{1,0:T(8,128)S(1)}, u32[]{:S(2)}, u32[]{:S(2)}) %collective-permute-start.16) | collective-permute-done | bytes 49184 | tf_op jit(solution)/shard_map/ppermute | solution.py:419
  449.7 7.6 %collective-permute-start.17 = (f32[8,1536]{1,0:T(8,128)S(1)}, f32[8,1536]{1,0:T(8,128)S(1)}, u32[]{:S(2)}, u32[]{:S(2)}) collective-permute-start(f32[8,1536]{1,0:T(8,128)S(1)} %add.89), channel_id=1, source_target_pairs={{0,8},{4,12},{8,0},{12,4},{16,24},{20,28},{24,16},{28,20},{1,9},{5... | collective-permute-start | bytes 147464 | tf_op jit(solution)/shard_map/ppermute | solution.py:419
  460.4 3.6 collective-permute-start.18
  464.0 2.4 fusion.5
  466.4 4.7 join_rows.3
  471.1 4.7 join_rows.4
  475.8 4.7 paste_halves.1
  (168 shorter events, 53.3 us)
Async XLA Ops:
  47.8 1.6 collective-permute-start
  50.2 4.5 collective-permute-start.1
  55.2 10.8 %copy-start.9 = (bf16[768,1536]{1,0:T(8,128)(2,1)S(1)}, bf16[768,1536]{1,0:T(8,128)(2,1)}, u32[]{:S(2)}) copy-start(bf16[768,1536]{1,0:T(8,128)(2,1)} %out_w.1) | copy-start | bytes 7077892
  75.1 18.6 %collective-permute-start.2 = (bf16[768,1536]{1,0:T(8,128)(2,1)}, bf16[768,1536]{1,0:T(8,128)(2,1)}, u32[]{:S(2)}, u32[]{:S(2)}) collective-permute-start(bf16[768,1536]{1,0:T(8,128)(2,1)} %constant_dynamic-slice_fusion.5), channel_id=1, source_target_pairs={{0,1},{1,0},{2,3},{3,2},{4,5},{5,4},{6,7},{7,6},{8,9},{9,8},{10,11... | collective-permute-start | bytes 7077896 | tf_op jit(solution)/shard_map/ppermute | solution.py:419
  75.7 9.3 %copy-start.10 = (bf16[1536,768]{1,0:T(8,128)(2,1)S(1)}, bf16[1536,768]{1,0:T(8,128)(2,1)}, u32[]{:S(2)}) copy-start(bf16[1536,768]{1,0:T(8,128)(2,1)} %get-tuple-element.60.dg) | copy-start | bytes 7077892
  82.8 8.5 %copy-start.4 = (bf16[768,1536]{1,0:T(8,128)(2,1)}, bf16[768,1536]{1,0:T(8,128)(2,1)S(1)}, u32[]{:S(2)}) copy-start(bf16[768,1536]{1,0:T(8,128)(2,1)S(1)} %convolution_convert_fusion.3.keep) | copy-start | bytes 7077892
  82.8 10.9 %slice-start = ((s8[4718592]{0:T(1024)(128)(4,1)}), s8[4194304]{0:T(1024)(128)(4,1)S(1)}, s32[]{:S(2)}) async-start(s8[4718592]{0:T(1024)(128)(4,1)} %bitcast.42), calls=%async_computation | async-start | bytes 8388608
  82.9 29.0 %collective-permute-start.5 = (bf16[384,1536]{1,0:T(8,128)(2,1)S(1)}, bf16[384,1536]{1,0:T(8,128)(2,1)}, u32[]{:S(2)}, u32[]{:S(2)}) collective-permute-start(bf16[384,1536]{1,0:T(8,128)(2,1)S(1)} %constant_dynamic-slice_fusion.4), channel_id=1, source_target_pairs={{0,4},{4,0},{8,12},{12,8},{16,20},{20,16},{24,28},{28,24},{1,5},{5... | collective-permute-start | bytes 3538952 | tf_op jit(solution)/shard_map/ppermute | solution.py:419
  85.0 8.7 %slice-start.1 = ((s8[4718592]{0:T(1024)(128)(4,1)}), s8[524288]{0:T(1024)(128)(4,1)S(1)}, s32[]{:S(2)}) async-start(s8[4718592]{0:T(1024)(128)(4,1)} %bitcast.42), calls=%async_computation.1 | async-start | bytes 1048576
  92.8 4.7 copy-start.7
  92.8 75.6 %collective-permute-start.6 = (bf16[768,768]{1,0:T(8,128)(2,1)S(1)}, bf16[768,768]{1,0:T(8,128)(2,1)}, u32[]{:S(2)}, u32[]{:S(2)}) collective-permute-start(bf16[768,768]{1,0:T(8,128)(2,1)S(1)} %constant_dynamic-slice_fusion.3.refs_1_), channel_id=1, source_target_pairs={{0,4},{4,0},{8,12},{12,8},{16,20},{20,16},{24,28},{28,24},{1,5},{5... | collective-permute-start | bytes 3538952 | tf_op jit(solution)/shard_map/ppermute | solution.py:419
  115.5 57.7 %collective-permute-start.7 = (bf16[96,1536]{1,0:T(8,128)(2,1)}, bf16[96,1536]{1,0:T(8,128)(2,1)}, u32[]{:S(2)}, u32[]{:S(2)}) collective-permute-start(bf16[96,1536]{1,0:T(8,128)(2,1)} %get-tuple-element.68.refs_11_), channel_id=1, source_target_pairs={{0,8},{4,12},{8,0},{12,4},{16,24},{20,28},{24,16},{28,20},{1,9},{5... | collective-permute-start | bytes 884744 | tf_op jit(solution)/shard_map/ppermute | solution.py:419
  117.5 55.6 %collective-permute-start.8 = (bf16[96,1536]{1,0:T(8,128)(2,1)}, bf16[96,1536]{1,0:T(8,128)(2,1)}, u32[]{:S(2)}, u32[]{:S(2)}) collective-permute-start(bf16[96,1536]{1,0:T(8,128)(2,1)} %get-tuple-element.73), channel_id=1, source_target_pairs={{0,16},{4,20},{8,24},{12,28},{16,0},{20,4},{24,8},{28,12},{1,17},{... | collective-permute-start | bytes 884744 | tf_op jit(solution)/shard_map/ppermute | solution.py:419
  120.1 53.0 %collective-permute-start.9 = (bf16[96,1536]{1,0:T(8,128)(2,1)}, bf16[96,1536]{1,0:T(8,128)(2,1)}, u32[]{:S(2)}, u32[]{:S(2)}) collective-permute-start(bf16[96,1536]{1,0:T(8,128)(2,1)} %get-tuple-element.74), channel_id=1, source_target_pairs={{0,24},{4,28},{8,16},{12,20},{16,8},{20,12},{24,0},{28,4},{1,25},{... | collective-permute-start | bytes 884744 | tf_op jit(solution)/shard_map/ppermute | solution.py:419
  168.4 4.8 copy-start.3
  192.3 16.9 %copy-start.2 = (bf16[1536,128]{1,0:T(8,128)(2,1)S(1)}, bf16[1536,128]{1,0:T(8,128)(2,1)}, u32[]{:S(2)}) copy-start(bf16[1536,128]{1,0:T(8,128)(2,1)} %get-tuple-element.70.refs_0_.refs_4_.ds) | copy-start | bytes 1179652
  192.3 37.2 %collective-permute-start.10 = (bf16[768,1536]{1,0:T(8,128)(2,1)}, bf16[768,1536]{1,0:T(8,128)(2,1)}, u32[]{:S(2)}, u32[]{:S(2)}) collective-permute-start(bf16[768,1536]{1,0:T(8,128)(2,1)} %constant_dynamic-slice_fusion.1), channel_id=1, source_target_pairs={{0,1},{1,0},{2,3},{3,2},{4,5},{5,4},{6,7},{7,6},{8,9},{9,8},{10,11... | collective-permute-start | bytes 7077896 | tf_op jit(solution)/shard_map/ppermute | solution.py:419
  192.4 5.3 %collective-permute-start.13 = (bf16[768,256]{1,0:T(8,128)(2,1)S(1)}, bf16[768,256]{1,0:T(8,128)(2,1)S(1)}, u32[]{:S(2)}, u32[]{:S(2)}) collective-permute-start(bf16[768,256]{1,0:T(8,128)(2,1)S(1)} %constant_dynamic-slice_fusion), channel_id=1, source_target_pairs={{0,1},{1,0},{2,3},{3,2},{4,5},{5,4},{6,7},{7,6},{8,9},{9,8},{10,11... | collective-permute-start | bytes 1179656 | tf_op jit(solution)/shard_map/ppermute | solution.py:419
  197.8 11.2 %collective-permute-start.14 = (bf16[768,256]{1,0:T(8,128)(2,1)S(1)}, bf16[768,256]{1,0:T(8,128)(2,1)S(1)}, u32[]{:S(2)}, u32[]{:S(2)}) collective-permute-start(bf16[768,256]{1,0:T(8,128)(2,1)S(1)} %add_convert_fusion.5), channel_id=1, source_target_pairs={{0,2},{1,3},{2,0},{3,1},{4,6},{5,7},{6,4},{7,5},{8,10},{9,11},{10,... | collective-permute-start | bytes 1179656 | tf_op jit(solution)/shard_map/ppermute | solution.py:419
  209.1 9.5 %copy-start.27 = (f32[8,128]{1,0:T(8,128)S(1)}, f32[8,128]{1,0:T(8,128)}, u32[]{:S(2)}) copy-start(f32[8,128]{1,0:T(8,128)} %get-tuple-element.93) | copy-start | bytes 12292
  209.1 10.2 %collective-permute-start.15 = (bf16[768,256]{1,0:T(8,128)(2,1)S(1)}, bf16[768,256]{1,0:T(8,128)(2,1)S(1)}, u32[]{:S(2)}, u32[]{:S(2)}) collective-permute-start(bf16[768,256]{1,0:T(8,128)(2,1)S(1)} %add_convert_fusion.4.own), channel_id=1, source_target_pairs={{0,1},{1,0},{2,3},{3,2},{4,5},{5,4},{6,7},{7,6},{8,9},{9,8},{10,11... | collective-permute-start | bytes 1179656 | tf_op jit(solution)/shard_map/ppermute | solution.py:419
  212.6 55.1 %collective-permute-start.26 = (bf16[768,768]{1,0:T(8,128)(2,1)S(1)}, bf16[768,768]{1,0:T(8,128)(2,1)}, u32[]{:S(2)}, u32[]{:S(2)}) collective-permute-start(bf16[768,768]{1,0:T(8,128)(2,1)S(1)} %copy-done.6), channel_id=1, source_target_pairs={{0,4},{4,0},{8,12},{12,8},{16,20},{20,16},{24,28},{28,24},{1,5},{5... | collective-permute-start | bytes 3538952 | tf_op jit(solution)/shard_map/ppermute | solution.py:419
  214.4 114.2 %collective-permute-start.3 = (bf16[768,1536]{1,0:T(8,128)(2,1)}, bf16[768,1536]{1,0:T(8,128)(2,1)}, u32[]{:S(2)}, u32[]{:S(2)}) collective-permute-start(bf16[768,1536]{1,0:T(8,128)(2,1)} %add_convert_fusion.3.refs_0_), channel_id=1, source_target_pairs={{0,2},{1,3},{2,0},{3,1},{4,6},{5,7},{6,4},{7,5},{8,10},{9,11},{10,... | collective-permute-start | bytes 7077896 | tf_op jit(solution)/shard_map/ppermute | solution.py:419
  218.6 24.8 %collective-permute-start.39 = (bf16[96,1536]{1,0:T(8,128)(2,1)}, bf16[96,1536]{1,0:T(8,128)(2,1)}, u32[]{:S(2)}, u32[]{:S(2)}) collective-permute-start(bf16[96,1536]{1,0:T(8,128)(2,1)} %add_rows.3.refs_2_), channel_id=1, source_target_pairs={{0,8},{4,12},{8,0},{12,4},{16,24},{20,28},{24,16},{28,20},{1,9},{5... | collective-permute-start | bytes 884744 | tf_op jit(solution)/shard_map/ppermute | solution.py:419
  219.4 24.6 %collective-permute-start.40 = (bf16[96,1536]{1,0:T(8,128)(2,1)}, bf16[96,1536]{1,0:T(8,128)(2,1)}, u32[]{:S(2)}, u32[]{:S(2)}) collective-permute-start(bf16[96,1536]{1,0:T(8,128)(2,1)} %add_rows.3.refs_2_), channel_id=1, source_target_pairs={{0,16},{4,20},{8,24},{12,28},{16,0},{20,4},{24,8},{28,12},{1,17},{... | collective-permute-start | bytes 884744 | tf_op jit(solution)/shard_map/ppermute | solution.py:419
  229.6 5.1 %copy-start.15 = (bf16[1536,256]{1,0:T(8,128)(2,1)S(1)}, bf16[1536,256]{1,0:T(8,128)(2,1)}, u32[]{:S(2)}) copy-start(bf16[1536,256]{1,0:T(8,128)(2,1)} %get-tuple-element.78.sb_i) | copy-start | bytes 2359300
  232.7 41.4 %copy-start = (bf16[768,1536]{1,0:T(8,128)(2,1)}, bf16[768,1536]{1,0:T(8,128)(2,1)S(1)}, u32[]{:S(2)}) copy-start(bf16[768,1536]{1,0:T(8,128)(2,1)S(1)} %add_convert_fusion.1.refs_4_.refs_0_) | copy-start | bytes 7077892
  232.7 4.5 copy-start.25
  232.7 85.7 %collective-permute-start.11 = (bf16[768,1536]{1,0:T(8,128)(2,1)S(1)}, bf16[768,1536]{1,0:T(8,128)(2,1)}, u32[]{:S(2)}, u32[]{:S(2)}) collective-permute-start(bf16[768,1536]{1,0:T(8,128)(2,1)S(1)} %add_convert_fusion.1.refs_4_.refs_0_), channel_id=1, source_target_pairs={{0,2},{1,3},{2,0},{3,1},{4,6},{5,7},{6,4},{7,5},{8,10},{9,11},{10,... | collective-permute-start | bytes 7077896 | tf_op jit(solution)/shard_map/ppermute | solution.py:419
  243.4 7.3 %collective-permute-start.34 = (bf16[88,1536]{1,0:T(8,128)(2,1)S(1)}, bf16[88,1536]{1,0:T(8,128)(2,1)S(1)}, u32[]{:S(2)}, u32[]{:S(2)}) collective-permute-start(bf16[88,1536]{1,0:T(8,128)(2,1)S(1)} %fusion.7), channel_id=1, source_target_pairs={{0,4},{4,0},{8,12},{12,8},{16,20},{20,16},{24,28},{28,24},{1,5},{5... | collective-permute-start | bytes 811016 | tf_op jit(solution)/shard_map/ppermute | solution.py:419
  244.0 23.2 %collective-permute-start.19 = (bf16[192,768]{1,0:T(8,128)(2,1)}, bf16[192,768]{1,0:T(8,128)(2,1)S(1)}, u32[]{:S(2)}, u32[]{:S(2)}) collective-permute-start(bf16[192,768]{1,0:T(8,128)(2,1)} %get-tuple-element.71.refs_1_), channel_id=1, source_target_pairs={{0,8},{4,12},{8,0},{12,4},{16,24},{20,28},{24,16},{28,20},{1,9},{5... | collective-permute-start | bytes 884744 | tf_op jit(solution)/shard_map/ppermute | solution.py:419
  250.7 9.2 %collective-permute-start.41 = (bf16[96,1536]{1,0:T(8,128)(2,1)}, bf16[96,1536]{1,0:T(8,128)(2,1)S(1)}, u32[]{:S(2)}, u32[]{:S(2)}) collective-permute-start(bf16[96,1536]{1,0:T(8,128)(2,1)} %add_rows.3.refs_2_), channel_id=1, source_target_pairs={{0,24},{4,28},{8,16},{12,20},{16,8},{20,12},{24,0},{28,4},{1,25},{... | collective-permute-start | bytes 884744 | tf_op jit(solution)/shard_map/ppermute | solution.py:419
  259.9 12.4 %collective-permute-start.35 = (bf16[88,1536]{1,0:T(8,128)(2,1)S(1)}, bf16[88,1536]{1,0:T(8,128)(2,1)S(1)}, u32[]{:S(2)}, u32[]{:S(2)}) collective-permute-start(bf16[88,1536]{1,0:T(8,128)(2,1)S(1)} %add_convert_fusion.7), channel_id=1, source_target_pairs={{0,8},{4,12},{8,0},{12,4},{16,24},{20,28},{24,16},{28,20},{1,9},{5... | collective-permute-start | bytes 811016 | tf_op jit(solution)/shard_map/ppermute | solution.py:419
  267.2 5.1 %copy-start.22 = (bf16[192,768]{1,0:T(8,128)(2,1)}, bf16[192,768]{1,0:T(8,128)(2,1)S(1)}, u32[]{:S(2)}) copy-start(bf16[192,768]{1,0:T(8,128)(2,1)S(1)} %collective-permute-done.19.refs_1_) | copy-start | bytes 884740
  267.2 55.9 %collective-permute-start.42 = (bf16[384,1536]{1,0:T(8,128)(2,1)}, bf16[384,1536]{1,0:T(8,128)(2,1)}, u32[]{:S(2)}, u32[]{:S(2)}) collective-permute-start(bf16[384,1536]{1,0:T(8,128)(2,1)} %pad_maximum_fusion.2.mine), channel_id=1, source_target_pairs={{0,4},{4,0},{8,12},{12,8},{16,20},{20,16},{24,28},{28,24},{1,5},{5... | collective-permute-start | bytes 3538952 | tf_op jit(solution)/shard_map/ppermute | solution.py:419
  267.7 22.9 %collective-permute-start.20 = (bf16[192,768]{1,0:T(8,128)(2,1)}, bf16[192,768]{1,0:T(8,128)(2,1)S(1)}, u32[]{:S(2)}, u32[]{:S(2)}) collective-permute-start(bf16[192,768]{1,0:T(8,128)(2,1)} %get-tuple-element.82), channel_id=1, source_target_pairs={{0,16},{4,20},{8,24},{12,28},{16,0},{20,4},{24,8},{28,12},{1,17},{... | collective-permute-start | bytes 884744 | tf_op jit(solution)/shard_map/ppermute | solution.py:419
  272.3 18.3 %collective-permute-start.21 = (bf16[192,768]{1,0:T(8,128)(2,1)}, bf16[192,768]{1,0:T(8,128)(2,1)S(1)}, u32[]{:S(2)}, u32[]{:S(2)}) collective-permute-start(bf16[192,768]{1,0:T(8,128)(2,1)} %get-tuple-element.83), channel_id=1, source_target_pairs={{0,24},{4,28},{8,16},{12,20},{16,8},{20,12},{24,0},{28,4},{1,25},{... | collective-permute-start | bytes 884744 | tf_op jit(solution)/shard_map/ppermute | solution.py:419
  274.0 16.6 %copy-start.14 = (bf16[88,1536]{1,0:T(8,128)(2,1)}, bf16[88,1536]{1,0:T(8,128)(2,1)S(1)}, u32[]{:S(2)}) copy-start(bf16[88,1536]{1,0:T(8,128)(2,1)S(1)} %add_convert_fusion.6) | copy-start | bytes 811012
  290.6 27.8 %copy-start.23 = (bf16[192,768]{1,0:T(8,128)(2,1)}, bf16[192,768]{1,0:T(8,128)(2,1)S(1)}, u32[]{:S(2)}) copy-start(bf16[192,768]{1,0:T(8,128)(2,1)S(1)} %collective-permute-done.20.refs_2_) | copy-start | bytes 884740
  290.6 35.4 %collective-permute-start.36 = (bf16[88,1536]{1,0:T(8,128)(2,1)S(1)}, bf16[88,1536]{1,0:T(8,128)(2,1)}, u32[]{:S(2)}, u32[]{:S(2)}) collective-permute-start(bf16[88,1536]{1,0:T(8,128)(2,1)S(1)} %add_convert_fusion.6), channel_id=1, source_target_pairs={{0,16},{4,20},{8,24},{12,28},{16,0},{20,4},{24,8},{28,12},{1,17},{... | collective-permute-start | bytes 811016 | tf_op jit(solution)/shard_map/ppermute | solution.py:419
  291.4 37.1 %collective-permute-start.27 = (bf16[192,768]{1,0:T(8,128)(2,1)}, bf16[192,768]{1,0:T(8,128)(2,1)S(1)}, u32[]{:S(2)}, u32[]{:S(2)}) collective-permute-start(bf16[192,768]{1,0:T(8,128)(2,1)} %get-tuple-element.85), channel_id=1, source_target_pairs={{0,8},{4,12},{8,0},{12,4},{16,24},{20,28},{24,16},{28,20},{1,9},{5... | collective-permute-start | bytes 884744 | tf_op jit(solution)/shard_map/ppermute | solution.py:419
  318.4 17.4 %collective-permute-start.28 = (bf16[192,768]{1,0:T(8,128)(2,1)}, bf16[192,768]{1,0:T(8,128)(2,1)}, u32[]{:S(2)}, u32[]{:S(2)}) collective-permute-start(bf16[192,768]{1,0:T(8,128)(2,1)} %get-tuple-element.86), channel_id=1, source_target_pairs={{0,16},{4,20},{8,24},{12,28},{16,0},{20,4},{24,8},{28,12},{1,17},{... | collective-permute-start | bytes 884744 | tf_op jit(solution)/shard_map/ppermute | solution.py:419
  323.1 19.1 %copy-start.1 = (bf16[768,1536]{1,0:T(8,128)(2,1)}, bf16[768,1536]{1,0:T(8,128)(2,1)S(1)}, u32[]{:S(2)}) copy-start(bf16[768,1536]{1,0:T(8,128)(2,1)S(1)} %add_convert_fusion.own) | copy-start | bytes 7077892
  323.1 89.2 %collective-permute-start.12 = (bf16[768,1536]{1,0:T(8,128)(2,1)S(1)}, bf16[768,1536]{1,0:T(8,128)(2,1)}, u32[]{:S(2)}, u32[]{:S(2)}) collective-permute-start(bf16[768,1536]{1,0:T(8,128)(2,1)S(1)} %add_convert_fusion.own), channel_id=1, source_target_pairs={{0,1},{1,0},{2,3},{3,2},{4,5},{5,4},{6,7},{7,6},{8,9},{9,8},{10,11... | collective-permute-start | bytes 7077896 | tf_op jit(solution)/shard_map/ppermute | solution.py:419
  326.1 36.1 %collective-permute-start.22 = (bf16[192,768]{1,0:T(8,128)(2,1)}, bf16[192,768]{1,0:T(8,128)(2,1)S(1)}, u32[]{:S(2)}, u32[]{:S(2)}) collective-permute-start(bf16[192,768]{1,0:T(8,128)(2,1)} %add_rows.4), channel_id=1, source_target_pairs={{0,8},{4,12},{8,0},{12,4},{16,24},{20,28},{24,16},{28,20},{1,9},{5... | collective-permute-start | bytes 884744 | tf_op jit(solution)/shard_map/ppermute | solution.py:419
  328.5 51.5 %collective-permute-start.23 = (bf16[192,768]{1,0:T(8,128)(2,1)}, bf16[192,768]{1,0:T(8,128)(2,1)}, u32[]{:S(2)}, u32[]{:S(2)}) collective-permute-start(bf16[192,768]{1,0:T(8,128)(2,1)} %add_rows.4), channel_id=1, source_target_pairs={{0,16},{4,20},{8,24},{12,28},{16,0},{20,4},{24,8},{28,12},{1,17},{... | collective-permute-start | bytes 884744 | tf_op jit(solution)/shard_map/ppermute | solution.py:419
  328.6 13.7 %copy-start.20 = (bf16[192,768]{1,0:T(8,128)(2,1)}, bf16[192,768]{1,0:T(8,128)(2,1)S(1)}, u32[]{:S(2)}) copy-start(bf16[192,768]{1,0:T(8,128)(2,1)S(1)} %collective-permute-done.27.refs_1_) | copy-start | bytes 884740
  328.6 52.7 %collective-permute-start.24 = (bf16[192,768]{1,0:T(8,128)(2,1)}, bf16[192,768]{1,0:T(8,128)(2,1)}, u32[]{:S(2)}, u32[]{:S(2)}) collective-permute-start(bf16[192,768]{1,0:T(8,128)(2,1)} %add_rows.4), channel_id=1, source_target_pairs={{0,24},{4,28},{8,16},{12,20},{16,8},{20,12},{24,0},{28,4},{1,25},{... | collective-permute-start | bytes 884744 | tf_op jit(solution)/shard_map/ppermute | solution.py:419
  335.8 18.9 %collective-permute-start.29 = (bf16[192,768]{1,0:T(8,128)(2,1)}, bf16[192,768]{1,0:T(8,128)(2,1)S(1)}, u32[]{:S(2)}, u32[]{:S(2)}) collective-permute-start(bf16[192,768]{1,0:T(8,128)(2,1)} %get-tuple-element.87), channel_id=1, source_target_pairs={{0,24},{4,28},{8,16},{12,20},{16,8},{20,12},{24,0},{28,4},{1,25},{... | collective-permute-start | bytes 884744 | tf_op jit(solution)/shard_map/ppermute | solution.py:419
  355.4 120.4 %collective-permute-start.4 = (bf16[768,1536]{1,0:T(8,128)(2,1)}, bf16[768,1536]{1,0:T(8,128)(2,1)}, u32[]{:S(2)}, u32[]{:S(2)}) collective-permute-start(bf16[768,1536]{1,0:T(8,128)(2,1)} %add_convert_fusion.2.own), channel_id=1, source_target_pairs={{0,1},{1,0},{2,3},{3,2},{4,5},{5,4},{6,7},{7,6},{8,9},{9,8},{10,11... | collective-permute-start | bytes 7077896 | tf_op jit(solution)/shard_map/ppermute | solution.py:419
  360.0 26.3 %copy-start.13 = (bf16[192,768]{1,0:T(8,128)(2,1)S(1)}, bf16[192,768]{1,0:T(8,128)(2,1)}, u32[]{:S(2)}) copy-start(bf16[192,768]{1,0:T(8,128)(2,1)} %add_rows.4) | copy-start | bytes 884740
  362.2 42.1 %copy-start.12 = (bf16[192,768]{1,0:T(8,128)(2,1)S(1)}, bf16[192,768]{1,0:T(8,128)(2,1)}, u32[]{:S(2)}) copy-start(bf16[192,768]{1,0:T(8,128)(2,1)} %add_rows.5) | copy-start | bytes 884740
  362.2 19.1 %copy-start.19 = (bf16[192,768]{1,0:T(8,128)(2,1)}, bf16[192,768]{1,0:T(8,128)(2,1)S(1)}, u32[]{:S(2)}) copy-start(bf16[192,768]{1,0:T(8,128)(2,1)S(1)} %collective-permute-done.22) | copy-start | bytes 884740
  362.2 31.8 %collective-permute-start.30 = (bf16[192,768]{1,0:T(8,128)(2,1)}, bf16[192,768]{1,0:T(8,128)(2,1)}, u32[]{:S(2)}, u32[]{:S(2)}) collective-permute-start(bf16[192,768]{1,0:T(8,128)(2,1)} %add_rows.5), channel_id=1, source_target_pairs={{0,8},{4,12},{8,0},{12,4},{16,24},{20,28},{24,16},{28,20},{1,9},{5... | collective-permute-start | bytes 884744 | tf_op jit(solution)/shard_map/ppermute | solution.py:419
  380.0 23.8 %collective-permute-start.31 = (bf16[192,768]{1,0:T(8,128)(2,1)}, bf16[192,768]{1,0:T(8,128)(2,1)}, u32[]{:S(2)}, u32[]{:S(2)}) collective-permute-start(bf16[192,768]{1,0:T(8,128)(2,1)} %add_rows.5), channel_id=1, source_target_pairs={{0,16},{4,20},{8,24},{12,28},{16,0},{20,4},{24,8},{28,12},{1,17},{... | collective-permute-start | bytes 884744 | tf_op jit(solution)/shard_map/ppermute | solution.py:419
  381.3 23.0 %collective-permute-start.32 = (bf16[192,768]{1,0:T(8,128)(2,1)}, bf16[192,768]{1,0:T(8,128)(2,1)}, u32[]{:S(2)}, u32[]{:S(2)}) collective-permute-start(bf16[192,768]{1,0:T(8,128)(2,1)} %add_rows.5), channel_id=1, source_target_pairs={{0,24},{4,28},{8,16},{12,20},{16,8},{20,12},{24,0},{28,4},{1,25},{... | collective-permute-start | bytes 884744 | tf_op jit(solution)/shard_map/ppermute | solution.py:419
  388.5 21.0 %copy-start.16 = (bf16[384,256]{1,0:T(8,128)(2,1)S(1)}, bf16[384,256]{1,0:T(8,128)(2,1)}, u32[]{:S(2)}) copy-start(bf16[384,256]{1,0:T(8,128)(2,1)} %convert_element_type.146) | copy-start | bytes 589828
  394.0 15.6 %collective-permute-start.37 = (bf16[384,256]{1,0:T(8,128)(2,1)}, bf16[384,256]{1,0:T(8,128)(2,1)}, u32[]{:S(2)}, u32[]{:S(2)}) collective-permute-start(bf16[384,256]{1,0:T(8,128)(2,1)} %convert_element_type.146), channel_id=1, source_target_pairs={{0,1},{1,0},{2,3},{3,2},{4,5},{5,4},{6,7},{7,6},{8,9},{9,8},{10,11... | collective-permute-start | bytes 589832 | tf_op jit(solution)/shard_map/ppermute | solution.py:419
  403.8 62.6 %collective-permute-start.25 = (bf16[768,768]{1,0:T(8,128)(2,1)}, bf16[768,768]{1,0:T(8,128)(2,1)}, u32[]{:S(2)}, u32[]{:S(2)}) collective-permute-start(bf16[768,768]{1,0:T(8,128)(2,1)} %pad_maximum_fusion.mine), channel_id=1, source_target_pairs={{0,4},{4,0},{8,12},{12,8},{16,20},{20,16},{24,28},{28,24},{1,5},{5... | collective-permute-start | bytes 3538952 | tf_op jit(solution)/shard_map/ppermute | solution.py:419
  406.5 64.6 %collective-permute-start.33 = (bf16[768,768]{1,0:T(8,128)(2,1)}, bf16[768,768]{1,0:T(8,128)(2,1)}, u32[]{:S(2)}, u32[]{:S(2)}) collective-permute-start(bf16[768,768]{1,0:T(8,128)(2,1)} %pad_maximum_fusion.1.mine), channel_id=1, source_target_pairs={{0,4},{4,0},{8,12},{12,8},{16,20},{20,16},{24,28},{28,24},{1,5},{5... | collective-permute-start | bytes 3538952 | tf_op jit(solution)/shard_map/ppermute | solution.py:419
  410.7 53.3 %collective-permute-start.38 = (bf16[768,256]{1,0:T(8,128)(2,1)S(1)}, bf16[768,256]{1,0:T(8,128)(2,1)}, u32[]{:S(2)}, u32[]{:S(2)}) collective-permute-start(bf16[768,256]{1,0:T(8,128)(2,1)S(1)} %maximum_select_fusion.1), channel_id=1, source_target_pairs={{0,2},{1,3},{2,0},{3,1},{4,6},{5,7},{6,4},{7,5},{8,10},{9,11},{10,... | collective-permute-start | bytes 1179656 | tf_op jit(solution)/shard_map/ppermute | solution.py:419
  425.5 23.4 %collective-permute-start.16 = (f32[8,1536]{1,0:T(8,128)}, f32[8,1536]{1,0:T(8,128)S(1)}, u32[]{:S(2)}, u32[]{:S(2)}) collective-permute-start(f32[8,1536]{1,0:T(8,128)} %get-tuple-element.80), channel_id=1, source_target_pairs={{0,4},{4,0},{8,12},{12,8},{16,20},{20,16},{24,28},{28,24},{1,5},{5... | collective-permute-start | bytes 147464 | tf_op jit(solution)/shard_map/ppermute | solution.py:419
  449.7 10.7 %collective-permute-start.17 = (f32[8,1536]{1,0:T(8,128)S(1)}, f32[8,1536]{1,0:T(8,128)S(1)}, u32[]{:S(2)}, u32[]{:S(2)}) collective-permute-start(f32[8,1536]{1,0:T(8,128)S(1)} %add.89), channel_id=1, source_target_pairs={{0,8},{4,12},{8,0},{12,4},{16,24},{20,28},{24,16},{28,20},{1,9},{5... | collective-permute-start | bytes 147464 | tf_op jit(solution)/shard_map/ppermute | solution.py:419
  460.4 20.1 %collective-permute-start.18 = (f32[8,1536]{1,0:T(8,128)S(1)}, f32[8,1536]{1,0:T(8,128)S(1)}, u32[]{:S(2)}, u32[]{:S(2)}) collective-permute-start(f32[8,1536]{1,0:T(8,128)S(1)} %add.90), channel_id=1, source_target_pairs={{0,16},{4,20},{8,24},{12,28},{16,0},{20,4},{24,8},{28,12},{1,17},{... | collective-permute-start | bytes 147464 | tf_op jit(solution)/shard_map/ppermute | solution.py:419
  (9 other events, 24.1 us)

commit v3 on v2

--- a/solution.py
+++ b/solution.py
@@ -11,6 +11,7 @@
 GROUP = 256
 LANES = 128
 EPS = 1e-05
+DP, TENSOR = "dp", "tensor"
 LOG2E = 1.4426950408889634
 F32 = jnp.float32
 BF16 = jnp.bfloat16
@@ -490,7 +491,7 @@
         place = jnp.concatenate([near[None], order]).astype(jnp.int32)
         return pl.pallas_call(
             partial(spread_kernel, count),
-            name="spread_rows",
+            name="sr",
             cost_estimate=small_cost(3),
             out_shape=outs,
             grid_spec=pltpu.PrefetchScalarGridSpec(
@@ -506,7 +507,7 @@
     place = jnp.concatenate([near * count + order, order]).astype(jnp.int32)
     return pl.pallas_call(
         partial(spread_blocks_kernel, count),
-        name="spread_rows",
+        name="sr",
         cost_estimate=small_cost(3),
         out_shape=outs,
         grid_spec=pltpu.PrefetchScalarGridSpec(
@@ -534,7 +535,7 @@
     spec = pl.BlockSpec(parts[0].shape, lambda: (0, 0))
     return pl.pallas_call(
         partial(add_kernel, count),
-        name="add_rows",
+        name="ar",
         cost_estimate=small_cost(2),
         out_shape=jax.ShapeDtypeStruct(parts[0].shape, BF16),
         in_specs=[spec] * count + [pl.BlockSpec(memory_space=pl.ANY)] * len(after),
@@ -555,7 +556,7 @@
         half = pl.BlockSpec((rows * count, cols), lambda i, pr: (0, 0))
         return pl.pallas_call(
             partial(join_kernel, count),
-            name="join_rows",
+            name="jr",
             cost_estimate=small_cost(4),
             out_shape=jax.ShapeDtypeStruct((rows * size, cols), F32),
             grid_spec=pltpu.PrefetchScalarGridSpec(
@@ -570,7 +571,7 @@
     place = jnp.concatenate([near * count + order, (1 - near) * count + order])
     return pl.pallas_call(
         partial(join_blocks_kernel, count),
-        name="join_rows",
+        name="jr",
         cost_estimate=small_cost(4),
         out_shape=jax.ShapeDtypeStruct((rows * size, cols), F32),
         grid_spec=pltpu.PrefetchScalarGridSpec(
@@ -639,7 +640,7 @@
     half = pl.BlockSpec((rows, cols), lambda i, pr: (0, 0))
     return pl.pallas_call(
         paste_kernel,
-        name="paste_halves",
+        name="ph",
         cost_estimate=small_cost(4),
         out_shape=jax.ShapeDtypeStruct((rows * 2, cols), own.dtype),
         grid_spec=pltpu.PrefetchScalarGridSpec(
@@ -664,7 +665,7 @@
     state = state_weight.shape[1] // 2
     group = GROUP
     blocks = tokens // group
-    me_t = lax.axis_index("tensor")
+    me_t = lax.axis_index(TENSOR)
     side = (me_t & 1).astype(jnp.int32).reshape(1)
 
     seg_row = segment_ids.astype(F32).reshape(blocks, 1, group)
@@ -689,12 +690,12 @@
         flops=0, transcendentals=0, bytes_accessed=int(us * 3.3e6)
     )
     params = pltpu.CompilerParams(
-        dimension_semantics=("arbitrary",), vmem_limit_bytes=60 * 1024 * 1024
+        vmem_limit_bytes=60 * 1024 * 1024
     )
 
     (normed, gate_pre, u, z, state_z, state_u, states, step_pre, y, s_in, d_gn, sums) = pl.pallas_call(
         partial(forward_kernel, (group, channels, heads, width, state)),
-        name="forward_scan",
+        name="fs",
         cost_estimate=cost(40),
         out_shape=(
             sds((tokens, model), BF16),
@@ -745,10 +746,10 @@
         row2(state_conv_bias), head_row, row2(gate_norm_gain), out_weight,
     )
 
-    sums = sum_doubling(sums, "tensor", tensor)
+    sums = sum_doubling(sums, TENSOR, tensor)
     gnormed, d_y, d_gate, grad_gnorm = pl.pallas_call(
         partial(gate_kernel, (group, channels, float(channels * tensor))),
-        name="gating",
+        name="gt",
         cost_estimate=cost(10),
         out_shape=(
             sds((tokens, channels), BF16), sds((tokens, channels), BF16),
@@ -765,11 +766,11 @@
         compiler_params=params,
     )(sums, seg_row, y, gate_pre, d_gn, row2(gate_norm_gain))
 
-    g_out = start_reduce(mm(gnormed, cotangent, TN).astype(BF16), "dp", dp)
+    g_out = start_reduce(mm(gnormed, cotangent, TN).astype(BF16), DP, dp)
     mix = mm(gnormed, out_weight).astype(BF16)
-    mix = start_half(mix, "tensor", tensor)
+    mix = start_half(mix, TENSOR, tensor)
     g_gate = mm(normed, d_gate, TN).astype(BF16)
-    g_gate = start_reduce(g_gate, "dp", dp)
+    g_gate = start_reduce(g_gate, DP, dp)
 
     part = channels
 
@@ -780,7 +781,7 @@
                 backward_kernel,
                 (group, part, k * (heads // 2), width, state, blocks, len(waits)),
             ),
-            name="backward_scan",
+            name="bs",
             cost_estimate=cost(42),
             out_shape=(
                 sds((tokens, part), BF16), sds((tokens, LANES), BF16),
@@ -819,21 +820,21 @@
             *waits,
         )
 
-    mix = near_half(mix, "tensor", tensor)
-    g_out = near_reduce(g_out, "dp", dp, [mix[1], g_gate[1]])
+    mix = near_half(mix, TENSOR, tensor)
+    g_out = near_reduce(g_out, DP, dp, [mix[1], g_gate[1]])
     d_input, d_step, d_states, grad_conv, grad_cb, grad_head = backward(
         0, [g_out[1]]
     )
 
     states_half = far_half(
-        near_half(start_half(d_states, "tensor", tensor), "tensor", tensor), "tensor", tensor,
+        near_half(start_half(d_states, TENSOR, tensor), TENSOR, tensor), TENSOR, tensor,
     ).astype(BF16)
-    g_in = start_reduce(mm(normed, d_input, TN).astype(BF16), "dp", dp)
-    g_out = far_reduce(g_out, "dp", dp, [d_step])
-    g_gate = near_reduce(g_gate, "dp", dp, [d_step])
+    g_in = start_reduce(mm(normed, d_input, TN).astype(BF16), DP, dp)
+    g_out = far_reduce(g_out, DP, dp, [d_step])
+    g_gate = near_reduce(g_gate, DP, dp, [d_step])
     local_back = pl.pallas_call(
         project_kernel,
-        name="project_back",
+        name="pb",
         cost_estimate=cost(10),
         out_shape=sds((tokens, model), BF16),
         grid_spec=pl.GridSpec(
@@ -849,18 +850,18 @@
         d_gate, d_input, d_step, gate_weight, input_weight, step_w,
         g_in[1], g_gate[1], g_out,
     )
-    back_half = near_half(start_half(local_back, "tensor", tensor), "tensor", tensor)
-    mix_half = far_half(mix, "tensor", tensor)
-    d_states = share_half(states_half, "tensor", tensor)
+    back_half = near_half(start_half(local_back, TENSOR, tensor), TENSOR, tensor)
+    mix_half = far_half(mix, TENSOR, tensor)
+    d_states = share_half(states_half, TENSOR, tensor)
     low = back_half[1]
-    g_gate = far_reduce(g_gate, "dp", dp, [low])
-    g_in = near_reduce(g_in, "dp", dp, [low])
-    g_in = far_reduce(g_in, "dp", dp)
-    back_half = far_half(back_half, "tensor", tensor).astype(BF16)
+    g_gate = far_reduce(g_gate, DP, dp, [low])
+    g_in = near_reduce(g_in, DP, dp, [low])
+    g_in = far_reduce(g_in, DP, dp)
+    back_half = far_half(back_half, TENSOR, tensor).astype(BF16)
 
     state_b, grad_sconv, grad_scb = pl.pallas_call(
         partial(state_kernel, (group, 2 * state, blocks)),
-        name="state_conv",
+        name="sc",
         cost_estimate=cost(6),
         out_shape=(
             sds((tokens, 2 * state), BF16), sds((8, 2 * state), F32), sds((8, 2 * state), F32),
@@ -890,15 +891,15 @@
     rows = tokens // 2
     hid_half = lax.dynamic_slice_in_dim(hidden, (me_t & 1) * rows, rows, 0)
     out_half = (hid_half.astype(F32) + mix_half).astype(BF16)
-    block_out = paste_halves(*share_half(out_half, "tensor", tensor), me_t)
-    back = share_half(back_half, "tensor", tensor)
+    block_out = paste_halves(*share_half(out_half, TENSOR, tensor), me_t)
+    back = share_half(back_half, TENSOR, tensor)
 
     own_first = lambda cols: pl.BlockSpec(
         (group, cols), lambda i, pr: (lax.rem(i + pr[0] * (blocks // 2), blocks), 0)
     )
     grad_hidden, grad_norm = pl.pallas_call(
         partial(final_kernel, blocks // 2),
-        name="final_grad",
+        name="fg",
         cost_estimate=cost(12),
         out_shape=(sds((tokens, model), F32), sds((8, model), F32)),
         grid_spec=pltpu.PrefetchScalarGridSpec(
@@ -915,9 +916,9 @@
         compiler_params=params,
     )(side, *back, state_b, state_weight, hidden, cotangent, row2(norm_gain))
 
-    grad_out = gather_rows(g_out, "dp", dp)
-    grad_gate = gather_rows(g_gate, "dp", dp)
-    grad_input = gather_rows(g_in, "dp", dp)
+    grad_out = gather_rows(g_out, DP, dp)
+    grad_gate = gather_rows(g_gate, DP, dp)
+    grad_input = gather_rows(g_in, DP, dp)
 
     def line(*parts):
         flat = jnp.concatenate([v.reshape(1, -1) for v in parts], axis=1)
@@ -938,17 +939,15 @@
     fill = -small.shape[0] % 8
     small = jnp.pad(small, ((0, fill), (0, 0)))
     lines = small.shape[0]
-    small = sum_doubling(
-        jnp.concatenate([small, g_state.reshape(-1, model)], axis=0), "dp", dp, BF16
-    )
+    small = sum_doubling(jnp.concatenate([small, g_state.reshape(-1, model)], axis=0), DP, dp, BF16)
     g_state = small[lines:].reshape(rows_t, 2 * state).astype(BF16)
-    grad_norm = sum_doubling(grad_norm, "dp", dp)[0]
+    grad_norm = sum_doubling(grad_norm, DP, dp)[0]
     pieces = [g_state]
     for b in range(bits_of(tensor)):
         low = (me_t >> b) & 1
         pieces = [
             jnp.where(low == 0, jnp.concatenate([v, w]), jnp.concatenate([w, v]))
-            for v, w in ((v, partner(v, "tensor", tensor, 1 << b)) for v in pieces)
+            for v, w in ((v, partner(v, TENSOR, tensor, 1 << b)) for v in pieces)
         ]
     grad_state = pieces[0].astype(F32)
 
@@ -986,17 +985,17 @@
 
 def solution(mesh):
     return jax.shard_map(
-        partial(body, mesh.shape["dp"], mesh.shape["tensor"]),
+        partial(body, mesh.shape[DP], mesh.shape[TENSOR]),
         mesh=mesh,
         in_specs=(
-            P("dp", None), P("dp"), P(), P(None, "tensor"), P(None, "tensor"),
-            P(None, "tensor"), P(), P(None, "tensor"), P(), P("tensor"), P(), P("tensor"),
-            P("tensor"), P("tensor"), P("tensor"), P("tensor", None), P("dp", None),
+            P(DP, None), P(DP), P(), P(None, TENSOR), P(None, TENSOR),
+            P(None, TENSOR), P(), P(None, TENSOR), P(), P(TENSOR), P(), P(TENSOR),
+            P(TENSOR), P(TENSOR), P(TENSOR), P(TENSOR, None), P(DP, None),
         ),
         out_specs=(
-            P("dp", None), P("dp", None), P(), P(None, "tensor"), P(None, "tensor"),
-            P(None, "tensor"), P(), P(None, "tensor"), P(), P("tensor"), P(), P("tensor"),
-            P("tensor"), P("tensor"), P("tensor"), P("tensor", None),
+            P(DP, None), P(DP, None), P(), P(None, TENSOR), P(None, TENSOR),
+            P(None, TENSOR), P(), P(None, TENSOR), P(), P(TENSOR), P(), P(TENSOR),
+            P(TENSOR), P(TENSOR), P(TENSOR), P(TENSOR, None),
         ),
         check_vma=False,
     )

time: 489 us -> 489 us (level)
  no operation moved by 1% of the time
where the time goes in v3:
time: 489 us; the launch traced here: 481 us
  Pallas kernels  160 us (33%)
  waiting for transfers between devices  130 us (27%)
  starting transfers between devices  87 us (18%)
  local copies, waits for them, and re-layouts  35.9 us (7%)
  other arithmetic  34.8 us (7%)
  matrix products  32.4 us (7%)
    ppermute x43, waiting for transfers between devices, partner(): return lax.ppermute(x, axis, [(i, i ^ mask) for i in range(size)])  130 us
    ppermute x43, starting transfers between devices, partner(): return lax.ppermute(x, axis, [(i, i ^ mask) for i in range(size)])  87 us
    pallas_call x1, Pallas kernels, backward(): pl.pallas_call(partial(backward_kernel, (group, part, k * (heads // 2), w...  41.2 us
    pallas_call x1, Pallas kernels, body(): pl.pallas_call(partial(forward_kernel, (group, channels, heads, width, st...  38.2 us
    dot_general x6, matrix products, mm(): return lax.dot_general(left, right, dims, preferred_element_type=F32)  32.4 us
    pallas_call x3, Pallas kernels, gather_rows(): pl.pallas_call(partial(join_kernel, count), name='jr', cost_estimate=smal...  14 us
    pallas_call x1, Pallas kernels, body(): pl.pallas_call(project_kernel, name='pb', cost_estimate=cost(10), out_sha...  13.7 us
    pallas_call x1, Pallas kernels, body(): pl.pallas_call(partial(final_kernel, blocks // 2), name='fg', cost_estima...  13.2 us
  transfers between devices with their start and end apart: 43, of which 15 were waited for; matrix products, arithmetic and copies ran while one was open for 16% of the time, Pallas kernels for 20%

profile of v3, /device:TPU:0, one launch (start us, length us, event | category | flops | bytes accessed | tf_op | source)
XLA Modules:
  0.0 481.3 jit_solution(5346174646616720695)
XLA Ops:
  9.6 38.2 %fs.1 = (bf16[1536,1536]{1,0:T(8,128)(2,1)}, f32[1536,768]{1,0:T(8,128)}, bf16[1536,768]{1,0:T(8,128)(2,1)}, f32[1536,768]{1,0:T(8,128)}, f32[1536,256]{1,0:T(8,...) custom-call(s32[1536]{0:T(1024)} %refs_0_.1, ...), custom_call_target="tpu_custom_call" | custom-call | bytes 132000000 | tf_op jit(solution)/shard_map/fs/pallas_call | solution.py:696
  50.2 2.8 collective-permute-start.1
  53.0 1.7 collective-permute-done.1
  55.2 10.8 %gt.1 = (bf16[1536,768]{1,0:T(8,128)(2,1)}, bf16[1536,768]{1,0:T(8,128)(2,1)}, bf16[1536,768]{1,0:T(8,128)(2,1)}, f32[8,768]{1,0:T(8,128)}) custom-call(f32[6,2,256]{2,1,0:T(2,128)} %add.78.sums, f32[6,1,256]{2,1,0:T(1,128)} %reshape.88.seg_row.refs_1_, f32[1536,768]{1,0:T(8,128)} %get-tuple-element.56.y_i.refs_3_, f32[1536,768]{1,0:T(8,128)} %get-tuple-element.57.gate_i, ...), custom_call_target="tpu_custom_call" | custom-call | bytes 33000000 | tf_op jit(solution)/shard_map/gt/pallas_call | solution.py:750
  66.0 6.2 %convolution_convert_fusion = bf16[1536,1536]{1,0:T(8,128)(2,1)S(1)} fusion(bf16[1536,768]{1,0:T(8,128)(2,1)} %get-tuple-element.59, bf16[768,1536]{1,0:T(8,128)(2,1)S(1)} %copy-done.9), kind=kOutput, calls=%fused_computation | convolution fusion | flops 3626237952 | bytes 9437184 | tf_op jit(solution)/shard_map/dot_general | solution.py:25
  72.2 1.7 constant_dynamic-slice_fusion.5
  75.7 7.1 %convolution_convert_fusion.3.keep = bf16[768,1536]{1,0:T(8,128)(2,1)S(1)} fusion(bf16[1536,768]{1,0:T(8,128)(2,1)} %get-tuple-element.59, bf16[1536,1536]{1,0:T(8,128)(2,1)} %cot.3), kind=kOutput, calls=%fused_computation.7 | convolution fusion | flops 3625058304 | bytes 9437184 | tf_op jit(solution)/shard_map/dot_general | solution.py:25
  82.9 2.1 collective-permute-start.5
  85.0 6.3 %convolution_convert_fusion.2.keep = bf16[1536,768]{1,0:T(8,128)(2,1)S(1)} fusion(bf16[1536,1536]{1,0:T(8,128)(2,1)} %get-tuple-element.67, bf16[1536,768]{1,0:T(8,128)(2,1)S(1)} %copy-done.10), kind=kOutput, calls=%fused_computation.6 | convolution fusion | flops 3625058304 | bytes 9437184 | tf_op jit(solution)/shard_map/dot_general | solution.py:25
  93.8 3.7 add_convert_fusion.3.refs_0_
  97.5 14.5 %collective-permute-done.5.got = bf16[384,1536]{1,0:T(8,128)(2,1)} collective-permute-done((bf16[384,1536]{1,0:T(8,128)(2,1)S(1)}, bf16[384,1536]{1,0:T(8,128)(2,1)}, u32[]{:S(2)}, u32[]{:S(2)}) %collective-permute-start.5) | collective-permute-done | bytes 1179680 | tf_op jit(solution)/shard_map/ppermute | solution.py:420
  112.0 3.5 sr.3
  115.5 2.1 collective-permute-start.7
  117.5 2.6 collective-permute-start.8
  120.1 41.2 %bs.1 = (bf16[1536,768]{1,0:T(8,128)(2,1)}, bf16[1536,128]{1,0:T(8,128)(2,1)}, bf16[1536,256]{1,0:T(8,128)(2,1)}, f32[8,768]{1,0:T(8,128)}, f32[8,768]{1,0:T(8,128)}, /*index=5*/f32[8,128]{1,0:T(8,128)}) custom-call(s32[1536]{0:T(1024)} %refs_0_.1, f32[6,1,256]{2,1,0:T(1,128)} %reshape.88.seg_row.refs_1_, bf16[1536,768]{1,0:T(8,128)(2,1)} %get-tuple-element.61.refs_2_, ...), custom_call_target="tpu_custom_call" | custom-call | bytes 138600000 | tf_op jit(solution)/shard_map/bs/pallas_call | solution.py:779
  161.3 7.0 %convolution_convert_fusion.1.keep = bf16[1536,768]{1,0:T(8,128)(2,1)S(1)} fusion(bf16[1536,1536]{1,0:T(8,128)(2,1)} %get-tuple-element.67, bf16[1536,768]{1,0:T(8,128)(2,1)} %get-tuple-element.69.di), kind=kOutput, calls=%fused_computation.5 | convolution fusion | flops 3625058304 | bytes 9437184 | tf_op jit(solution)/shard_map/dot_general | solution.py:25
  168.4 3.6 sr.4
  173.2 2.1 ar.3.refs_2_
  175.3 13.7 %pb.1 = bf16[1536,1536]{1,0:T(8,128)(2,1)} custom-call(bf16[1536,768]{1,0:T(8,128)(2,1)} %get-tuple-element.60.dg, bf16[1536,768]{1,0:T(8,128)(2,1)} %get-tuple-element.69.di, bf16[1536,128]{1,0:T(8,128)(2,1)} %get-tuple-element.70.refs_0_.refs_4_.ds, bf16[1536,768]{1,0:T(8,128)(2,1)} %gate_w.3, bf16[1536,768]{1,0:T(8,128)(2,1)} %input_w.3, ...), custom_call_target="tpu_custom_call" | custom-call | bytes 33000000 | tf_op jit(solution)/shard_map/pb/pallas_call | solution.py:835
  189.0 3.3 constant_dynamic-slice_fusion.1
  192.9 4.7 collective-permute-done.13
  197.8 1.8 collective-permute-start.14
  200.8 8.1 %collective-permute-done.14 = bf16[768,256]{1,0:T(8,128)(2,1)S(1)} collective-permute-done((bf16[768,256]{1,0:T(8,128)(2,1)S(1)}, bf16[768,256]{1,0:T(8,128)(2,1)S(1)}, u32[]{:S(2)}, u32[]{:S(2)}) %collective-permute-start.14) | collective-permute-done | bytes 393248 | tf_op jit(solution)/shard_map/ppermute | solution.py:420
  209.2 3.3 fusion.14
  212.6 1.8 collective-permute-start.26
  219.4 3.5 collective-permute-start.40
  222.9 6.7 %sc.1 = (bf16[1536,256]{1,0:T(8,128)(2,1)}, f32[8,256]{1,0:T(8,128)}, f32[8,256]{1,0:T(8,128)}) custom-call(s32[1]{0:T(128)} %bitcast.place, f32[6,1,256]{2,1,0:T(1,128)} %reshape.88.seg_row.refs_1_, bf16[768,256]{1,0:T(8,128)(2,1)} %copy-done.11, bf16[768,256]{1,0:T(8,128)(2,1)} %copy-done.18, f32[1536,256]{1,0:T(8,128)} %get-tuple-element.76.z_i, ...), custom_call_target="tpu_custom_call" | custom-call | bytes 19800000 | tf_op jit(solution)/shard_map/sc/pallas_call | solution.py:862
  229.6 3.1 add_convert_fusion.1.refs_4_.refs_0_
  234.7 2.5 fusion.2
  237.8 1.8 reshape.96
  239.6 2.8 concatenate.50
  244.0 6.7 %collective-permute-done.34 = bf16[88,1536]{1,0:T(8,128)(2,1)S(1)} collective-permute-done((bf16[88,1536]{1,0:T(8,128)(2,1)S(1)}, bf16[88,1536]{1,0:T(8,128)(2,1)S(1)}, u32[]{:S(2)}, u32[]{:S(2)}) %collective-permute-start.34) | collective-permute-done | bytes 270368 | tf_op jit(solution)/shard_map/ppermute | solution.py:420
  252.5 7.3 %collective-permute-done.41 = bf16[96,1536]{1,0:T(8,128)(2,1)S(1)} collective-permute-done((bf16[96,1536]{1,0:T(8,128)(2,1)}, bf16[96,1536]{1,0:T(8,128)(2,1)S(1)}, u32[]{:S(2)}, u32[]{:S(2)}) %collective-permute-start.41) | collective-permute-done | bytes 294944 | tf_op jit(solution)/shard_map/ppermute | solution.py:420
  259.9 5.1 %collective-permute-start.35 = (bf16[88,1536]{1,0:T(8,128)(2,1)S(1)}, bf16[88,1536]{1,0:T(8,128)(2,1)S(1)}, u32[]{:S(2)}, u32[]{:S(2)}) collective-permute-start(bf16[88,1536]{1,0:T(8,128)(2,1)S(1)} %add_convert_fusion.7), channel_id=1, source_target_pairs={{0,8},{4,12},{8,0},{12,4},{16,24},{20,28},{24,16},{28,20},{1,9},{5... | collective-permute-start | bytes 811016 | tf_op jit(solution)/shard_map/ppermute | solution.py:420
  264.9 2.2 pad_maximum_fusion.2.mine
  268.3 4.0 collective-permute-done.35
  274.0 3.5 sr.5
  277.6 13.0 %collective-permute-done.20.refs_2_ = bf16[192,768]{1,0:T(8,128)(2,1)S(1)} collective-permute-done((bf16[192,768]{1,0:T(8,128)(2,1)}, bf16[192,768]{1,0:T(8,128)(2,1)S(1)}, u32[]{:S(2)}, u32[]{:S(2)}) %collective-permute-start.20) | collective-permute-done | bytes 294944 | tf_op jit(solution)/shard_map/ppermute | solution.py:420
  291.4 12.6 %collective-permute-start.27 = (bf16[192,768]{1,0:T(8,128)(2,1)}, bf16[192,768]{1,0:T(8,128)(2,1)S(1)}, u32[]{:S(2)}, u32[]{:S(2)}) collective-permute-start(bf16[192,768]{1,0:T(8,128)(2,1)} %get-tuple-element.85), channel_id=1, source_target_pairs={{0,8},{4,12},{8,0},{12,4},{16,24},{20,28},{24,16},{28,20},{1,9},{5... | collective-permute-start | bytes 884744 | tf_op jit(solution)/shard_map/ppermute | solution.py:420
  304.0 14.4 %collective-permute-done.11 = bf16[768,1536]{1,0:T(8,128)(2,1)} collective-permute-done((bf16[768,1536]{1,0:T(8,128)(2,1)S(1)}, bf16[768,1536]{1,0:T(8,128)(2,1)}, u32[]{:S(2)}, u32[]{:S(2)}) %collective-permute-start.11) | collective-permute-done | bytes 2359328 | tf_op jit(solution)/shard_map/ppermute | solution.py:420
  318.4 1.7 collective-permute-start.28
  320.1 3.0 add_convert_fusion.own
  323.2 2.9 ar.4
  326.1 2.5 collective-permute-start.22
  328.6 2.4 collective-permute-start.24
  331.0 4.8 collective-permute-done.28.refs_2_
  336.8 5.4 %add_convert_fusion.2.own = bf16[768,1536]{1,0:T(8,128)(2,1)} fusion(bf16[768,1536]{1,0:T(8,128)(2,1)} %collective-permute-done.3, bf16[768,1536]{1,0:T(8,128)(2,1)} %add_convert_fusion.3.refs_0_, bf16[1536,1536]{1,0:T(8,128)(2,1)} %hid.3, s32[]{:T(128)S(6)} %select_n.37), kind=kLoop, calls=%fused_computation.3 | loop fusion | flops 7077888 | bytes 9437188 | tf_op jit(solution)/shard_map/convert_element_type | solution.py:893
  342.2 12.4 %collective-permute-done.29.refs_3_ = bf16[192,768]{1,0:T(8,128)(2,1)S(1)} collective-permute-done((bf16[192,768]{1,0:T(8,128)(2,1)}, bf16[192,768]{1,0:T(8,128)(2,1)S(1)}, u32[]{:S(2)}, u32[]{:S(2)}) %collective-permute-start.29) | collective-permute-done | bytes 294944 | tf_op jit(solution)/shard_map/ppermute | solution.py:420
  355.4 4.7 jr.5
  360.0 2.1 ar.5
  362.2 17.9 %collective-permute-start.30 = (bf16[192,768]{1,0:T(8,128)(2,1)}, bf16[192,768]{1,0:T(8,128)(2,1)}, u32[]{:S(2)}, u32[]{:S(2)}) collective-permute-start(bf16[192,768]{1,0:T(8,128)(2,1)} %ar.5), channel_id=1, source_target_pairs={{0,8},{4,12},{8,0},{12,4},{16,24},{20,28},{24,16},{28,20},{1,9},{5... | collective-permute-start | bytes 884744 | tf_op jit(solution)/shard_map/ppermute | solution.py:420
  384.5 1.8 convert_element_type.146
  386.3 2.2 pad_maximum_fusion.mine
  388.5 5.4 %collective-permute-done.30 = bf16[192,768]{1,0:T(8,128)(2,1)} collective-permute-done((bf16[192,768]{1,0:T(8,128)(2,1)}, bf16[192,768]{1,0:T(8,128)(2,1)}, u32[]{:S(2)}, u32[]{:S(2)}) %collective-permute-start.30) | collective-permute-done | bytes 294944 | tf_op jit(solution)/shard_map/ppermute | solution.py:420
  394.0 9.8 %collective-permute-done.31 = bf16[192,768]{1,0:T(8,128)(2,1)} collective-permute-done((bf16[192,768]{1,0:T(8,128)(2,1)}, bf16[192,768]{1,0:T(8,128)(2,1)}, u32[]{:S(2)}, u32[]{:S(2)}) %collective-permute-start.31) | collective-permute-done | bytes 294944 | tf_op jit(solution)/shard_map/ppermute | solution.py:420
  404.3 2.2 pad_maximum_fusion.1.mine
  412.3 13.2 %fg.1 = (f32[1536,1536]{1,0:T(8,128)}, f32[8,1536]{1,0:T(8,128)}) custom-call(s32[1]{0:T(128)} %bitcast.place, bf16[768,1536]{1,0:T(8,128)(2,1)} %copy-done.1, bf16[768,1536]{1,0:T(8,128)(2,1)} %collective-permute-done.12.got, bf16[1536,256]{1,0:T(8,128)(2,1)} %get-tuple-element.78.sb_i, bf16[1536,256]{1,0:T(8,128)(2,1)} %sw.1, bf16[1536,1536]{1,0:T(8,128)(2,1)} %hid.3, ...), custom_call_target="tpu_custom_call" | custom-call | bytes 39600000 | tf_op jit(solution)/shard_map/fg/pallas_call | solution.py:900
  427.4 21.6 %collective-permute-done.16 = f32[8,1536]{1,0:T(8,128)S(1)} collective-permute-done((f32[8,1536]{1,0:T(8,128)}, f32[8,1536]{1,0:T(8,128)S(1)}, u32[]{:S(2)}, u32[]{:S(2)}) %collective-permute-start.16) | collective-permute-done | bytes 49184 | tf_op jit(solution)/shard_map/ppermute | solution.py:420
  449.7 7.6 %collective-permute-start.17 = (f32[8,1536]{1,0:T(8,128)S(1)}, f32[8,1536]{1,0:T(8,128)S(1)}, u32[]{:S(2)}, u32[]{:S(2)}) collective-permute-start(f32[8,1536]{1,0:T(8,128)S(1)} %add.89), channel_id=1, source_target_pairs={{0,8},{4,12},{8,0},{12,4},{16,24},{20,28},{24,16},{28,20},{1,9},{5... | collective-permute-start | bytes 147464 | tf_op jit(solution)/shard_map/ppermute | solution.py:420
  460.4 3.6 collective-permute-start.18
  464.0 2.4 fusion.5
  466.4 4.7 jr.3
  471.1 4.7 jr.4
  475.8 4.7 ph.1
  (168 shorter events, 53.3 us)
Async XLA Ops:
  47.8 1.6 collective-permute-start
  50.2 4.5 collective-permute-start.1
  55.2 10.8 %copy-start.9 = (bf16[768,1536]{1,0:T(8,128)(2,1)S(1)}, bf16[768,1536]{1,0:T(8,128)(2,1)}, u32[]{:S(2)}) copy-start(bf16[768,1536]{1,0:T(8,128)(2,1)} %out_w.1) | copy-start | bytes 7077892
  75.1 18.6 %collective-permute-start.2 = (bf16[768,1536]{1,0:T(8,128)(2,1)}, bf16[768,1536]{1,0:T(8,128)(2,1)}, u32[]{:S(2)}, u32[]{:S(2)}) collective-permute-start(bf16[768,1536]{1,0:T(8,128)(2,1)} %constant_dynamic-slice_fusion.5), channel_id=1, source_target_pairs={{0,1},{1,0},{2,3},{3,2},{4,5},{5,4},{6,7},{7,6},{8,9},{9,8},{10,11... | collective-permute-start | bytes 7077896 | tf_op jit(solution)/shard_map/ppermute | solution.py:420
  75.7 9.3 %copy-start.10 = (bf16[1536,768]{1,0:T(8,128)(2,1)S(1)}, bf16[1536,768]{1,0:T(8,128)(2,1)}, u32[]{:S(2)}) copy-start(bf16[1536,768]{1,0:T(8,128)(2,1)} %get-tuple-element.60.dg) | copy-start | bytes 7077892
  82.8 8.5 %copy-start.4 = (bf16[768,1536]{1,0:T(8,128)(2,1)}, bf16[768,1536]{1,0:T(8,128)(2,1)S(1)}, u32[]{:S(2)}) copy-start(bf16[768,1536]{1,0:T(8,128)(2,1)S(1)} %convolution_convert_fusion.3.keep) | copy-start | bytes 7077892
  82.8 10.9 %slice-start = ((s8[4718592]{0:T(1024)(128)(4,1)}), s8[4194304]{0:T(1024)(128)(4,1)S(1)}, s32[]{:S(2)}) async-start(s8[4718592]{0:T(1024)(128)(4,1)} %bitcast.42), calls=%async_computation | async-start | bytes 8388608
  82.9 29.0 %collective-permute-start.5 = (bf16[384,1536]{1,0:T(8,128)(2,1)S(1)}, bf16[384,1536]{1,0:T(8,128)(2,1)}, u32[]{:S(2)}, u32[]{:S(2)}) collective-permute-start(bf16[384,1536]{1,0:T(8,128)(2,1)S(1)} %constant_dynamic-slice_fusion.4), channel_id=1, source_target_pairs={{0,4},{4,0},{8,12},{12,8},{16,20},{20,16},{24,28},{28,24},{1,5},{5... | collective-permute-start | bytes 3538952 | tf_op jit(solution)/shard_map/ppermute | solution.py:420
  85.0 8.7 %slice-start.1 = ((s8[4718592]{0:T(1024)(128)(4,1)}), s8[524288]{0:T(1024)(128)(4,1)S(1)}, s32[]{:S(2)}) async-start(s8[4718592]{0:T(1024)(128)(4,1)} %bitcast.42), calls=%async_computation.1 | async-start | bytes 1048576
  92.8 4.7 copy-start.7
  92.8 75.6 %collective-permute-start.6 = (bf16[768,768]{1,0:T(8,128)(2,1)S(1)}, bf16[768,768]{1,0:T(8,128)(2,1)}, u32[]{:S(2)}, u32[]{:S(2)}) collective-permute-start(bf16[768,768]{1,0:T(8,128)(2,1)S(1)} %constant_dynamic-slice_fusion.3.refs_1_), channel_id=1, source_target_pairs={{0,4},{4,0},{8,12},{12,8},{16,20},{20,16},{24,28},{28,24},{1,5},{5... | collective-permute-start | bytes 3538952 | tf_op jit(solution)/shard_map/ppermute | solution.py:420
  115.5 57.7 %collective-permute-start.7 = (bf16[96,1536]{1,0:T(8,128)(2,1)}, bf16[96,1536]{1,0:T(8,128)(2,1)}, u32[]{:S(2)}, u32[]{:S(2)}) collective-permute-start(bf16[96,1536]{1,0:T(8,128)(2,1)} %get-tuple-element.68.refs_11_), channel_id=1, source_target_pairs={{0,8},{4,12},{8,0},{12,4},{16,24},{20,28},{24,16},{28,20},{1,9},{5... | collective-permute-start | bytes 884744 | tf_op jit(solution)/shard_map/ppermute | solution.py:420
  117.5 55.6 %collective-permute-start.8 = (bf16[96,1536]{1,0:T(8,128)(2,1)}, bf16[96,1536]{1,0:T(8,128)(2,1)}, u32[]{:S(2)}, u32[]{:S(2)}) collective-permute-start(bf16[96,1536]{1,0:T(8,128)(2,1)} %get-tuple-element.73), channel_id=1, source_target_pairs={{0,16},{4,20},{8,24},{12,28},{16,0},{20,4},{24,8},{28,12},{1,17},{... | collective-permute-start | bytes 884744 | tf_op jit(solution)/shard_map/ppermute | solution.py:420
  120.1 53.0 %collective-permute-start.9 = (bf16[96,1536]{1,0:T(8,128)(2,1)}, bf16[96,1536]{1,0:T(8,128)(2,1)}, u32[]{:S(2)}, u32[]{:S(2)}) collective-permute-start(bf16[96,1536]{1,0:T(8,128)(2,1)} %get-tuple-element.74), channel_id=1, source_target_pairs={{0,24},{4,28},{8,16},{12,20},{16,8},{20,12},{24,0},{28,4},{1,25},{... | collective-permute-start | bytes 884744 | tf_op jit(solution)/shard_map/ppermute | solution.py:420
  168.4 4.8 copy-start.3
  192.3 16.9 %copy-start.2 = (bf16[1536,128]{1,0:T(8,128)(2,1)S(1)}, bf16[1536,128]{1,0:T(8,128)(2,1)}, u32[]{:S(2)}) copy-start(bf16[1536,128]{1,0:T(8,128)(2,1)} %get-tuple-element.70.refs_0_.refs_4_.ds) | copy-start | bytes 1179652
  192.3 37.2 %collective-permute-start.10 = (bf16[768,1536]{1,0:T(8,128)(2,1)}, bf16[768,1536]{1,0:T(8,128)(2,1)}, u32[]{:S(2)}, u32[]{:S(2)}) collective-permute-start(bf16[768,1536]{1,0:T(8,128)(2,1)} %constant_dynamic-slice_fusion.1), channel_id=1, source_target_pairs={{0,1},{1,0},{2,3},{3,2},{4,5},{5,4},{6,7},{7,6},{8,9},{9,8},{10,11... | collective-permute-start | bytes 7077896 | tf_op jit(solution)/shard_map/ppermute | solution.py:420
  192.4 5.3 %collective-permute-start.13 = (bf16[768,256]{1,0:T(8,128)(2,1)S(1)}, bf16[768,256]{1,0:T(8,128)(2,1)S(1)}, u32[]{:S(2)}, u32[]{:S(2)}) collective-permute-start(bf16[768,256]{1,0:T(8,128)(2,1)S(1)} %constant_dynamic-slice_fusion), channel_id=1, source_target_pairs={{0,1},{1,0},{2,3},{3,2},{4,5},{5,4},{6,7},{7,6},{8,9},{9,8},{10,11... | collective-permute-start | bytes 1179656 | tf_op jit(solution)/shard_map/ppermute | solution.py:420
  197.8 11.2 %collective-permute-start.14 = (bf16[768,256]{1,0:T(8,128)(2,1)S(1)}, bf16[768,256]{1,0:T(8,128)(2,1)S(1)}, u32[]{:S(2)}, u32[]{:S(2)}) collective-permute-start(bf16[768,256]{1,0:T(8,128)(2,1)S(1)} %add_convert_fusion.5), channel_id=1, source_target_pairs={{0,2},{1,3},{2,0},{3,1},{4,6},{5,7},{6,4},{7,5},{8,10},{9,11},{10,... | collective-permute-start | bytes 1179656 | tf_op jit(solution)/shard_map/ppermute | solution.py:420
  209.1 9.5 %copy-start.27 = (f32[8,128]{1,0:T(8,128)S(1)}, f32[8,128]{1,0:T(8,128)}, u32[]{:S(2)}) copy-start(f32[8,128]{1,0:T(8,128)} %get-tuple-element.93) | copy-start | bytes 12292
  209.1 10.2 %collective-permute-start.15 = (bf16[768,256]{1,0:T(8,128)(2,1)S(1)}, bf16[768,256]{1,0:T(8,128)(2,1)S(1)}, u32[]{:S(2)}, u32[]{:S(2)}) collective-permute-start(bf16[768,256]{1,0:T(8,128)(2,1)S(1)} %add_convert_fusion.4.own), channel_id=1, source_target_pairs={{0,1},{1,0},{2,3},{3,2},{4,5},{5,4},{6,7},{7,6},{8,9},{9,8},{10,11... | collective-permute-start | bytes 1179656 | tf_op jit(solution)/shard_map/ppermute | solution.py:420
  212.6 55.1 %collective-permute-start.26 = (bf16[768,768]{1,0:T(8,128)(2,1)S(1)}, bf16[768,768]{1,0:T(8,128)(2,1)}, u32[]{:S(2)}, u32[]{:S(2)}) collective-permute-start(bf16[768,768]{1,0:T(8,128)(2,1)S(1)} %copy-done.6), channel_id=1, source_target_pairs={{0,4},{4,0},{8,12},{12,8},{16,20},{20,16},{24,28},{28,24},{1,5},{5... | collective-permute-start | bytes 3538952 | tf_op jit(solution)/shard_map/ppermute | solution.py:420
  214.4 114.2 %collective-permute-start.3 = (bf16[768,1536]{1,0:T(8,128)(2,1)}, bf16[768,1536]{1,0:T(8,128)(2,1)}, u32[]{:S(2)}, u32[]{:S(2)}) collective-permute-start(bf16[768,1536]{1,0:T(8,128)(2,1)} %add_convert_fusion.3.refs_0_), channel_id=1, source_target_pairs={{0,2},{1,3},{2,0},{3,1},{4,6},{5,7},{6,4},{7,5},{8,10},{9,11},{10,... | collective-permute-start | bytes 7077896 | tf_op jit(solution)/shard_map/ppermute | solution.py:420
  218.6 24.8 %collective-permute-start.39 = (bf16[96,1536]{1,0:T(8,128)(2,1)}, bf16[96,1536]{1,0:T(8,128)(2,1)}, u32[]{:S(2)}, u32[]{:S(2)}) collective-permute-start(bf16[96,1536]{1,0:T(8,128)(2,1)} %ar.3.refs_2_), channel_id=1, source_target_pairs={{0,8},{4,12},{8,0},{12,4},{16,24},{20,28},{24,16},{28,20},{1,9},{5... | collective-permute-start | bytes 884744 | tf_op jit(solution)/shard_map/ppermute | solution.py:420
  219.4 24.6 %collective-permute-start.40 = (bf16[96,1536]{1,0:T(8,128)(2,1)}, bf16[96,1536]{1,0:T(8,128)(2,1)}, u32[]{:S(2)}, u32[]{:S(2)}) collective-permute-start(bf16[96,1536]{1,0:T(8,128)(2,1)} %ar.3.refs_2_), channel_id=1, source_target_pairs={{0,16},{4,20},{8,24},{12,28},{16,0},{20,4},{24,8},{28,12},{1,17},{... | collective-permute-start | bytes 884744 | tf_op jit(solution)/shard_map/ppermute | solution.py:420
  229.6 5.1 %copy-start.15 = (bf16[1536,256]{1,0:T(8,128)(2,1)S(1)}, bf16[1536,256]{1,0:T(8,128)(2,1)}, u32[]{:S(2)}) copy-start(bf16[1536,256]{1,0:T(8,128)(2,1)} %get-tuple-element.78.sb_i) | copy-start | bytes 2359300
  232.7 41.4 %copy-start = (bf16[768,1536]{1,0:T(8,128)(2,1)}, bf16[768,1536]{1,0:T(8,128)(2,1)S(1)}, u32[]{:S(2)}) copy-start(bf16[768,1536]{1,0:T(8,128)(2,1)S(1)} %add_convert_fusion.1.refs_4_.refs_0_) | copy-start | bytes 7077892
  232.7 4.5 copy-start.25
  232.7 85.7 %collective-permute-start.11 = (bf16[768,1536]{1,0:T(8,128)(2,1)S(1)}, bf16[768,1536]{1,0:T(8,128)(2,1)}, u32[]{:S(2)}, u32[]{:S(2)}) collective-permute-start(bf16[768,1536]{1,0:T(8,128)(2,1)S(1)} %add_convert_fusion.1.refs_4_.refs_0_), channel_id=1, source_target_pairs={{0,2},{1,3},{2,0},{3,1},{4,6},{5,7},{6,4},{7,5},{8,10},{9,11},{10,... | collective-permute-start | bytes 7077896 | tf_op jit(solution)/shard_map/ppermute | solution.py:420
  243.4 7.3 %collective-permute-start.34 = (bf16[88,1536]{1,0:T(8,128)(2,1)S(1)}, bf16[88,1536]{1,0:T(8,128)(2,1)S(1)}, u32[]{:S(2)}, u32[]{:S(2)}) collective-permute-start(bf16[88,1536]{1,0:T(8,128)(2,1)S(1)} %fusion.7), channel_id=1, source_target_pairs={{0,4},{4,0},{8,12},{12,8},{16,20},{20,16},{24,28},{28,24},{1,5},{5... | collective-permute-start | bytes 811016 | tf_op jit(solution)/shard_map/ppermute | solution.py:420
  244.0 23.2 %collective-permute-start.19 = (bf16[192,768]{1,0:T(8,128)(2,1)}, bf16[192,768]{1,0:T(8,128)(2,1)S(1)}, u32[]{:S(2)}, u32[]{:S(2)}) collective-permute-start(bf16[192,768]{1,0:T(8,128)(2,1)} %get-tuple-element.71.refs_1_), channel_id=1, source_target_pairs={{0,8},{4,12},{8,0},{12,4},{16,24},{20,28},{24,16},{28,20},{1,9},{5... | collective-permute-start | bytes 884744 | tf_op jit(solution)/shard_map/ppermute | solution.py:420
  250.7 9.2 %collective-permute-start.41 = (bf16[96,1536]{1,0:T(8,128)(2,1)}, bf16[96,1536]{1,0:T(8,128)(2,1)S(1)}, u32[]{:S(2)}, u32[]{:S(2)}) collective-permute-start(bf16[96,1536]{1,0:T(8,128)(2,1)} %ar.3.refs_2_), channel_id=1, source_target_pairs={{0,24},{4,28},{8,16},{12,20},{16,8},{20,12},{24,0},{28,4},{1,25},{... | collective-permute-start | bytes 884744 | tf_op jit(solution)/shard_map/ppermute | solution.py:420
  259.9 12.4 %collective-permute-start.35 = (bf16[88,1536]{1,0:T(8,128)(2,1)S(1)}, bf16[88,1536]{1,0:T(8,128)(2,1)S(1)}, u32[]{:S(2)}, u32[]{:S(2)}) collective-permute-start(bf16[88,1536]{1,0:T(8,128)(2,1)S(1)} %add_convert_fusion.7), channel_id=1, source_target_pairs={{0,8},{4,12},{8,0},{12,4},{16,24},{20,28},{24,16},{28,20},{1,9},{5... | collective-permute-start | bytes 811016 | tf_op jit(solution)/shard_map/ppermute | solution.py:420
  267.2 5.1 %copy-start.22 = (bf16[192,768]{1,0:T(8,128)(2,1)}, bf16[192,768]{1,0:T(8,128)(2,1)S(1)}, u32[]{:S(2)}) copy-start(bf16[192,768]{1,0:T(8,128)(2,1)S(1)} %collective-permute-done.19.refs_1_) | copy-start | bytes 884740
  267.2 55.9 %collective-permute-start.42 = (bf16[384,1536]{1,0:T(8,128)(2,1)}, bf16[384,1536]{1,0:T(8,128)(2,1)}, u32[]{:S(2)}, u32[]{:S(2)}) collective-permute-start(bf16[384,1536]{1,0:T(8,128)(2,1)} %pad_maximum_fusion.2.mine), channel_id=1, source_target_pairs={{0,4},{4,0},{8,12},{12,8},{16,20},{20,16},{24,28},{28,24},{1,5},{5... | collective-permute-start | bytes 3538952 | tf_op jit(solution)/shard_map/ppermute | solution.py:420
  267.7 22.9 %collective-permute-start.20 = (bf16[192,768]{1,0:T(8,128)(2,1)}, bf16[192,768]{1,0:T(8,128)(2,1)S(1)}, u32[]{:S(2)}, u32[]{:S(2)}) collective-permute-start(bf16[192,768]{1,0:T(8,128)(2,1)} %get-tuple-element.82), channel_id=1, source_target_pairs={{0,16},{4,20},{8,24},{12,28},{16,0},{20,4},{24,8},{28,12},{1,17},{... | collective-permute-start | bytes 884744 | tf_op jit(solution)/shard_map/ppermute | solution.py:420
  272.3 18.3 %collective-permute-start.21 = (bf16[192,768]{1,0:T(8,128)(2,1)}, bf16[192,768]{1,0:T(8,128)(2,1)S(1)}, u32[]{:S(2)}, u32[]{:S(2)}) collective-permute-start(bf16[192,768]{1,0:T(8,128)(2,1)} %get-tuple-element.83), channel_id=1, source_target_pairs={{0,24},{4,28},{8,16},{12,20},{16,8},{20,12},{24,0},{28,4},{1,25},{... | collective-permute-start | bytes 884744 | tf_op jit(solution)/shard_map/ppermute | solution.py:420
  274.0 16.6 %copy-start.14 = (bf16[88,1536]{1,0:T(8,128)(2,1)}, bf16[88,1536]{1,0:T(8,128)(2,1)S(1)}, u32[]{:S(2)}) copy-start(bf16[88,1536]{1,0:T(8,128)(2,1)S(1)} %add_convert_fusion.6) | copy-start | bytes 811012
  290.6 27.8 %copy-start.23 = (bf16[192,768]{1,0:T(8,128)(2,1)}, bf16[192,768]{1,0:T(8,128)(2,1)S(1)}, u32[]{:S(2)}) copy-start(bf16[192,768]{1,0:T(8,128)(2,1)S(1)} %collective-permute-done.20.refs_2_) | copy-start | bytes 884740
  290.6 35.4 %collective-permute-start.36 = (bf16[88,1536]{1,0:T(8,128)(2,1)S(1)}, bf16[88,1536]{1,0:T(8,128)(2,1)}, u32[]{:S(2)}, u32[]{:S(2)}) collective-permute-start(bf16[88,1536]{1,0:T(8,128)(2,1)S(1)} %add_convert_fusion.6), channel_id=1, source_target_pairs={{0,16},{4,20},{8,24},{12,28},{16,0},{20,4},{24,8},{28,12},{1,17},{... | collective-permute-start | bytes 811016 | tf_op jit(solution)/shard_map/ppermute | solution.py:420
  291.4 37.1 %collective-permute-start.27 = (bf16[192,768]{1,0:T(8,128)(2,1)}, bf16[192,768]{1,0:T(8,128)(2,1)S(1)}, u32[]{:S(2)}, u32[]{:S(2)}) collective-permute-start(bf16[192,768]{1,0:T(8,128)(2,1)} %get-tuple-element.85), channel_id=1, source_target_pairs={{0,8},{4,12},{8,0},{12,4},{16,24},{20,28},{24,16},{28,20},{1,9},{5... | collective-permute-start | bytes 884744 | tf_op jit(solution)/shard_map/ppermute | solution.py:420
  318.4 17.4 %collective-permute-start.28 = (bf16[192,768]{1,0:T(8,128)(2,1)}, bf16[192,768]{1,0:T(8,128)(2,1)}, u32[]{:S(2)}, u32[]{:S(2)}) collective-permute-start(bf16[192,768]{1,0:T(8,128)(2,1)} %get-tuple-element.86), channel_id=1, source_target_pairs={{0,16},{4,20},{8,24},{12,28},{16,0},{20,4},{24,8},{28,12},{1,17},{... | collective-permute-start | bytes 884744 | tf_op jit(solution)/shard_map/ppermute | solution.py:420
  323.1 19.1 %copy-start.1 = (bf16[768,1536]{1,0:T(8,128)(2,1)}, bf16[768,1536]{1,0:T(8,128)(2,1)S(1)}, u32[]{:S(2)}) copy-start(bf16[768,1536]{1,0:T(8,128)(2,1)S(1)} %add_convert_fusion.own) | copy-start | bytes 7077892
  323.1 89.2 %collective-permute-start.12 = (bf16[768,1536]{1,0:T(8,128)(2,1)S(1)}, bf16[768,1536]{1,0:T(8,128)(2,1)}, u32[]{:S(2)}, u32[]{:S(2)}) collective-permute-start(bf16[768,1536]{1,0:T(8,128)(2,1)S(1)} %add_convert_fusion.own), channel_id=1, source_target_pairs={{0,1},{1,0},{2,3},{3,2},{4,5},{5,4},{6,7},{7,6},{8,9},{9,8},{10,11... | collective-permute-start | bytes 7077896 | tf_op jit(solution)/shard_map/ppermute | solution.py:420
  326.1 36.1 %collective-permute-start.22 = (bf16[192,768]{1,0:T(8,128)(2,1)}, bf16[192,768]{1,0:T(8,128)(2,1)S(1)}, u32[]{:S(2)}, u32[]{:S(2)}) collective-permute-start(bf16[192,768]{1,0:T(8,128)(2,1)} %ar.4), channel_id=1, source_target_pairs={{0,8},{4,12},{8,0},{12,4},{16,24},{20,28},{24,16},{28,20},{1,9},{5... | collective-permute-start | bytes 884744 | tf_op jit(solution)/shard_map/ppermute | solution.py:420
  328.5 51.5 %collective-permute-start.23 = (bf16[192,768]{1,0:T(8,128)(2,1)}, bf16[192,768]{1,0:T(8,128)(2,1)}, u32[]{:S(2)}, u32[]{:S(2)}) collective-permute-start(bf16[192,768]{1,0:T(8,128)(2,1)} %ar.4), channel_id=1, source_target_pairs={{0,16},{4,20},{8,24},{12,28},{16,0},{20,4},{24,8},{28,12},{1,17},{... | collective-permute-start | bytes 884744 | tf_op jit(solution)/shard_map/ppermute | solution.py:420
  328.6 13.7 %copy-start.20 = (bf16[192,768]{1,0:T(8,128)(2,1)}, bf16[192,768]{1,0:T(8,128)(2,1)S(1)}, u32[]{:S(2)}) copy-start(bf16[192,768]{1,0:T(8,128)(2,1)S(1)} %collective-permute-done.27.refs_1_) | copy-start | bytes 884740
  328.6 52.7 %collective-permute-start.24 = (bf16[192,768]{1,0:T(8,128)(2,1)}, bf16[192,768]{1,0:T(8,128)(2,1)}, u32[]{:S(2)}, u32[]{:S(2)}) collective-permute-start(bf16[192,768]{1,0:T(8,128)(2,1)} %ar.4), channel_id=1, source_target_pairs={{0,24},{4,28},{8,16},{12,20},{16,8},{20,12},{24,0},{28,4},{1,25},{... | collective-permute-start | bytes 884744 | tf_op jit(solution)/shard_map/ppermute | solution.py:420
  335.8 18.9 %collective-permute-start.29 = (bf16[192,768]{1,0:T(8,128)(2,1)}, bf16[192,768]{1,0:T(8,128)(2,1)S(1)}, u32[]{:S(2)}, u32[]{:S(2)}) collective-permute-start(bf16[192,768]{1,0:T(8,128)(2,1)} %get-tuple-element.87), channel_id=1, source_target_pairs={{0,24},{4,28},{8,16},{12,20},{16,8},{20,12},{24,0},{28,4},{1,25},{... | collective-permute-start | bytes 884744 | tf_op jit(solution)/shard_map/ppermute | solution.py:420
  355.4 120.4 %collective-permute-start.4 = (bf16[768,1536]{1,0:T(8,128)(2,1)}, bf16[768,1536]{1,0:T(8,128)(2,1)}, u32[]{:S(2)}, u32[]{:S(2)}) collective-permute-start(bf16[768,1536]{1,0:T(8,128)(2,1)} %add_convert_fusion.2.own), channel_id=1, source_target_pairs={{0,1},{1,0},{2,3},{3,2},{4,5},{5,4},{6,7},{7,6},{8,9},{9,8},{10,11... | collective-permute-start | bytes 7077896 | tf_op jit(solution)/shard_map/ppermute | solution.py:420
  360.0 26.3 %copy-start.13 = (bf16[192,768]{1,0:T(8,128)(2,1)S(1)}, bf16[192,768]{1,0:T(8,128)(2,1)}, u32[]{:S(2)}) copy-start(bf16[192,768]{1,0:T(8,128)(2,1)} %ar.4) | copy-start | bytes 884740
  362.2 42.1 %copy-start.12 = (bf16[192,768]{1,0:T(8,128)(2,1)S(1)}, bf16[192,768]{1,0:T(8,128)(2,1)}, u32[]{:S(2)}) copy-start(bf16[192,768]{1,0:T(8,128)(2,1)} %ar.5) | copy-start | bytes 884740
  362.2 19.1 %copy-start.19 = (bf16[192,768]{1,0:T(8,128)(2,1)}, bf16[192,768]{1,0:T(8,128)(2,1)S(1)}, u32[]{:S(2)}) copy-start(bf16[192,768]{1,0:T(8,128)(2,1)S(1)} %collective-permute-done.22) | copy-start | bytes 884740
  362.2 31.8 %collective-permute-start.30 = (bf16[192,768]{1,0:T(8,128)(2,1)}, bf16[192,768]{1,0:T(8,128)(2,1)}, u32[]{:S(2)}, u32[]{:S(2)}) collective-permute-start(bf16[192,768]{1,0:T(8,128)(2,1)} %ar.5), channel_id=1, source_target_pairs={{0,8},{4,12},{8,0},{12,4},{16,24},{20,28},{24,16},{28,20},{1,9},{5... | collective-permute-start | bytes 884744 | tf_op jit(solution)/shard_map/ppermute | solution.py:420
  380.0 23.8 %collective-permute-start.31 = (bf16[192,768]{1,0:T(8,128)(2,1)}, bf16[192,768]{1,0:T(8,128)(2,1)}, u32[]{:S(2)}, u32[]{:S(2)}) collective-permute-start(bf16[192,768]{1,0:T(8,128)(2,1)} %ar.5), channel_id=1, source_target_pairs={{0,16},{4,20},{8,24},{12,28},{16,0},{20,4},{24,8},{28,12},{1,17},{... | collective-permute-start | bytes 884744 | tf_op jit(solution)/shard_map/ppermute | solution.py:420
  381.3 23.0 %collective-permute-start.32 = (bf16[192,768]{1,0:T(8,128)(2,1)}, bf16[192,768]{1,0:T(8,128)(2,1)}, u32[]{:S(2)}, u32[]{:S(2)}) collective-permute-start(bf16[192,768]{1,0:T(8,128)(2,1)} %ar.5), channel_id=1, source_target_pairs={{0,24},{4,28},{8,16},{12,20},{16,8},{20,12},{24,0},{28,4},{1,25},{... | collective-permute-start | bytes 884744 | tf_op jit(solution)/shard_map/ppermute | solution.py:420
  388.5 21.0 %copy-start.16 = (bf16[384,256]{1,0:T(8,128)(2,1)S(1)}, bf16[384,256]{1,0:T(8,128)(2,1)}, u32[]{:S(2)}) copy-start(bf16[384,256]{1,0:T(8,128)(2,1)} %convert_element_type.146) | copy-start | bytes 589828
  394.0 15.6 %collective-permute-start.37 = (bf16[384,256]{1,0:T(8,128)(2,1)}, bf16[384,256]{1,0:T(8,128)(2,1)}, u32[]{:S(2)}, u32[]{:S(2)}) collective-permute-start(bf16[384,256]{1,0:T(8,128)(2,1)} %convert_element_type.146), channel_id=1, source_target_pairs={{0,1},{1,0},{2,3},{3,2},{4,5},{5,4},{6,7},{7,6},{8,9},{9,8},{10,11... | collective-permute-start | bytes 589832 | tf_op jit(solution)/shard_map/ppermute | solution.py:420
  403.8 62.6 %collective-permute-start.25 = (bf16[768,768]{1,0:T(8,128)(2,1)}, bf16[768,768]{1,0:T(8,128)(2,1)}, u32[]{:S(2)}, u32[]{:S(2)}) collective-permute-start(bf16[768,768]{1,0:T(8,128)(2,1)} %pad_maximum_fusion.mine), channel_id=1, source_target_pairs={{0,4},{4,0},{8,12},{12,8},{16,20},{20,16},{24,28},{28,24},{1,5},{5... | collective-permute-start | bytes 3538952 | tf_op jit(solution)/shard_map/ppermute | solution.py:420
  406.5 64.6 %collective-permute-start.33 = (bf16[768,768]{1,0:T(8,128)(2,1)}, bf16[768,768]{1,0:T(8,128)(2,1)}, u32[]{:S(2)}, u32[]{:S(2)}) collective-permute-start(bf16[768,768]{1,0:T(8,128)(2,1)} %pad_maximum_fusion.1.mine), channel_id=1, source_target_pairs={{0,4},{4,0},{8,12},{12,8},{16,20},{20,16},{24,28},{28,24},{1,5},{5... | collective-permute-start | bytes 3538952 | tf_op jit(solution)/shard_map/ppermute | solution.py:420
  410.7 53.3 %collective-permute-start.38 = (bf16[768,256]{1,0:T(8,128)(2,1)S(1)}, bf16[768,256]{1,0:T(8,128)(2,1)}, u32[]{:S(2)}, u32[]{:S(2)}) collective-permute-start(bf16[768,256]{1,0:T(8,128)(2,1)S(1)} %maximum_select_fusion.1), channel_id=1, source_target_pairs={{0,2},{1,3},{2,0},{3,1},{4,6},{5,7},{6,4},{7,5},{8,10},{9,11},{10,... | collective-permute-start | bytes 1179656 | tf_op jit(solution)/shard_map/ppermute | solution.py:420
  425.5 23.4 %collective-permute-start.16 = (f32[8,1536]{1,0:T(8,128)}, f32[8,1536]{1,0:T(8,128)S(1)}, u32[]{:S(2)}, u32[]{:S(2)}) collective-permute-start(f32[8,1536]{1,0:T(8,128)} %get-tuple-element.80), channel_id=1, source_target_pairs={{0,4},{4,0},{8,12},{12,8},{16,20},{20,16},{24,28},{28,24},{1,5},{5... | collective-permute-start | bytes 147464 | tf_op jit(solution)/shard_map/ppermute | solution.py:420
  449.7 10.7 %collective-permute-start.17 = (f32[8,1536]{1,0:T(8,128)S(1)}, f32[8,1536]{1,0:T(8,128)S(1)}, u32[]{:S(2)}, u32[]{:S(2)}) collective-permute-start(f32[8,1536]{1,0:T(8,128)S(1)} %add.89), channel_id=1, source_target_pairs={{0,8},{4,12},{8,0},{12,4},{16,24},{20,28},{24,16},{28,20},{1,9},{5... | collective-permute-start | bytes 147464 | tf_op jit(solution)/shard_map/ppermute | solution.py:420
  460.4 20.1 %collective-permute-start.18 = (f32[8,1536]{1,0:T(8,128)S(1)}, f32[8,1536]{1,0:T(8,128)S(1)}, u32[]{:S(2)}, u32[]{:S(2)}) collective-permute-start(f32[8,1536]{1,0:T(8,128)S(1)} %add.90), channel_id=1, source_target_pairs={{0,16},{4,20},{8,24},{12,28},{16,0},{20,4},{24,8},{28,12},{1,17},{... | collective-permute-start | bytes 147464 | tf_op jit(solution)/shard_map/ppermute | solution.py:420
  (9 other events, 24.1 us)
